TPU v7x, 256 devices: a whole 4x4x8 slice. The times are simulated.
256 devices in a mesh: sec: 2 (over core), blk: 128 (over y, x, z).
Axes of the slice: x: 4, y: 4, z: 8, core: 2. Of those that a mesh axis runs over, the one named last changes fastest.
Arguments:
- columns: bfloat16 [2, 128, 8, 128, 2048], P('sec', 'blk'), may hold values from -6 to 6
- mixing: bfloat16 [2, 128, 128, 128], P('sec', 'blk'), may hold values from -0.5 to 0.5
- lagged_flux: bfloat16 [128, 8, 2048], P('blk'), may hold values from -6 to 6
- coefficients: float32 [8], replicated, may hold values from 0.5 to 2
- ocean_mask: int32 [128, 2048], P('blk'), may hold values 0 or 1
- atm_tile: int32 [128, 5, 16], P('blk'), may hold values from 0 to 15
- ocean_tile: int32 [128, 5, 16], P('blk'), may hold values from 0 to 15
- live: int32 [128, 5, 16], P('blk'), may hold values from 0 to 1, as said below
- weights: bfloat16 [128, 5, 16, 128, 128], P('blk'), may hold values from -0.5 to 0.5
Outputs:
- new_columns: bfloat16 [2, 128, 8, 128, 2048], P('sec', 'blk')
- flux_out: bfloat16 [2, 128, 8, 2048], P('sec', 'blk')
Inputs may be any that keep to these rules, and one draw needn't show every extreme that they name: The share of live slots differs from block to block.
All inputs are finite; a program needn't handle non-finite values. No bound on the sum of `ocean_mask` on one device may be relied on, other than what follows from the above.
Results may differ from a plain program's by a relative error of at most 0.0062.
Values may be sent and summed in bfloat16 or wider, within the bound.
No kernel may reach another device: no remote copies, remote signals or barrier semaphores. Data moves between devices by JAX's collectives and lax.ppermute only.
A program may use at most 128 MiB of HBM per device.

v0:
```python
import jax
import jax.numpy as jnp
from jax import lax
from jax.sharding import PartitionSpec as P

step_weight = 0.25


def passed_along(value, axis, steps):
    count = lax.axis_size(axis)
    first, last = (max(0, -steps), min(count, count - steps))
    return lax.ppermute(value, axis, [(source, source + steps) for source in range(first, last)])


def local(
    columns, mixing, lagged_flux, coefficients, ocean_mask, atm_tile, ocean_tile, live, weights
):
    section = lax.axis_index("sec")
    column_data = columns[0, 0]
    fields, levels, cells = column_data.shape
    spans = atm_tile.shape[1]
    slot_count = atm_tile.shape[2]
    tile_cells = weights.shape[3]
    tiles = cells // tile_cells
    reach = (spans - 1) // 2
    width = fields * tile_cells
    mixed = column_data.astype(jnp.float32) + jnp.einsum(
        "kl,flc->fkc", mixing[0, 0], column_data, preferred_element_type=jnp.float32
    )
    atm_level = mixed[:, 0, :] - step_weight * lagged_flux[0].astype(jnp.float32)
    atm_surface = atm_level.astype(jnp.bfloat16)
    ocean_level = mixed[:, 0, :]
    arrived = passed_along(atm_surface, "sec", 1)
    surface_tiles = arrived.reshape(fields, tiles, tile_cells).transpose(1, 0, 2)
    picked = surface_tiles[atm_tile[0]]
    weight_block = weights[0]
    live_block = live[0]
    contrib = jnp.einsum(
        "psfi,psij->psfj", picked, weight_block, preferred_element_type=jnp.float32
    )
    contrib = (
        (contrib * live_block[:, :, None, None].astype(jnp.float32))
        .astype(jnp.bfloat16)
        .reshape(spans, slot_count, width)
    )
    target = jnp.where(live_block == 1, ocean_tile[0], -1)
    piece_list = []
    target_list = []
    for offset_pos in range(spans):
        offset = offset_pos - reach
        if offset == 0:
            piece_list.append(contrib[offset_pos])
            target_list.append(target[offset_pos])
        else:
            moved_tiles, moved_target = passed_along(
                (contrib[offset_pos], target[offset_pos]), "blk", offset
            )
            piece_list.append(moved_tiles)
            target_list.append(moved_target)
    items = jnp.concatenate(piece_list, axis=0)
    item_target = jnp.concatenate(target_list, axis=0)
    tile_hot = (item_target[:, None] == jnp.arange(tiles, dtype=jnp.int32)[None, :]).astype(
        jnp.bfloat16
    )
    summed = jnp.einsum("mt,mx->tx", tile_hot, items, preferred_element_type=jnp.float32)
    remapped = summed.reshape(tiles, fields, tile_cells).transpose(1, 0, 2).reshape(fields, cells)
    across = remapped[0] - ocean_level[0]
    along = remapped[1] - ocean_level[1]
    speed = jnp.sqrt(across * across + along * along + 1.0)
    ocean_flux = (
        coefficients[:, None]
        * speed[None, :]
        * (remapped - ocean_level)
        * ocean_mask[0][None, :].astype(jnp.float32)
    ).astype(jnp.bfloat16)
    flux_tiles = (
        ocean_flux.reshape(fields, tiles, tile_cells).transpose(1, 0, 2).reshape(tiles, width)
    )
    back_items = flux_tiles[jnp.clip(item_target, 0, tiles - 1)] * (item_target >= 0)[
        :, None
    ].astype(jnp.bfloat16)
    back_pieces = back_items.reshape(spans, slot_count, width)
    return_list = []
    for offset_pos in range(spans):
        offset = offset_pos - reach
        if offset == 0:
            return_list.append(back_pieces[offset_pos])
        else:
            return_list.append(passed_along(back_pieces[offset_pos], "blk", -offset))
    returned = jnp.stack(return_list, axis=0)
    back_product = jnp.einsum(
        "psfj,psij->psfi",
        returned.reshape(spans, slot_count, fields, tile_cells),
        weight_block,
        preferred_element_type=jnp.float32,
    )
    atm_hot = (atm_tile[0][:, :, None] == jnp.arange(tiles, dtype=jnp.int32)[None, None, :]).astype(
        jnp.float32
    )
    atm_sum = jnp.einsum("pst,psfi->tfi", atm_hot, back_product, precision=lax.Precision.HIGHEST)
    atm_flux = atm_sum.transpose(1, 0, 2).reshape(fields, cells).astype(jnp.bfloat16)
    atm_home = passed_along(atm_flux, "sec", -1)
    is_atm = section == 0
    ocean_top = (ocean_level + step_weight * ocean_flux.astype(jnp.float32)).astype(jnp.bfloat16)
    top_level = jnp.where(is_atm, atm_surface, ocean_top)
    rounded = mixed.astype(jnp.bfloat16).at[:, 0, :].set(top_level)
    flux_here = jnp.where(is_atm, atm_home, ocean_flux)
    return (rounded[None, None], flux_here[None, None])


def solution(mesh):
    in_specs = (
        P("sec", "blk", None, None, None),
        P("sec", "blk", None, None),
        P("blk", None, None),
        P(),
        P("blk", None),
        P("blk", None, None),
        P("blk", None, None),
        P("blk", None, None),
        P("blk", None, None, None, None),
    )
    out_specs = (P("sec", "blk", None, None, None), P("sec", "blk", None, None))
    return jax.shard_map(local, mesh=mesh, in_specs=in_specs, out_specs=out_specs, check_vma=False)
```

profile of v0, /device:TPU:25, one launch (start us, length us, event | category | flops | bytes accessed | tf_op | source)
XLA Modules:
  0.0 84.0 jit_solution(16571944579379320433)
XLA Ops:
  0.6 0.0 copy-start
  0.6 0.0 copy-start.1
  0.7 0.0 copy-start.3
  0.7 0.0 copy-start.6
  0.7 0.0 copy-start.2
  0.7 4.9 %bitcast_add_fusion = f32[8,128,2048]{2,1,0:T(8,128)S(1)} fusion(bf16[1,1,8,128,2048]{4,3,2,1,0:T(8,128)(2,1)} %param.11, bf16[1,1,128,128]{3,2,1,0:T(8,128)(2,1)} %param.12), kind=kOutput, calls=%fused_computation.2 | convolution fusion | flops 541065216 | bytes 12615680 | tf_op jit(solution)/shard_map/kl,flc->fkc/dot_general | solution.py:27
  5.6 0.0 copy-done.1
  5.6 1.3 %collective-permute-start.4 = (bf16[8,2048]{1,0:T(8,128)(2,1)S(1)}, bf16[8,2048]{1,0:T(8,128)(2,1)S(1)}, u32[]{:S(2)}, u32[]{:S(2)}) collective-permute-start(bf16[8,2048]{1,0:T(8,128)(2,1)S(1)} %fusion.17), channel_id=1, source_target_pairs={{0,128},{1,129},{2,130},{3,131},{4,132},{5,133},{6,134},{7,135},{8... | collective-permute-start | bytes 98312 | tf_op jit(solution)/shard_map/ppermute | solution.py:12
  6.9 0.0 copy-done.3
  6.9 0.0 copy-done.6
  7.0 10.3 %collective-permute-start = (s32[16]{0:T(128)S(1)}, s32[16]{0:T(128)S(1)}, u32[]{:S(2)}, u32[]{:S(2)}) collective-permute-start(s32[16]{0:T(128)S(1)} %get-tuple-element.33), channel_id=1, source_target_pairs={{2,0},{3,1},{4,2},{5,3},{6,4},{7,5},{8,6},{9,7},{10,8},{11,9},{12,... | collective-permute-start | bytes 200 | tf_op jit(solution)/shard_map/ppermute | solution.py:12
  17.3 2.6 %collective-permute-start.1 = (s32[16]{0:T(128)S(1)}, s32[16]{0:T(128)S(1)}, u32[]{:S(2)}, u32[]{:S(2)}) collective-permute-start(s32[16]{0:T(128)S(1)} %get-tuple-element.32), channel_id=1, source_target_pairs={{1,0},{2,1},{3,2},{4,3},{5,4},{6,5},{7,6},{8,7},{9,8},{10,9},{11,1... | collective-permute-start | bytes 200 | tf_op jit(solution)/shard_map/ppermute | solution.py:12
  19.9 2.6 %collective-permute-start.2 = (s32[16]{0:T(128)S(1)}, s32[16]{0:T(128)S(1)}, u32[]{:S(2)}, u32[]{:S(2)}) collective-permute-start(s32[16]{0:T(128)S(1)} %get-tuple-element.30), channel_id=1, source_target_pairs={{0,1},{1,2},{2,3},{3,4},{4,5},{5,6},{6,7},{7,8},{8,9},{9,10},{10,1... | collective-permute-start | bytes 200 | tf_op jit(solution)/shard_map/ppermute | solution.py:12
  22.6 2.4 %collective-permute-start.3 = (s32[16]{0:T(128)S(1)}, s32[16]{0:T(128)S(1)}, u32[]{:S(2)}, u32[]{:S(2)}) collective-permute-start(s32[16]{0:T(128)S(1)} %get-tuple-element.29), channel_id=1, source_target_pairs={{0,2},{1,3},{2,4},{3,5},{4,6},{5,7},{6,8},{7,9},{8,10},{9,11},{10,... | collective-permute-start | bytes 200 | tf_op jit(solution)/shard_map/ppermute | solution.py:12
  25.0 0.0 copy-done.2
  25.1 0.0 copy-start.4
  25.1 2.7 %convert_bitcast_fusion = bf16[1,1,8,128,2048]{4,3,2,1,0:T(8,128)(2,1)} fusion(f32[8,128,2048]{2,1,0:T(8,128)S(1)} %bitcast_add_fusion), kind=kLoop, calls=%fused_computation.4 | loop fusion | flops 2097152 | bytes 12582912 | tf_op jit(solution)/shard_map/broadcast_in_dim | solution.py:108
  27.7 0.0 copy-start.5
  27.7 0.1 reshape.420
  27.8 0.0 copy-done.4
  27.8 0.0 collective-permute-done
  27.9 0.0 collective-permute-done.1
  27.9 0.6 collective-permute-done.2
  28.4 3.6 %collective-permute-done.3 = s32[16]{0:T(128)S(1)} collective-permute-done((s32[16]{0:T(128)S(1)}, s32[16]{0:T(128)S(1)}, u32[]{:S(2)}, u32[]{:S(2)}) %collective-permute-start.3) | collective-permute-done | bytes 96 | tf_op jit(solution)/shard_map/ppermute | solution.py:12
  32.0 0.1 concatenate.39
  32.1 0.1 concatenate.32
  32.2 0.0 collective-permute-done.4
  32.2 0.6 gather_fusion
  32.8 0.0 copy-done
  32.9 0.8 fusion.8
  33.7 3.9 %collective-permute-start.5 = (bf16[16,1024]{1,0:T(8,128)(2,1)S(1)}, bf16[16,1024]{1,0:T(8,128)(2,1)S(1)}, u32[]{:S(2)}, u32[]{:S(2)}) collective-permute-start(bf16[16,1024]{1,0:T(8,128)(2,1)S(1)} %bitcast.256), channel_id=1, source_target_pairs={{2,0},{3,1},{4,2},{5,3},{6,4},{7,5},{8,6},{9,7},{10,8},{11,9},{12,... | collective-permute-start | bytes 98312 | tf_op jit(solution)/shard_map/ppermute | solution.py:12
  37.6 2.6 %collective-permute-start.6 = (bf16[16,1024]{1,0:T(8,128)(2,1)S(1)}, bf16[16,1024]{1,0:T(8,128)(2,1)S(1)}, u32[]{:S(2)}, u32[]{:S(2)}) collective-permute-start(bf16[16,1024]{1,0:T(8,128)(2,1)S(1)} %bitcast.261), channel_id=1, source_target_pairs={{1,0},{2,1},{3,2},{4,3},{5,4},{6,5},{7,6},{8,7},{9,8},{10,9},{11,1... | collective-permute-start | bytes 98312 | tf_op jit(solution)/shard_map/ppermute | solution.py:12
  40.3 2.6 %collective-permute-start.7 = (bf16[16,1024]{1,0:T(8,128)(2,1)S(1)}, bf16[16,1024]{1,0:T(8,128)(2,1)S(1)}, u32[]{:S(2)}, u32[]{:S(2)}) collective-permute-start(bf16[16,1024]{1,0:T(8,128)(2,1)S(1)} %bitcast.255), channel_id=1, source_target_pairs={{0,1},{1,2},{2,3},{3,4},{4,5},{5,6},{6,7},{7,8},{8,9},{9,10},{10,1... | collective-permute-start | bytes 98312 | tf_op jit(solution)/shard_map/ppermute | solution.py:12
  43.0 2.4 %collective-permute-start.8 = (bf16[16,1024]{1,0:T(8,128)(2,1)S(1)}, bf16[16,1024]{1,0:T(8,128)(2,1)S(1)}, u32[]{:S(2)}, u32[]{:S(2)}) collective-permute-start(bf16[16,1024]{1,0:T(8,128)(2,1)S(1)} %bitcast.254), channel_id=1, source_target_pairs={{0,2},{1,3},{2,4},{3,5},{4,6},{5,7},{6,8},{7,9},{8,10},{9,11},{10,... | collective-permute-start | bytes 98312 | tf_op jit(solution)/shard_map/ppermute | solution.py:12
  45.3 0.0 collective-permute-done.5
  45.4 0.0 collective-permute-done.6
  45.4 3.8 %collective-permute-done.7 = bf16[16,1024]{1,0:T(8,128)(2,1)S(1)} collective-permute-done((bf16[16,1024]{1,0:T(8,128)(2,1)S(1)}, bf16[16,1024]{1,0:T(8,128)(2,1)S(1)}, u32[]{:S(2)}, u32[]{:S(2)}) %collective-permute-start.7) | collective-permute-done | bytes 32800 | tf_op jit(solution)/shard_map/ppermute | solution.py:12
  49.2 3.7 %collective-permute-done.8 = bf16[16,1024]{1,0:T(8,128)(2,1)S(1)} collective-permute-done((bf16[16,1024]{1,0:T(8,128)(2,1)S(1)}, bf16[16,1024]{1,0:T(8,128)(2,1)S(1)}, u32[]{:S(2)}, u32[]{:S(2)}) %collective-permute-start.8) | collective-permute-done | bytes 32800 | tf_op jit(solution)/shard_map/ppermute | solution.py:12
  52.8 0.3 convolution_bitcast_fusion.1
  53.1 0.0 copy-done.5
  53.1 0.1 copy_bitcast_fusion.5
  53.2 0.7 gather_fusion.1
  54.0 0.1 broadcast_multiply_fusion
  54.1 1.9 %collective-permute-start.9 = (bf16[16,1024]{1,0:T(8,128)(2,1)S(1)}, bf16[16,1024]{1,0:T(8,128)(2,1)S(1)}, u32[]{:S(2)}, u32[]{:S(2)}) collective-permute-start(bf16[16,1024]{1,0:T(8,128)(2,1)S(1)} %get-tuple-element.20), channel_id=1, source_target_pairs={{0,2},{1,3},{2,4},{3,5},{4,6},{5,7},{6,8},{7,9},{8,10},{9,11},{10,... | collective-permute-start | bytes 98312 | tf_op jit(solution)/shard_map/ppermute | solution.py:12
  56.1 3.1 %collective-permute-start.10 = (bf16[16,1024]{1,0:T(8,128)(2,1)S(1)}, bf16[16,1024]{1,0:T(8,128)(2,1)S(1)}, u32[]{:S(2)}, u32[]{:S(2)}) collective-permute-start(bf16[16,1024]{1,0:T(8,128)(2,1)S(1)} %get-tuple-element.19), channel_id=1, source_target_pairs={{0,1},{1,2},{2,3},{3,4},{4,5},{5,6},{6,7},{7,8},{8,9},{9,10},{10,1... | collective-permute-start | bytes 98312 | tf_op jit(solution)/shard_map/ppermute | solution.py:12
  59.2 7.3 %collective-permute-start.11 = (bf16[16,1024]{1,0:T(8,128)(2,1)S(1)}, bf16[16,1024]{1,0:T(8,128)(2,1)S(1)}, u32[]{:S(2)}, u32[]{:S(2)}) collective-permute-start(bf16[16,1024]{1,0:T(8,128)(2,1)S(1)} %get-tuple-element.17), channel_id=1, source_target_pairs={{1,0},{2,1},{3,2},{4,3},{5,4},{6,5},{7,6},{8,7},{9,8},{10,9},{11,1... | collective-permute-start | bytes 98312 | tf_op jit(solution)/shard_map/ppermute | solution.py:12
  66.5 3.4 %collective-permute-start.12 = (bf16[16,1024]{1,0:T(8,128)(2,1)S(1)}, bf16[16,1024]{1,0:T(8,128)(2,1)S(1)}, u32[]{:S(2)}, u32[]{:S(2)}) collective-permute-start(bf16[16,1024]{1,0:T(8,128)(2,1)S(1)} %get-tuple-element.16), channel_id=1, source_target_pairs={{2,0},{3,1},{4,2},{5,3},{6,4},{7,5},{8,6},{9,7},{10,8},{11,9},{12,... | collective-permute-start | bytes 98312 | tf_op jit(solution)/shard_map/ppermute | solution.py:12
  69.9 0.0 collective-permute-done.9
  69.9 0.0 collective-permute-done.10
  69.9 0.0 collective-permute-done.11
  69.9 2.1 %collective-permute-done.12 = bf16[16,1024]{1,0:T(8,128)(2,1)S(1)} collective-permute-done((bf16[16,1024]{1,0:T(8,128)(2,1)S(1)}, bf16[16,1024]{1,0:T(8,128)(2,1)S(1)}, u32[]{:S(2)}, u32[]{:S(2)}) %collective-permute-start.12) | collective-permute-done | bytes 32800 | tf_op jit(solution)/shard_map/ppermute | solution.py:12
  72.1 1.4 %fusion.1 = f32[5,16,8,128]{3,2,1,0:T(8,128)S(1)} fusion(bf16[5,16,8,128]{3,2,1,0:T(8,128)(2,1)S(1)} %bitcast_dynamic-update-slice_fusion, bf16[1,5,16,128,128]{4,3,2,1,0:T(8,128)(2,1)S(1)} %copy-done), kind=kOutput, calls=%fused_computation.5 | convolution fusion | flops 20971520 | bytes 3112960 | tf_op jit(solution)/shard_map/psfj,psij->psfi/dot_general | solution.py:91
  73.6 0.3 fusion.12
  73.9 7.3 %collective-permute-start.13 = (bf16[8,2048]{1,0:T(8,128)(2,1)S(1)}, bf16[8,2048]{1,0:T(8,128)(2,1)S(1)}, u32[]{:S(2)}, u32[]{:S(2)}) collective-permute-start(bf16[8,2048]{1,0:T(8,128)(2,1)S(1)} %bitcast.262), channel_id=1, source_target_pairs={{128,0},{129,1},{130,2},{131,3},{132,4},{133,5},{134,6},{135,7},{1... | collective-permute-start | bytes 98312 | tf_op jit(solution)/shard_map/ppermute | solution.py:12
  81.2 0.1 fusion.26
  81.3 0.1 copy.13
  81.4 1.9 %scatter.4 = bf16[1,1,8,128,2048]{4,3,2,1,0:T(8,128)(2,1)} dynamic-update-slice(bf16[1,1,8,128,2048]{4,3,2,1,0:T(8,128)(2,1)} %convert_bitcast_fusion, bf16[1,1,8,1,2048]{4,3,2,1,0:T(2,128)(2,1)S(1)} %copy.13, s32[]{:T(128)} %constant.43.clone.1, s32[]{:T(128)} %constant.43.clone.1, s32[]{:T(128)} %constant.43.clone.1, s32[]{:T(128)} %constant.43.clone.1, s32[]{:T(128)} %constant.43.clone.1) | dynamic-update-slice | bytes 65540 | tf_op jit(solution)/shard_map/scatter | solution.py:106
  83.2 0.0 collective-permute-done.13
  83.3 0.7 fusion.28
  (39 shorter events, 0.4 us)
Async XLA Ops:
  0.6 32.2 %copy-start = (bf16[1,5,16,128,128]{4,3,2,1,0:T(8,128)(2,1)S(1)}, bf16[1,5,16,128,128]{4,3,2,1,0:T(8,128)(2,1)}, u32[]{:S(2)}) copy-start(bf16[1,5,16,128,128]{4,3,2,1,0:T(8,128)(2,1)} %param.19) | copy-start | bytes 7864324
  0.6 4.9 %copy-start.1 = (bf16[1,8,2048]{2,1,0:T(8,128)(2,1)S(1)}, bf16[1,8,2048]{2,1,0:T(8,128)(2,1)}, u32[]{:S(2)}) copy-start(bf16[1,8,2048]{2,1,0:T(8,128)(2,1)} %param.13) | copy-start | bytes 98308
  0.7 6.3 %copy-start.3 = (s32[1,5,16]{2,0,1:T(1,128)S(1)}, s32[1,5,16]{2,0,1:T(1,128)}, u32[]{:S(2)}) copy-start(s32[1,5,16]{2,0,1:T(1,128)} %param.18) | copy-start | bytes 964
  0.7 6.3 %copy-start.6 = (s32[1,5,16]{2,0,1:T(1,128)S(1)}, s32[1,5,16]{2,0,1:T(1,128)}, u32[]{:S(2)}) copy-start(s32[1,5,16]{2,0,1:T(1,128)} %param.17) | copy-start | bytes 964
  0.7 24.3 %copy-start.2 = (s32[1,5,16]{2,0,1:T(1,128)S(1)}, s32[1,5,16]{2,0,1:T(1,128)}, u32[]{:S(2)}) copy-start(s32[1,5,16]{2,0,1:T(1,128)} %param.16) | copy-start | bytes 964
  5.6 26.6 %collective-permute-start.4 = (bf16[8,2048]{1,0:T(8,128)(2,1)S(1)}, bf16[8,2048]{1,0:T(8,128)(2,1)S(1)}, u32[]{:S(2)}, u32[]{:S(2)}) collective-permute-start(bf16[8,2048]{1,0:T(8,128)(2,1)S(1)} %fusion.17), channel_id=1, source_target_pairs={{0,128},{1,129},{2,130},{3,131},{4,132},{5,133},{6,134},{7,135},{8... | collective-permute-start | bytes 98312 | tf_op jit(solution)/shard_map/ppermute | solution.py:12
  7.0 20.9 %collective-permute-start = (s32[16]{0:T(128)S(1)}, s32[16]{0:T(128)S(1)}, u32[]{:S(2)}, u32[]{:S(2)}) collective-permute-start(s32[16]{0:T(128)S(1)} %get-tuple-element.33), channel_id=1, source_target_pairs={{2,0},{3,1},{4,2},{5,3},{6,4},{7,5},{8,6},{9,7},{10,8},{11,9},{12,... | collective-permute-start | bytes 200 | tf_op jit(solution)/shard_map/ppermute | solution.py:12
  17.3 10.6 %collective-permute-start.1 = (s32[16]{0:T(128)S(1)}, s32[16]{0:T(128)S(1)}, u32[]{:S(2)}, u32[]{:S(2)}) collective-permute-start(s32[16]{0:T(128)S(1)} %get-tuple-element.32), channel_id=1, source_target_pairs={{1,0},{2,1},{3,2},{4,3},{5,4},{6,5},{7,6},{8,7},{9,8},{10,9},{11,1... | collective-permute-start | bytes 200 | tf_op jit(solution)/shard_map/ppermute | solution.py:12
  19.9 8.5 %collective-permute-start.2 = (s32[16]{0:T(128)S(1)}, s32[16]{0:T(128)S(1)}, u32[]{:S(2)}, u32[]{:S(2)}) collective-permute-start(s32[16]{0:T(128)S(1)} %get-tuple-element.30), channel_id=1, source_target_pairs={{0,1},{1,2},{2,3},{3,4},{4,5},{5,6},{6,7},{7,8},{8,9},{9,10},{10,1... | collective-permute-start | bytes 200 | tf_op jit(solution)/shard_map/ppermute | solution.py:12
  22.6 9.4 %collective-permute-start.3 = (s32[16]{0:T(128)S(1)}, s32[16]{0:T(128)S(1)}, u32[]{:S(2)}, u32[]{:S(2)}) collective-permute-start(s32[16]{0:T(128)S(1)} %get-tuple-element.29), channel_id=1, source_target_pairs={{0,2},{1,3},{2,4},{3,5},{4,6},{5,7},{6,8},{7,9},{8,10},{9,11},{10,... | collective-permute-start | bytes 200 | tf_op jit(solution)/shard_map/ppermute | solution.py:12
  25.1 2.8 %copy-start.4 = (s32[1,2048]{1,0:T(1,128)S(1)}, s32[1,2048]{1,0:T(1,128)}, u32[]{:S(2)}) copy-start(s32[1,2048]{1,0:T(1,128)} %param.15) | copy-start | bytes 24580
  27.7 25.4 %copy-start.5 = (f32[8]{0:T(128)S(1)}, f32[8]{0:T(128)}, u32[]{:S(2)}) copy-start(f32[8]{0:T(128)} %param.14) | copy-start | bytes 100
  33.7 11.7 %collective-permute-start.5 = (bf16[16,1024]{1,0:T(8,128)(2,1)S(1)}, bf16[16,1024]{1,0:T(8,128)(2,1)S(1)}, u32[]{:S(2)}, u32[]{:S(2)}) collective-permute-start(bf16[16,1024]{1,0:T(8,128)(2,1)S(1)} %bitcast.256), channel_id=1, source_target_pairs={{2,0},{3,1},{4,2},{5,3},{6,4},{7,5},{8,6},{9,7},{10,8},{11,9},{12,... | collective-permute-start | bytes 98312 | tf_op jit(solution)/shard_map/ppermute | solution.py:12
  37.6 7.7 %collective-permute-start.6 = (bf16[16,1024]{1,0:T(8,128)(2,1)S(1)}, bf16[16,1024]{1,0:T(8,128)(2,1)S(1)}, u32[]{:S(2)}, u32[]{:S(2)}) collective-permute-start(bf16[16,1024]{1,0:T(8,128)(2,1)S(1)} %bitcast.261), channel_id=1, source_target_pairs={{1,0},{2,1},{3,2},{4,3},{5,4},{6,5},{7,6},{8,7},{9,8},{10,9},{11,1... | collective-permute-start | bytes 98312 | tf_op jit(solution)/shard_map/ppermute | solution.py:12
  40.3 8.9 %collective-permute-start.7 = (bf16[16,1024]{1,0:T(8,128)(2,1)S(1)}, bf16[16,1024]{1,0:T(8,128)(2,1)S(1)}, u32[]{:S(2)}, u32[]{:S(2)}) collective-permute-start(bf16[16,1024]{1,0:T(8,128)(2,1)S(1)} %bitcast.255), channel_id=1, source_target_pairs={{0,1},{1,2},{2,3},{3,4},{4,5},{5,6},{6,7},{7,8},{8,9},{9,10},{10,1... | collective-permute-start | bytes 98312 | tf_op jit(solution)/shard_map/ppermute | solution.py:12
  43.0 9.9 %collective-permute-start.8 = (bf16[16,1024]{1,0:T(8,128)(2,1)S(1)}, bf16[16,1024]{1,0:T(8,128)(2,1)S(1)}, u32[]{:S(2)}, u32[]{:S(2)}) collective-permute-start(bf16[16,1024]{1,0:T(8,128)(2,1)S(1)} %bitcast.254), channel_id=1, source_target_pairs={{0,2},{1,3},{2,4},{3,5},{4,6},{5,7},{6,8},{7,9},{8,10},{9,11},{10,... | collective-permute-start | bytes 98312 | tf_op jit(solution)/shard_map/ppermute | solution.py:12
  54.1 15.8 %collective-permute-start.9 = (bf16[16,1024]{1,0:T(8,128)(2,1)S(1)}, bf16[16,1024]{1,0:T(8,128)(2,1)S(1)}, u32[]{:S(2)}, u32[]{:S(2)}) collective-permute-start(bf16[16,1024]{1,0:T(8,128)(2,1)S(1)} %get-tuple-element.20), channel_id=1, source_target_pairs={{0,2},{1,3},{2,4},{3,5},{4,6},{5,7},{6,8},{7,9},{8,10},{9,11},{10,... | collective-permute-start | bytes 98312 | tf_op jit(solution)/shard_map/ppermute | solution.py:12
  56.1 13.8 %collective-permute-start.10 = (bf16[16,1024]{1,0:T(8,128)(2,1)S(1)}, bf16[16,1024]{1,0:T(8,128)(2,1)S(1)}, u32[]{:S(2)}, u32[]{:S(2)}) collective-permute-start(bf16[16,1024]{1,0:T(8,128)(2,1)S(1)} %get-tuple-element.19), channel_id=1, source_target_pairs={{0,1},{1,2},{2,3},{3,4},{4,5},{5,6},{6,7},{7,8},{8,9},{9,10},{10,1... | collective-permute-start | bytes 98312 | tf_op jit(solution)/shard_map/ppermute | solution.py:12
  59.2 10.7 %collective-permute-start.11 = (bf16[16,1024]{1,0:T(8,128)(2,1)S(1)}, bf16[16,1024]{1,0:T(8,128)(2,1)S(1)}, u32[]{:S(2)}, u32[]{:S(2)}) collective-permute-start(bf16[16,1024]{1,0:T(8,128)(2,1)S(1)} %get-tuple-element.17), channel_id=1, source_target_pairs={{1,0},{2,1},{3,2},{4,3},{5,4},{6,5},{7,6},{8,7},{9,8},{10,9},{11,1... | collective-permute-start | bytes 98312 | tf_op jit(solution)/shard_map/ppermute | solution.py:12
  66.5 5.6 %collective-permute-start.12 = (bf16[16,1024]{1,0:T(8,128)(2,1)S(1)}, bf16[16,1024]{1,0:T(8,128)(2,1)S(1)}, u32[]{:S(2)}, u32[]{:S(2)}) collective-permute-start(bf16[16,1024]{1,0:T(8,128)(2,1)S(1)} %get-tuple-element.16), channel_id=1, source_target_pairs={{2,0},{3,1},{4,2},{5,3},{6,4},{7,5},{8,6},{9,7},{10,8},{11,9},{12,... | collective-permute-start | bytes 98312 | tf_op jit(solution)/shard_map/ppermute | solution.py:12
  73.9 9.3 %collective-permute-start.13 = (bf16[8,2048]{1,0:T(8,128)(2,1)S(1)}, bf16[8,2048]{1,0:T(8,128)(2,1)S(1)}, u32[]{:S(2)}, u32[]{:S(2)}) collective-permute-start(bf16[8,2048]{1,0:T(8,128)(2,1)S(1)} %bitcast.262), channel_id=1, source_target_pairs={{128,0},{129,1},{130,2},{131,3},{132,4},{133,5},{134,6},{135,7},{1... | collective-permute-start | bytes 98312 | tf_op jit(solution)/shard_map/ppermute | solution.py:12
where the time goes:
time: 84.4 us; the launch traced here: 84 us
  starting transfers between devices  53.8 us (64%)
  waiting for transfers between devices  13.7 us (16%)
  matrix products  7.66 us (9%)
  local copies, waits for them, and re-layouts  3.85 us (5%)
  other arithmetic  3.73 us (4%)
  between operations  1.18 us (1%)
    ppermute x14, starting transfers between devices, passed_along(): lax.ppermute(value, axis, [(source, source + steps) for source in range(f...  53.8 us
    ppermute x14, waiting for transfers between devices, passed_along(): lax.ppermute(value, axis, [(source, source + steps) for source in range(f...  13.7 us
    dot_general x1, matrix products, local(): jnp.einsum('kl,flc->fkc', mixing[0, 0], column_data, preferred_element_ty...  4.85 us
    broadcast_in_dim x2, other arithmetic, local(): return (rounded[None, None], flux_here[None, None])  3.36 us
    scatter x1, local copies, waits for them, and re-layouts, local(): rounded = mixed.astype(jnp.bfloat16).at[:, 0, :].set(top_level)  1.87 us
  transfers between devices with their start and end apart: 14, of which 5 were waited for; matrix products, arithmetic and copies ran while one was open for 6% of the time, Pallas kernels for 0%

commit v1 on v0

v1 whole, which is shorter than its diff:
```python
import jax
import jax.numpy as jnp
import numpy as np
from jax import lax
from jax.experimental import pallas as pl
from jax.experimental.pallas import tpu as pltpu
from jax.sharding import PartitionSpec as P

step_weight = 0.25
axes = ("sec", "blk")
VMEM = pl.BlockSpec(memory_space=pltpu.VMEM)
SMEM = pl.BlockSpec(memory_space=pltpu.SMEM)
ANY = pl.BlockSpec(memory_space=pl.ANY)


def partner(block, distance, phase, count):
    other = block + distance if (block // distance) % 2 == phase else block - distance
    return other if 0 <= other < count else block


def exchange_pairs(count, phase):
    first = [(b, partner(b, 2, phase, count)) for b in range(count)]
    second = [(count + b, count + partner(b, 1, phase, count)) for b in range(count)]
    return first + second


def swap_pairs(count):
    return [(b, count + b) for b in range(count)] + [(count + b, b) for b in range(count)]


def level_kernel(meta, columns, mixing, lagged, out, buffer, semaphore):
    fields = buffer.shape[0]
    copies = [
        pltpu.make_async_copy(columns.at[0, 0, f], buffer.at[f], semaphore.at[f])
        for f in range(fields)
    ]
    for copy in copies:
        copy.start()
    rows = mixing[0, 0, 0:16, :]
    for f in range(fields):
        copies[f].wait()
        product = jnp.dot(rows, buffer[f], preferred_element_type=jnp.float32)
        level = product + buffer[f, 0:16, :].astype(jnp.float32)
        out[f : f + 1, :] = level[0:1, :]

    @pl.when(meta[0] == 0)
    def _():
        surface = out[...] - step_weight * lagged[0].astype(jnp.float32)
        out[...] = surface.astype(jnp.bfloat16).astype(jnp.float32)


def remap_kernel(meta, atm_tile, ocean_tile, live, surface, weights, first, second, own, tiles, sums):
    count, fields, width = tiles.shape
    for t in range(count):
        tiles[t] = surface[:, t * width : (t + 1) * width]
    sums[...] = jnp.zeros_like(sums)
    slots = live.shape[2]
    half = slots // 2
    jobs = [(g, k) for k in range(slots) for g in (0, 1)]
    jobs += [(2, k) for k in range(half)]
    for g, k in jobs:
        p = meta[1 + g]
        slot = k if g < 2 else k + meta[0] * half
        part = tiles[atm_tile[0, p, slot]].astype(jnp.bfloat16)
        product = jnp.dot(part, weights[0, p, slot], preferred_element_type=jnp.float32)
        product = product.astype(jnp.bfloat16).astype(jnp.float32)
        target = ocean_tile[0, p, slot]
        keep = live[0, p, slot] == 1
        sums[g, target] = sums[g, target] + jnp.where(keep, product, 0.0)
    for t in range(count):
        span = slice(t * width, (t + 1) * width)
        first[:, span] = sums[0, t].astype(jnp.bfloat16)
        second[:, span] = sums[1, t].astype(jnp.bfloat16)
        own[:, span] = sums[2, t]


def back_kernel(meta, atm_tile, ocean_tile, live, first, second, own, weights, out, tiles, sums):
    _, count, fields, width = tiles.shape
    for t in range(count):
        span = slice(t * width, (t + 1) * width)
        tiles[0, t] = first[:, span].astype(jnp.float32)
        tiles[1, t] = second[:, span].astype(jnp.float32)
        tiles[2, t] = own[:, span].astype(jnp.float32)
    sums[...] = jnp.zeros_like(sums)
    slots = live.shape[2]
    half = slots // 2
    jobs = [(g, k) for k in range(slots) for g in (0, 1)]
    jobs += [(2, k) for k in range(half)]
    for i, (g, k) in enumerate(jobs):
        p = meta[1 + g]
        slot = k if g < 2 else k + meta[0] * half
        part = tiles[g, ocean_tile[0, p, slot]].astype(jnp.bfloat16)
        product = lax.dot_general(
            part,
            weights[0, p, slot],
            (((1,), (1,)), ((), ())),
            preferred_element_type=jnp.float32,
        )
        target = atm_tile[0, p, slot]
        keep = live[0, p, slot] * meta[4 + g] == 1
        sums[i % 2, target] = sums[i % 2, target] + jnp.where(keep, product, 0.0)
    for t in range(count):
        out[:, t * width : (t + 1) * width] = sums[0, t] + sums[1, t]


def mix_kernel(columns, mixing, top, out):
    field = pl.program_id(0)
    column = columns[0, 0, 0]
    mixed = column.astype(jnp.float32) + jnp.dot(
        mixing[0, 0], column, preferred_element_type=jnp.float32
    )
    out[0, 0, 0] = mixed.astype(jnp.bfloat16)
    row = lax.broadcasted_iota(jnp.int32, (16, column.shape[1]), 0)
    above = jnp.broadcast_to(top[pl.ds(field, 1), :], (16, column.shape[1]))
    out[0, 0, 0, 0:16, :] = jnp.where(row == 0, above, mixed[0:16, :]).astype(jnp.bfloat16)


def local(
    columns, mixing, lagged_flux, coefficients, ocean_mask, atm_tile, ocean_tile, live, weights
):
    _, _, fields, levels, cells = columns.shape
    width = weights.shape[3]
    tiles = cells // width
    count = lax.axis_size("blk")
    sec = lax.axis_index("sec")
    blk = lax.axis_index("blk")
    table = np.zeros((2, count, 8), np.int32)
    for core in (0, 1):
        for b in range(count):
            others = [partner(b, 2 - core, phase, count) for phase in (1, 0)]
            table[core, b, 0] = core
            table[core, b, 1:3] = [other - b + 2 for other in others]
            table[core, b, 3] = 2
            table[core, b, 4:6] = [other != b for other in others]
            table[core, b, 6] = 1
    meta = lax.dynamic_slice(jnp.asarray(table), (sec, blk, 0), (1, 1, 8)).reshape(8)
    swap = swap_pairs(count)
    wide = exchange_pairs(count, 1)
    near = exchange_pairs(count, 0)
    field_f32 = jax.ShapeDtypeStruct((fields, cells), jnp.float32)
    field_bf16 = jax.ShapeDtypeStruct((fields, cells), jnp.bfloat16)

    level = pl.pallas_call(
        level_kernel,
        out_shape=field_f32,
        in_specs=[SMEM, ANY, VMEM, VMEM],
        out_specs=VMEM,
        scratch_shapes=[
            pltpu.VMEM((fields, levels, cells), jnp.bfloat16),
            pltpu.SemaphoreType.DMA((fields,)),
        ],
        compiler_params=pltpu.CompilerParams(vmem_limit_bytes=24 << 20),
    )(meta, columns, mixing, lagged_flux)
    other_level = lax.ppermute(level, axes, swap)
    is_atm = sec == 0
    surface = jnp.where(is_atm, level, other_level)
    ocean_level = jnp.where(is_atm, other_level, level)

    first, second, own = pl.pallas_call(
        remap_kernel,
        out_shape=(field_bf16, field_bf16, field_f32),
        in_specs=[SMEM, SMEM, SMEM, SMEM, VMEM, VMEM],
        out_specs=(VMEM, VMEM, VMEM),
        scratch_shapes=[
            pltpu.VMEM((tiles, fields, width), jnp.float32),
            pltpu.VMEM((3, tiles, fields, width), jnp.float32),
        ],
        compiler_params=pltpu.CompilerParams(vmem_limit_bytes=24 << 20),
    )(meta, atm_tile, ocean_tile, live, surface, weights)
    got_first = lax.ppermute(first, axes, wide)
    got_second = lax.ppermute(second, axes, near)
    partial = (
        own
        + jnp.where(meta[4] == 1, got_first.astype(jnp.float32), 0.0)
        + jnp.where(meta[5] == 1, got_second.astype(jnp.float32), 0.0)
    )
    remapped = partial + lax.ppermute(partial, axes, swap)

    difference = remapped - ocean_level
    speed = jnp.sqrt(
        difference[0:1] * difference[0:1] + difference[1:2] * difference[1:2] + 1.0
    )
    ocean_flux = (
        coefficients[:, None] * speed * difference * ocean_mask.astype(jnp.float32)
    ).astype(jnp.bfloat16)
    top = jnp.where(
        is_atm, surface, ocean_level + step_weight * ocean_flux.astype(jnp.float32)
    )

    flux_first = lax.ppermute(ocean_flux, axes, wide)
    flux_second = lax.ppermute(ocean_flux, axes, near)

    block = (1, 1, 1, levels, cells)
    new_columns = pl.pallas_call(
        mix_kernel,
        grid=(fields,),
        out_shape=jax.ShapeDtypeStruct(columns.shape, jnp.bfloat16),
        in_specs=[
            pl.BlockSpec(block, lambda f: (0, 0, f, 0, 0)),
            pl.BlockSpec((1, 1, levels, levels), lambda f: (0, 0, 0, 0)),
            pl.BlockSpec((fields, cells), lambda f: (0, 0)),
        ],
        out_specs=pl.BlockSpec(block, lambda f: (0, 0, f, 0, 0)),
        cost_estimate=pl.CostEstimate(
            flops=2 * fields * levels * levels * cells,
            transcendentals=0,
            bytes_accessed=4 * fields * levels * cells,
        ),
        compiler_params=pltpu.CompilerParams(vmem_limit_bytes=24 << 20),
    )(columns, mixing, top)

    half = pl.pallas_call(
        back_kernel,
        out_shape=field_f32,
        in_specs=[SMEM, SMEM, SMEM, SMEM, VMEM, VMEM, VMEM, VMEM],
        out_specs=VMEM,
        scratch_shapes=[
            pltpu.VMEM((3, tiles, fields, width), jnp.float32),
            pltpu.VMEM((2, tiles, fields, width), jnp.float32),
        ],
        compiler_params=pltpu.CompilerParams(vmem_limit_bytes=24 << 20),
    )(meta, atm_tile, ocean_tile, live, flux_first, flux_second, ocean_flux, weights)
    atm_flux = (half + lax.ppermute(half, axes, swap)).astype(jnp.bfloat16)
    flux_here = jnp.where(is_atm, atm_flux, ocean_flux)
    return (new_columns, flux_here[None, None])


def solution(mesh):
    in_specs = (
        P("sec", "blk", None, None, None),
        P("sec", "blk", None, None),
        P("blk", None, None),
        P(),
        P("blk", None),
        P("blk", None, None),
        P("blk", None, None),
        P("blk", None, None),
        P("blk", None, None, None, None),
    )
    out_specs = (P("sec", "blk", None, None, None), P("sec", "blk", None, None))
    return jax.shard_map(local, mesh=mesh, in_specs=in_specs, out_specs=out_specs, check_vma=False)
```

time: 84.4 us -> 46.1 us (0.55)
  starting transfers between devices: 53.8 us -> 21.8 us
  Pallas kernels: 0 us -> 9.81 us
  waiting for transfers between devices: 13.7 us -> 5.33 us
  matrix products: 7.66 us -> 0 us
  other arithmetic: 3.73 us -> 0.81 us
  local copies, waits for them, and re-layouts: 3.85 us -> 5.9 us
  between operations: 1.18 us -> 2.12 us
    ppermute x14 -> x7, starting transfers between devices: 53.8 us -> 21.8 us  [the longest x1 9.86 us: local(): got_first = lax.ppermute(first, axes, wide)]
    pallas_call x0 -> x4, Pallas kernels: none -> 9.81 us  [the longest x1 4.62 us: local(): pl.pallas_call(mix_kernel, grid=(fields,), out_shape=jax.ShapeDtypeStruct...]
    ppermute x14 -> x7, waiting for transfers between devices: 13.7 us -> 5.33 us  [the longest x1 3.57 us: local(): flux_first = lax.ppermute(ocean_flux, axes, wide)]
    dot_general x5 -> x0, matrix products: 7.66 us -> none  [the longest x1 4.85 us: local(): jnp.einsum('kl,flc->fkc', mixing[0, 0], column_data, preferred_element_ty...]
    unnamed x33 -> x25, local copies, waits for them, and re-layouts: 0.17 us -> 3.74 us
    broadcast_in_dim x2 -> x1, other arithmetic: 3.36 us -> 0.63 us  [local(): return (new_columns, flux_here[None, None])]
    scatter x1 -> x0, local copies, waits for them, and re-layouts: 1.87 us -> none  [local(): rounded = mixed.astype(jnp.bfloat16).at[:, 0, :].set(top_level)]
    gather x2 -> x0, local copies, waits for them, and re-layouts: 1.39 us -> none  [the longest x1 0.74 us: local(): flux_tiles[jnp.clip(item_target, 0, tiles - 1)]]
  transfers between devices with their start and end apart: 14 -> 7, of which waited for: 5 -> 3; matrix products, arithmetic and copies ran while one was open for 6% -> 3% of each run, Pallas kernels for 0% -> 10%
where the time goes in v1:
time: 46.1 us; the launch traced here: 45.8 us
  starting transfers between devices  21.8 us (47%)
  Pallas kernels  9.81 us (21%)
  local copies, waits for them, and re-layouts  5.9 us (13%)
  waiting for transfers between devices  5.33 us (12%)
  between operations  2.12 us (5%)
  other arithmetic  0.81 us (2%)
    ppermute x1, starting transfers between devices, local(): got_first = lax.ppermute(first, axes, wide)  9.86 us
    ppermute x1, starting transfers between devices, local(): flux_first = lax.ppermute(ocean_flux, axes, wide)  5.28 us
    pallas_call x1, Pallas kernels, local(): pl.pallas_call(mix_kernel, grid=(fields,), out_shape=jax.ShapeDtypeStruct...  4.62 us
    unnamed x25, local copies, waits for them, and re-layouts  3.74 us
    ppermute x1, waiting for transfers between devices, local(): flux_first = lax.ppermute(ocean_flux, axes, wide)  3.57 us
    ppermute x1, starting transfers between devices, local(): remapped = partial + lax.ppermute(partial, axes, swap)  3.21 us
    pallas_call x1, Pallas kernels, local(): pl.pallas_call(level_kernel, out_shape=field_f32, in_specs=[SMEM, ANY, VM...  2.43 us
    ppermute x1, starting transfers between devices, local(): atm_flux = (half + lax.ppermute(half, axes, swap)).astype(jnp.bfloat16)  1.78 us
  transfers between devices with their start and end apart: 7, of which 3 were waited for; matrix products, arithmetic and copies ran while one was open for 3% of the time, Pallas kernels for 10%

profile of v1, /device:TPU:25, one launch (start us, length us, event | category | flops | bytes accessed | tf_op | source)
XLA Modules:
  0.0 45.8 jit_solution(14842425926499139257)
XLA Ops:
  0.6 0.0 copy-start.7
  0.6 0.0 copy-start.8
  0.7 0.0 copy-start.9
  0.7 0.0 copy-start.6
  0.7 0.0 copy-start.10
  0.7 0.7 %fusion.4.meta = s32[8]{0:T(128)S(1)} fusion(s32[2,128,8]{2,1,0:T(8,128)} %constant.27.clone, s32[]{:T(128)S(6)} %select_n.43, s32[]{:T(128)S(6)} %select_n.44), kind=kLoop, calls=%fused_computation.15 | loop fusion | bytes 72 | tf_op jit(solution)/shard_map/reshape | solution.py:136
  1.4 0.0 copy-start
  1.4 2.2 %copy-done = bf16[1,1,8,128,2048]{4,3,2,1,0:T(8,128)(2,1)S(1)} copy-done((bf16[1,1,8,128,2048]{4,3,2,1,0:T(8,128)(2,1)S(1)}, bf16[1,1,8,128,2048]{4,3,2,1,0:T(8,128)(2,1)}, u32[]{:S(2)}) %copy-start) | copy-done | bytes 4194328
  3.6 0.0 copy-start.3
  3.6 0.8 %copy-done.3 = bf16[1,1,128,128]{3,2,1,0:T(8,128)(2,1)S(1)} copy-done((bf16[1,1,128,128]{3,2,1,0:T(8,128)(2,1)S(1)}, bf16[1,1,128,128]{3,2,1,0:T(8,128)(2,1)}, u32[]{:S(2)}) %copy-start.3) | copy-done | bytes 32792
  4.3 0.0 copy-start.5
  4.4 0.8 %copy-done.5 = bf16[1,8,2048]{2,1,0:T(8,128)(2,1)S(1)} copy-done((bf16[1,8,2048]{2,1,0:T(8,128)(2,1)S(1)}, bf16[1,8,2048]{2,1,0:T(8,128)(2,1)}, u32[]{:S(2)}) %copy-start.5) | copy-done | bytes 32792
  5.1 0.0 copy-start.2
  5.1 2.4 %shard_map.113 = f32[8,2048]{1,0:T(8,128)S(1)} custom-call(s32[8]{0:T(128)S(1)} %fusion.4.meta, bf16[1,1,8,128,2048]{4,3,2,1,0:T(8,128)(2,1)S(1)} %copy-done, bf16[1,1,128,128]{3,2,1,0:T(8,128)(2,1)S(1)} %copy-done.3, bf16[1,8,2048]{2,1,0:T(8,128)(2,1)S(1)} %copy-done.5), custom_call_target="tpu_custom_call" | custom-call | tf_op jit(solution)/shard_map/pallas_call | solution.py:143
  7.5 0.0 copy-start.4
  7.6 0.8 %collective-permute-start = (f32[8,2048]{1,0:T(8,128)S(1)}, f32[8,2048]{1,0:T(8,128)S(1)}, u32[]{:S(2)}, u32[]{:S(2)}) collective-permute-start(f32[8,2048]{1,0:T(8,128)S(1)} %shard_map.113), channel_id=1, source_target_pairs={{0,128},{1,129},{2,130},{3,131},{4,132},{5,133},{6,134},{7,135},{8... | collective-permute-start | bytes 196616 | tf_op jit(solution)/shard_map/ppermute | solution.py:154
  8.3 0.0 copy-done.7
  8.3 0.0 copy-start.1
  8.3 0.0 copy-done.8
  8.4 0.0 copy-done.9
  8.4 0.9 %constant_dynamic-slice_fusion = s32[1,1,8]{2,1,0:T(1,128)S(1)} fusion(s32[2,128,8]{2,1,0:T(8,128)} %constant.27.clone, s32[]{:T(128)S(6)} %select_n.43, s32[]{:T(128)S(6)} %select_n.44), kind=kLoop, calls=%fused_computation.13 | loop fusion | bytes 72 | tf_op jit(solution)/shard_map/dynamic_slice | solution.py:136
  9.2 0.0 collective-permute-done
  9.2 0.0 copy-done.2
  9.3 1.2 %shard_map.114 = (bf16[8,2048]{1,0:T(8,128)(2,1)S(1)}, bf16[8,2048]{1,0:T(8,128)(2,1)S(1)}, f32[8,2048]{1,0:T(8,128)S(1)}) custom-call(s32[8]{0:T(128)S(1)} %fusion.4.meta, s32[1,5,16]{2,1,0:T(8,128)S(1)} %copy.12.atm_tile, s32[1,5,16]{2,1,0:T(8,128)S(1)} %copy.13.ocean_tile, s32[1,5,16]{2,1,0:T(8,128)S(1)} %copy.14.live, ...), custom_call_target="tpu_custom_call" | custom-call | tf_op jit(solution)/shard_map/pallas_call | solution.py:159
  10.5 9.9 %collective-permute-start.1 = (bf16[8,2048]{1,0:T(8,128)(2,1)S(1)}, bf16[8,2048]{1,0:T(8,128)(2,1)S(1)}, u32[]{:S(2)}, u32[]{:S(2)}) collective-permute-start(bf16[8,2048]{1,0:T(8,128)(2,1)S(1)} %get-tuple-element.6), channel_id=1, source_target_pairs={{0,0},{1,1},{2,4},{3,5},{4,2},{5,3},{6,8},{7,9},{8,6},{9,7},{10,12... | collective-permute-start | bytes 98312 | tf_op jit(solution)/shard_map/ppermute | solution.py:170
  20.4 0.1 collective-permute-start.2
  20.5 0.6 %fusion.3 = (s32[1,1,1]{2,1,0:T(1,128)}, s32[1,1,1]{2,1,0:T(1,128)}) fusion(s32[1,1,8]{2,1,0:T(1,128)S(1)} %constant_dynamic-slice_fusion), kind=kLoop, calls=%fused_computation.14 | loop fusion | bytes 16 | tf_op jit(solution)/shard_map/slice | solution.py:174
  22.3 0.0 collective-permute-done.1
  22.4 0.9 %collective-permute-done.2 = bf16[8,2048]{1,0:T(8,128)(2,1)S(1)} collective-permute-done((bf16[8,2048]{1,0:T(8,128)(2,1)S(1)}, bf16[8,2048]{1,0:T(8,128)(2,1)S(1)}, u32[]{:S(2)}, u32[]{:S(2)}) %collective-permute-start.2) | collective-permute-done | bytes 32800 | tf_op jit(solution)/shard_map/ppermute | solution.py:171
  23.2 3.2 %collective-permute-start.3 = (f32[8,2048]{1,0:T(8,128)S(1)}, f32[8,2048]{1,0:T(8,128)S(1)}, u32[]{:S(2)}, u32[]{:S(2)}) collective-permute-start(f32[8,2048]{1,0:T(8,128)S(1)} %select_add_fusion), channel_id=1, source_target_pairs={{0,128},{1,129},{2,130},{3,131},{4,132},{5,133},{6,134},{7,135},{8... | collective-permute-start | bytes 196616 | tf_op jit(solution)/shard_map/ppermute | solution.py:177
  26.4 0.0 copy-done.6
  26.4 0.9 %collective-permute-done.3 = f32[8,2048]{1,0:T(8,128)S(1)} collective-permute-done((f32[8,2048]{1,0:T(8,128)S(1)}, f32[8,2048]{1,0:T(8,128)S(1)}, u32[]{:S(2)}, u32[]{:S(2)}) %collective-permute-start.3) | collective-permute-done | bytes 65568 | tf_op jit(solution)/shard_map/ppermute | solution.py:177
  27.4 0.0 copy-done.10
  27.4 0.1 add_select_fusion
  27.5 0.8 %collective-permute-start.5 = (bf16[8,2048]{1,0:T(8,128)(2,1)S(1)}, bf16[8,2048]{1,0:T(8,128)(2,1)S(1)}, u32[]{:S(2)}, u32[]{:S(2)}) collective-permute-start(bf16[8,2048]{1,0:T(8,128)(2,1)S(1)} %get-tuple-element.9.own), channel_id=1, source_target_pairs={{0,2},{1,3},{2,0},{3,1},{4,6},{5,7},{6,4},{7,5},{8,10},{9,11},{10,... | collective-permute-start | bytes 98312 | tf_op jit(solution)/shard_map/ppermute | solution.py:191
  28.3 5.3 %collective-permute-start.4 = (bf16[8,2048]{1,0:T(8,128)(2,1)S(1)}, bf16[8,2048]{1,0:T(8,128)(2,1)S(1)}, u32[]{:S(2)}, u32[]{:S(2)}) collective-permute-start(bf16[8,2048]{1,0:T(8,128)(2,1)S(1)} %get-tuple-element.9.own), channel_id=1, source_target_pairs={{0,0},{1,1},{2,4},{3,5},{4,2},{5,3},{6,8},{7,9},{8,6},{9,7},{10,12... | collective-permute-start | bytes 98312 | tf_op jit(solution)/shard_map/ppermute | solution.py:190
  33.6 0.0 collective-permute-done.5.second
  33.6 3.6 %collective-permute-done.4.first = bf16[8,2048]{1,0:T(8,128)(2,1)S(1)} collective-permute-done((bf16[8,2048]{1,0:T(8,128)(2,1)S(1)}, bf16[8,2048]{1,0:T(8,128)(2,1)S(1)}, u32[]{:S(2)}, u32[]{:S(2)}) %collective-permute-start.4) | collective-permute-done | bytes 32800 | tf_op jit(solution)/shard_map/ppermute | solution.py:190
  37.2 1.5 %shard_map.116 = f32[8,2048]{1,0:T(8,128)S(1)} custom-call(s32[8]{0:T(128)S(1)} %fusion.4.meta, s32[1,5,16]{2,1,0:T(8,128)S(1)} %copy.12.atm_tile, s32[1,5,16]{2,1,0:T(8,128)S(1)} %copy.13.ocean_tile, s32[1,5,16]{2,1,0:T(8,128)S(1)} %copy.14.live, bf16[8,2048]{1,0:T(8,128)(2,1)S(1)} %collective-permute-done.4.first, ...), custom_call_target="tpu_custom_call" | custom-call | tf_op jit(solution)/shard_map/pallas_call | solution.py:212
  38.7 1.8 %collective-permute-start.6 = (f32[8,2048]{1,0:T(8,128)S(1)}, f32[8,2048]{1,0:T(8,128)S(1)}, u32[]{:S(2)}, u32[]{:S(2)}) collective-permute-start(f32[8,2048]{1,0:T(8,128)S(1)} %shard_map.116), channel_id=1, source_target_pairs={{0,128},{1,129},{2,130},{3,131},{4,132},{5,133},{6,134},{7,135},{8... | collective-permute-start | bytes 196616 | tf_op jit(solution)/shard_map/ppermute | solution.py:223
  40.5 0.0 copy-done.4
  40.5 0.0 copy-done.1
  40.5 4.6 %shard_map.115 = bf16[1,1,8,128,2048]{4,3,2,1,0:T(8,128)(2,1)} custom-call(bf16[1,1,8,128,2048]{4,3,2,1,0:T(8,128)(2,1)S(1)} %copy-done.1, bf16[1,1,128,128]{3,2,1,0:T(8,128)(2,1)S(1)} %copy-done.4, f32[8,2048]{1,0:T(8,128)S(1)} %get-tuple-element.8.top), custom_call_target="tpu_custom_call" | custom-call | flops 536870912 | bytes 8388608 | tf_op jit(solution)/shard_map/pallas_call | solution.py:194
  45.1 0.0 collective-permute-done.6
  45.2 0.6 %fusion.1 = bf16[1,1,8,2048]{3,2,1,0:T(8,128)(2,1)} fusion(bf16[8,2048]{1,0:T(8,128)(2,1)S(1)} %get-tuple-element.9.own, f32[8,2048]{1,0:T(8,128)S(1)} %shard_map.116, f32[8,2048]{1,0:T(8,128)S(1)} %collective-permute-done.6, pred[]{:T(512)S(6)} %eq.15), kind=kLoop, calls=%fused_computation.6 | loop fusion | flops 49152 | bytes 196609 | tf_op jit(solution)/shard_map/broadcast_in_dim | solution.py:225
  (8 shorter events, 0.1 us)
Async XLA Ops:
  0.6 7.7 %copy-start.7 = (s32[1,5,16]{2,0,1:T(1,128)S(1)}, s32[1,5,16]{2,0,1:T(1,128)}, u32[]{:S(2)}) copy-start(s32[1,5,16]{2,0,1:T(1,128)} %param.15) | copy-start | bytes 964
  0.6 7.7 %copy-start.8 = (s32[1,5,16]{2,0,1:T(1,128)S(1)}, s32[1,5,16]{2,0,1:T(1,128)}, u32[]{:S(2)}) copy-start(s32[1,5,16]{2,0,1:T(1,128)} %param.16) | copy-start | bytes 964
  0.7 7.7 %copy-start.9 = (s32[1,5,16]{2,0,1:T(1,128)S(1)}, s32[1,5,16]{2,0,1:T(1,128)}, u32[]{:S(2)}) copy-start(s32[1,5,16]{2,0,1:T(1,128)} %param.17) | copy-start | bytes 964
  0.7 25.8 %copy-start.6 = (s32[1,2048]{1,0:T(1,128)S(1)}, s32[1,2048]{1,0:T(1,128)}, u32[]{:S(2)}) copy-start(s32[1,2048]{1,0:T(1,128)} %param.14) | copy-start | bytes 24580
  0.7 26.7 %copy-start.10 = (f32[8]{0:T(128)S(1)}, f32[8]{0:T(128)}, u32[]{:S(2)}) copy-start(f32[8]{0:T(128)} %param.13) | copy-start | bytes 100
  1.4 2.2 %copy-start = (bf16[1,1,8,128,2048]{4,3,2,1,0:T(8,128)(2,1)S(1)}, bf16[1,1,8,128,2048]{4,3,2,1,0:T(8,128)(2,1)}, u32[]{:S(2)}) copy-start(bf16[1,1,8,128,2048]{4,3,2,1,0:T(8,128)(2,1)} %columns.3) | copy-start | bytes 12582916
  3.6 0.8 %copy-start.3 = (bf16[1,1,128,128]{3,2,1,0:T(8,128)(2,1)S(1)}, bf16[1,1,128,128]{3,2,1,0:T(8,128)(2,1)}, u32[]{:S(2)}) copy-start(bf16[1,1,128,128]{3,2,1,0:T(8,128)(2,1)} %mixing.3) | copy-start | bytes 98308
  4.3 0.8 %copy-start.5 = (bf16[1,8,2048]{2,1,0:T(8,128)(2,1)S(1)}, bf16[1,8,2048]{2,1,0:T(8,128)(2,1)}, u32[]{:S(2)}) copy-start(bf16[1,8,2048]{2,1,0:T(8,128)(2,1)} %lagged.1) | copy-start | bytes 98308
  5.1 4.1 %copy-start.2 = (bf16[1,5,16,128,128]{4,3,2,1,0:T(8,128)(2,1)S(1)}, bf16[1,5,16,128,128]{4,3,2,1,0:T(8,128)(2,1)}, u32[]{:S(2)}) copy-start(bf16[1,5,16,128,128]{4,3,2,1,0:T(8,128)(2,1)} %weights.3) | copy-start | bytes 7864324
  7.5 33.0 %copy-start.4 = (bf16[1,1,128,128]{3,2,1,0:T(8,128)(2,1)S(1)}, bf16[1,1,128,128]{3,2,1,0:T(8,128)(2,1)}, u32[]{:S(2)}) copy-start(bf16[1,1,128,128]{3,2,1,0:T(8,128)(2,1)} %mixing.3) | copy-start | bytes 98308
  7.6 1.7 %collective-permute-start = (f32[8,2048]{1,0:T(8,128)S(1)}, f32[8,2048]{1,0:T(8,128)S(1)}, u32[]{:S(2)}, u32[]{:S(2)}) collective-permute-start(f32[8,2048]{1,0:T(8,128)S(1)} %shard_map.113), channel_id=1, source_target_pairs={{0,128},{1,129},{2,130},{3,131},{4,132},{5,133},{6,134},{7,135},{8... | collective-permute-start | bytes 196616 | tf_op jit(solution)/shard_map/ppermute | solution.py:154
  8.3 32.2 %copy-start.1 = (bf16[1,1,8,128,2048]{4,3,2,1,0:T(8,128)(2,1)S(1)}, bf16[1,1,8,128,2048]{4,3,2,1,0:T(8,128)(2,1)}, u32[]{:S(2)}) copy-start(bf16[1,1,8,128,2048]{4,3,2,1,0:T(8,128)(2,1)} %columns.3) | copy-start | bytes 12582916
  10.5 11.9 %collective-permute-start.1 = (bf16[8,2048]{1,0:T(8,128)(2,1)S(1)}, bf16[8,2048]{1,0:T(8,128)(2,1)S(1)}, u32[]{:S(2)}, u32[]{:S(2)}) collective-permute-start(bf16[8,2048]{1,0:T(8,128)(2,1)S(1)} %get-tuple-element.6), channel_id=1, source_target_pairs={{0,0},{1,1},{2,4},{3,5},{4,2},{5,3},{6,8},{7,9},{8,6},{9,7},{10,12... | collective-permute-start | bytes 98312 | tf_op jit(solution)/shard_map/ppermute | solution.py:170
  20.4 2.9 %collective-permute-start.2 = (bf16[8,2048]{1,0:T(8,128)(2,1)S(1)}, bf16[8,2048]{1,0:T(8,128)(2,1)S(1)}, u32[]{:S(2)}, u32[]{:S(2)}) collective-permute-start(bf16[8,2048]{1,0:T(8,128)(2,1)S(1)} %get-tuple-element.7), channel_id=1, source_target_pairs={{0,2},{1,3},{2,0},{3,1},{4,6},{5,7},{6,4},{7,5},{8,10},{9,11},{10,... | collective-permute-start | bytes 98312 | tf_op jit(solution)/shard_map/ppermute | solution.py:171
  23.2 4.1 %collective-permute-start.3 = (f32[8,2048]{1,0:T(8,128)S(1)}, f32[8,2048]{1,0:T(8,128)S(1)}, u32[]{:S(2)}, u32[]{:S(2)}) collective-permute-start(f32[8,2048]{1,0:T(8,128)S(1)} %select_add_fusion), channel_id=1, source_target_pairs={{0,128},{1,129},{2,130},{3,131},{4,132},{5,133},{6,134},{7,135},{8... | collective-permute-start | bytes 196616 | tf_op jit(solution)/shard_map/ppermute | solution.py:177
  27.5 6.1 %collective-permute-start.5 = (bf16[8,2048]{1,0:T(8,128)(2,1)S(1)}, bf16[8,2048]{1,0:T(8,128)(2,1)S(1)}, u32[]{:S(2)}, u32[]{:S(2)}) collective-permute-start(bf16[8,2048]{1,0:T(8,128)(2,1)S(1)} %get-tuple-element.9.own), channel_id=1, source_target_pairs={{0,2},{1,3},{2,0},{3,1},{4,6},{5,7},{6,4},{7,5},{8,10},{9,11},{10,... | collective-permute-start | bytes 98312 | tf_op jit(solution)/shard_map/ppermute | solution.py:191
  28.3 8.9 %collective-permute-start.4 = (bf16[8,2048]{1,0:T(8,128)(2,1)S(1)}, bf16[8,2048]{1,0:T(8,128)(2,1)S(1)}, u32[]{:S(2)}, u32[]{:S(2)}) collective-permute-start(bf16[8,2048]{1,0:T(8,128)(2,1)S(1)} %get-tuple-element.9.own), channel_id=1, source_target_pairs={{0,0},{1,1},{2,4},{3,5},{4,2},{5,3},{6,8},{7,9},{8,6},{9,7},{10,12... | collective-permute-start | bytes 98312 | tf_op jit(solution)/shard_map/ppermute | solution.py:190
  38.7 6.4 %collective-permute-start.6 = (f32[8,2048]{1,0:T(8,128)S(1)}, f32[8,2048]{1,0:T(8,128)S(1)}, u32[]{:S(2)}, u32[]{:S(2)}) collective-permute-start(f32[8,2048]{1,0:T(8,128)S(1)} %shard_map.116), channel_id=1, source_target_pairs={{0,128},{1,129},{2,130},{3,131},{4,132},{5,133},{6,134},{7,135},{8... | collective-permute-start | bytes 196616 | tf_op jit(solution)/shard_map/ppermute | solution.py:223

commit v2 on v1

v2 whole, which is shorter than its diff:
```python
import jax
import jax.numpy as jnp
from jax import lax
from jax.experimental import pallas as pl
from jax.experimental.pallas import tpu as pltpu
from jax.sharding import PartitionSpec as P

step_weight = 0.25
axes = ("sec", "blk")
VMEM = pl.BlockSpec(memory_space=pltpu.VMEM)
SMEM = pl.BlockSpec(memory_space=pltpu.SMEM)
ANY = pl.BlockSpec(memory_space=pl.ANY)
HBM = pl.BlockSpec(memory_space=pltpu.HBM)


def partner(block, distance, phase, count):
    other = block + distance if (block // distance) % 2 == phase else block - distance
    return other if 0 <= other < count else block


def exchange_pairs(count, phase):
    first = [(b, partner(b, 2, phase, count)) for b in range(count)]
    second = [(count + b, count + partner(b, 1, phase, count)) for b in range(count)]
    return first + second


def swap_pairs(count):
    return [(b, count + b) for b in range(count)] + [(count + b, b) for b in range(count)]


def place():
    count = lax.axis_size("blk")
    core = lax.axis_index("sec")
    block = lax.axis_index("blk")
    reach = 2 - core
    shift = 1 - core
    place_in_pair = jnp.bitwise_and(lax.shift_right_logical(block, shift), 1)
    wide_step = jnp.where(place_in_pair == 1, reach, -reach)
    near_step = -wide_step
    found = []
    for step in (wide_step, near_step):
        other = block + step
        found.append(jnp.logical_and(other >= 0, other < count))
    return core, (wide_step + 2, near_step + 2), found


def level_kernel(columns, mixing, lagged, out, buffer, rows, late, semaphore, extra):
    fields = buffer.shape[0]
    small = [
        pltpu.make_async_copy(mixing.at[0, 0, 0:16], rows, extra.at[0]),
        pltpu.make_async_copy(lagged.at[0], late, extra.at[1]),
    ]
    copies = [
        pltpu.make_async_copy(columns.at[0, 0, f], buffer.at[f], semaphore.at[f])
        for f in range(fields)
    ]
    small[0].start()
    for copy in copies:
        copy.start()
    small[1].start()
    small[0].wait()
    for f in range(fields):
        copies[f].wait()
        product = jnp.dot(rows[...], buffer[f], preferred_element_type=jnp.float32)
        level = product + buffer[f, 0:16, :].astype(jnp.float32)
        out[f : f + 1, :] = level[0:1, :]
    small[1].wait()

    @pl.when(lax.axis_index("sec") == 0)
    def _():
        surface = out[...] - step_weight * late[...].astype(jnp.float32)
        out[...] = surface.astype(jnp.bfloat16).astype(jnp.float32)


def slot_jobs(core, distances, slots):
    half = slots // 2
    jobs = [(g, distances[g], k) for k in range(slots) for g in (0, 1)]
    return jobs + [(2, 2, k + core * half) for k in range(half)]


def remap_kernel(codes, surface, weights, first, second, own, tiles, sums):
    count, fields, width = tiles.shape
    core, distances, _ = place()
    for t in range(count):
        tiles[t] = surface[:, t * width : (t + 1) * width]
    sums[...] = jnp.zeros_like(sums)
    for g, p, slot in slot_jobs(core, distances, weights.shape[2]):
        code = codes[0, p, slot]
        part = tiles[jnp.bitwise_and(code, 255)].astype(jnp.bfloat16)
        product = jnp.dot(part, weights[0, p, slot], preferred_element_type=jnp.float32)
        product = product.astype(jnp.bfloat16).astype(jnp.float32)
        target = jnp.bitwise_and(lax.shift_right_logical(code, 8), 255)
        keep = lax.shift_right_logical(code, 16) == 1
        sums[g, target] = sums[g, target] + jnp.where(keep, product, 0.0)
    for t in range(count):
        span = slice(t * width, (t + 1) * width)
        first[:, span] = sums[0, t].astype(jnp.bfloat16)
        second[:, span] = sums[1, t].astype(jnp.bfloat16)
        own[:, span] = sums[2, t]


def back_kernel(codes, second, first, own, weights, after, out, tiles, sums):
    del after
    _, count, fields, width = tiles.shape
    core, distances, found = place()
    for t in range(count):
        span = slice(t * width, (t + 1) * width)
        tiles[0, t] = first[:, span].astype(jnp.float32)
        tiles[1, t] = second[:, span].astype(jnp.float32)
        tiles[2, t] = own[:, span].astype(jnp.float32)
    sums[...] = jnp.zeros_like(sums)
    for i, (g, p, slot) in enumerate(slot_jobs(core, distances, weights.shape[2])):
        code = codes[0, p, slot]
        source = jnp.bitwise_and(lax.shift_right_logical(code, 8), 255)
        part = tiles[g, source].astype(jnp.bfloat16)
        product = lax.dot_general(
            part,
            weights[0, p, slot],
            (((1,), (1,)), ((), ())),
            preferred_element_type=jnp.float32,
        )
        target = jnp.bitwise_and(code, 255)
        keep = lax.shift_right_logical(code, 16) == 1
        if g < 2:
            keep = jnp.logical_and(keep, found[g])
        sums[i % 2, target] = sums[i % 2, target] + jnp.where(keep, product, 0.0)
    for t in range(count):
        out[:, t * width : (t + 1) * width] = sums[0, t] + sums[1, t]


def mix_kernel(columns, mixing, top, out, done):
    done[...] = jnp.zeros_like(done)
    field = pl.program_id(0)
    column = columns[0, 0, 0]
    mixed = column.astype(jnp.float32) + jnp.dot(
        mixing[0, 0], column, preferred_element_type=jnp.float32
    )
    out[0, 0, 0] = mixed.astype(jnp.bfloat16)
    row = lax.broadcasted_iota(jnp.int32, (16, column.shape[1]), 0)
    above = jnp.broadcast_to(top[pl.ds(field, 1), :], (16, column.shape[1]))
    out[0, 0, 0, 0:16, :] = jnp.where(row == 0, above, mixed[0:16, :]).astype(jnp.bfloat16)


def local(
    columns, mixing, lagged_flux, coefficients, ocean_mask, atm_tile, ocean_tile, live, weights
):
    _, _, fields, levels, cells = columns.shape
    width = weights.shape[3]
    tiles = cells // width
    count = lax.axis_size("blk")
    core, _, found = place()
    codes = atm_tile + 256 * ocean_tile + 65536 * live
    swap = swap_pairs(count)
    wide = exchange_pairs(count, 1)
    near = exchange_pairs(count, 0)
    field_f32 = jax.ShapeDtypeStruct((fields, cells), jnp.float32)
    field_bf16 = jax.ShapeDtypeStruct((fields, cells), jnp.bfloat16)

    level = pl.pallas_call(
        level_kernel,
        out_shape=field_f32,
        in_specs=[HBM, HBM, HBM],
        out_specs=VMEM,
        scratch_shapes=[
            pltpu.VMEM((fields, levels, cells), jnp.bfloat16),
            pltpu.VMEM((16, levels), jnp.bfloat16),
            pltpu.VMEM((fields, cells), jnp.bfloat16),
            pltpu.SemaphoreType.DMA((fields,)),
            pltpu.SemaphoreType.DMA((2,)),
        ],
        compiler_params=pltpu.CompilerParams(vmem_limit_bytes=24 << 20),
    )(*(pltpu.with_memory_space_constraint(x, pltpu.HBM) for x in (columns, mixing, lagged_flux)))
    level, weights = lax.optimization_barrier((level, weights))
    other_level = lax.ppermute(level, axes, swap)
    is_atm = core == 0
    surface = jnp.where(is_atm, level, other_level)
    ocean_level = jnp.where(is_atm, other_level, level)

    first, second, own = pl.pallas_call(
        remap_kernel,
        out_shape=(field_bf16, field_bf16, field_f32),
        in_specs=[SMEM, VMEM, VMEM],
        out_specs=(VMEM, VMEM, VMEM),
        scratch_shapes=[
            pltpu.VMEM((tiles, fields, width), jnp.float32),
            pltpu.VMEM((3, tiles, fields, width), jnp.float32),
        ],
        compiler_params=pltpu.CompilerParams(vmem_limit_bytes=24 << 20),
    )(codes, surface, weights)
    got_first = lax.ppermute(first, axes, wide)
    got_second = lax.ppermute(second, axes, near)
    partial = (
        own
        + jnp.where(found[0], got_first.astype(jnp.float32), 0.0)
        + jnp.where(found[1], got_second.astype(jnp.float32), 0.0)
    )
    remapped = partial + lax.ppermute(partial, axes, swap)

    difference = remapped - ocean_level
    speed = jnp.sqrt(
        difference[0:1] * difference[0:1] + difference[1:2] * difference[1:2] + 1.0
    )
    ocean_flux = (
        coefficients[:, None] * speed * difference * ocean_mask.astype(jnp.float32)
    ).astype(jnp.bfloat16)
    top = jnp.where(
        is_atm, surface, ocean_level + step_weight * ocean_flux.astype(jnp.float32)
    )

    flux_first = lax.ppermute(ocean_flux, axes, wide)
    flux_second = lax.ppermute(ocean_flux, axes, near)

    block = (1, 1, 1, levels, cells)
    new_columns, done = pl.pallas_call(
        mix_kernel,
        grid=(fields,),
        out_shape=(
            jax.ShapeDtypeStruct(columns.shape, jnp.bfloat16),
            jax.ShapeDtypeStruct((8, 128), jnp.float32),
        ),
        in_specs=[
            pl.BlockSpec(block, lambda f: (0, 0, f, 0, 0)),
            pl.BlockSpec((1, 1, levels, levels), lambda f: (0, 0, 0, 0)),
            pl.BlockSpec((fields, cells), lambda f: (0, 0)),
        ],
        out_specs=(
            pl.BlockSpec(block, lambda f: (0, 0, f, 0, 0)),
            pl.BlockSpec((8, 128), lambda f: (0, 0)),
        ),
        cost_estimate=pl.CostEstimate(
            flops=2 * fields * levels * levels * cells,
            transcendentals=0,
            bytes_accessed=4 * fields * levels * cells,
        ),
        compiler_params=pltpu.CompilerParams(vmem_limit_bytes=24 << 20),
    )(pltpu.with_memory_space_constraint(columns, pltpu.HBM), mixing, top)

    half = pl.pallas_call(
        back_kernel,
        out_shape=field_f32,
        in_specs=[SMEM, VMEM, VMEM, VMEM, VMEM, ANY],
        out_specs=VMEM,
        scratch_shapes=[
            pltpu.VMEM((3, tiles, fields, width), jnp.float32),
            pltpu.VMEM((2, tiles, fields, width), jnp.float32),
        ],
        compiler_params=pltpu.CompilerParams(vmem_limit_bytes=24 << 20),
    )(codes, flux_second, flux_first, ocean_flux, weights, done)
    atm_flux = (half + lax.ppermute(half, axes, swap)).astype(jnp.bfloat16)
    flux_here = jnp.where(is_atm, atm_flux, ocean_flux)
    return (new_columns, flux_here[None, None])


def solution(mesh):
    in_specs = (
        P("sec", "blk", None, None, None),
        P("sec", "blk", None, None),
        P("blk", None, None),
        P(),
        P("blk", None),
        P("blk", None, None),
        P("blk", None, None),
        P("blk", None, None),
        P("blk", None, None, None, None),
    )
    out_specs = (P("sec", "blk", None, None, None), P("sec", "blk", None, None))
    return jax.shard_map(local, mesh=mesh, in_specs=in_specs, out_specs=out_specs, check_vma=False)
```

time: 46.1 us -> 41.4 us (0.90)
  local copies, waits for them, and re-layouts: 5.9 us -> 0.03 us
  Pallas kernels: 9.81 us -> 13.6 us
  starting transfers between devices: 21.8 us -> 20.5 us
  between operations: 2.12 us -> 0.83 us
    pallas_call x3, Pallas kernels: 8.59 us -> 12.5 us  [the longest x1 7.47 us: local(): pl.pallas_call(mix_kernel, grid=(fields,), out_shape=(jax.ShapeDtypeStruc...]
    unnamed x25 -> x14, local copies, waits for them, and re-layouts: 3.74 us -> 0.03 us
    ppermute x1, waiting for transfers between devices: 3.57 us -> 0.01 us  [local(): flux_first = lax.ppermute(ocean_flux, axes, wide)]
    ppermute x1, waiting for transfers between devices: 0.01 us -> 1.17 us  [local(): got_first = lax.ppermute(first, axes, wide)]
    ppermute x1, waiting for transfers between devices: 0.01 us -> 0.9 us  [local(): atm_flux = (half + lax.ppermute(half, axes, swap)).astype(jnp.bfloat16)]
    ppermute x1, waiting for transfers between devices: 0.01 us -> 0.88 us  [local(): other_level = lax.ppermute(level, axes, swap)]
    dynamic_slice x1 -> x0, local copies, waits for them, and re-layouts: 0.85 us -> none  [local(): lax.dynamic_slice(jnp.asarray(table), (sec, blk, 0), (1, 1, 8)).reshape(8)]
    ppermute x1, starting transfers between devices: 0.82 us -> 0.09 us  [local(): flux_second = lax.ppermute(ocean_flux, axes, near)]
  transfers between devices with their start and end apart: 7 -> 7, of which waited for: 3 -> 5; matrix products, arithmetic and copies ran while one was open for 3% -> 0% of each run, Pallas kernels for 10% -> 18%
where the time goes in v2:
time: 41.4 us; the launch traced here: 41.2 us
  starting transfers between devices  20.5 us (50%)
  Pallas kernels  13.6 us (33%)
  waiting for transfers between devices  5.4 us (13%)
  between operations  0.83 us (2%)
  other arithmetic  0.81 us (2%)
    ppermute x1, starting transfers between devices, local(): got_first = lax.ppermute(first, axes, wide)  9.85 us
    pallas_call x1, Pallas kernels, local(): pl.pallas_call(mix_kernel, grid=(fields,), out_shape=(jax.ShapeDtypeStruc...  7.47 us
    ppermute x1, starting transfers between devices, local(): flux_first = lax.ppermute(ocean_flux, axes, wide)  5.3 us
    pallas_call x1, Pallas kernels, local(): pl.pallas_call(level_kernel, out_shape=field_f32, in_specs=[HBM, HBM, HBM...  3.61 us
    ppermute x1, starting transfers between devices, local(): remapped = partial + lax.ppermute(partial, axes, swap)  3.22 us
    ppermute x1, waiting for transfers between devices, local(): got_second = lax.ppermute(second, axes, near)  1.56 us
    pallas_call x1, Pallas kernels, local(): pl.pallas_call(back_kernel, out_shape=field_f32, in_specs=[SMEM, VMEM, VM...  1.42 us
    ppermute x1, waiting for transfers between devices, local(): got_first = lax.ppermute(first, axes, wide)  1.17 us
  transfers between devices with their start and end apart: 7, of which 5 were waited for; matrix products, arithmetic and copies ran while one was open for 0% of the time, Pallas kernels for 18%

profile of v2, /device:TPU:25, one launch (start us, length us, event | category | flops | bytes accessed | tf_op | source)
XLA Modules:
  0.0 41.2 jit_solution(17632184802174297715)
XLA Ops:
  0.6 0.0 copy-start.1
  0.6 0.0 copy-start
  0.7 0.0 copy-start.3
  0.7 0.0 copy-start.5
  0.7 0.0 copy-start.4
  0.7 0.0 copy-start.2
  0.7 0.0 copy-start.6
  0.7 3.6 %shard_map.104 = f32[8,2048]{1,0:T(8,128)S(1)} custom-call(bf16[1,1,8,128,2048]{4,3,2,1,0:T(8,128)(2,1)} %columns.3, bf16[1,1,128,128]{3,2,1,0:T(8,128)(2,1)} %mixing.3, bf16[1,8,2048]{2,1,0:T(8,128)(2,1)} %lagged.1), custom_call_target="tpu_custom_call" | custom-call | tf_op jit(solution)/shard_map/pallas_call | solution.py:159
  4.3 0.8 %collective-permute-start = (f32[8,2048]{1,0:T(8,128)S(1)}, f32[8,2048]{1,0:T(8,128)S(1)}, u32[]{:S(2)}, u32[]{:S(2)}) collective-permute-start(f32[8,2048]{1,0:T(8,128)S(1)} %shard_map.104), channel_id=1, source_target_pairs={{0,128},{1,129},{2,130},{3,131},{4,132},{5,133},{6,134},{7,135},{8... | collective-permute-start | bytes 196616 | tf_op jit(solution)/shard_map/ppermute | solution.py:174
  5.1 0.0 copy-done.3
  5.1 0.0 copy-done.5
  5.1 0.0 copy-done.4
  5.1 0.9 %collective-permute-done = f32[8,2048]{1,0:T(8,128)S(1)} collective-permute-done((f32[8,2048]{1,0:T(8,128)S(1)}, f32[8,2048]{1,0:T(8,128)S(1)}, u32[]{:S(2)}, u32[]{:S(2)}) %collective-permute-start) | collective-permute-done | bytes 65568 | tf_op jit(solution)/shard_map/ppermute | solution.py:174
  6.0 0.0 copy-done
  6.0 1.1 %shard_map.105 = (bf16[8,2048]{1,0:T(8,128)(2,1)S(1)}, bf16[8,2048]{1,0:T(8,128)(2,1)S(1)}, f32[8,2048]{1,0:T(8,128)S(1)}) custom-call(s32[1,5,16]{2,1,0:T(8,128)S(1)} %fusion.3.codes, f32[8,2048]{1,0:T(8,128)S(1)} %broadcast_select_fusion.1.surface, bf16[1,5,16,128,128]{4,3,2,1,0:T(8,128)(2,1)S(1)} %copy-done), custom_call_target="tpu_custom_call" | custom-call | tf_op jit(solution)/shard_map/pallas_call | solution.py:179
  7.1 9.9 %collective-permute-start.1 = (bf16[8,2048]{1,0:T(8,128)(2,1)S(1)}, bf16[8,2048]{1,0:T(8,128)(2,1)S(1)}, u32[]{:S(2)}, u32[]{:S(2)}) collective-permute-start(bf16[8,2048]{1,0:T(8,128)(2,1)S(1)} %get-tuple-element.12), channel_id=1, source_target_pairs={{0,0},{1,1},{2,4},{3,5},{4,2},{5,3},{6,8},{7,9},{8,6},{9,7},{10,12... | collective-permute-start | bytes 98312 | tf_op jit(solution)/shard_map/ppermute | solution.py:190
  17.0 0.1 collective-permute-start.2
  17.1 1.2 %collective-permute-done.1 = bf16[8,2048]{1,0:T(8,128)(2,1)S(1)} collective-permute-done((bf16[8,2048]{1,0:T(8,128)(2,1)S(1)}, bf16[8,2048]{1,0:T(8,128)(2,1)S(1)}, u32[]{:S(2)}, u32[]{:S(2)}) %collective-permute-start.1) | collective-permute-done | bytes 32800 | tf_op jit(solution)/shard_map/ppermute | solution.py:190
  18.3 1.6 %collective-permute-done.2 = bf16[8,2048]{1,0:T(8,128)(2,1)S(1)} collective-permute-done((bf16[8,2048]{1,0:T(8,128)(2,1)S(1)}, bf16[8,2048]{1,0:T(8,128)(2,1)S(1)}, u32[]{:S(2)}, u32[]{:S(2)}) %collective-permute-start.2) | collective-permute-done | bytes 32800 | tf_op jit(solution)/shard_map/ppermute | solution.py:191
  19.9 3.2 %collective-permute-start.3 = (f32[8,2048]{1,0:T(8,128)S(1)}, f32[8,2048]{1,0:T(8,128)S(1)}, u32[]{:S(2)}, u32[]{:S(2)}) collective-permute-start(f32[8,2048]{1,0:T(8,128)S(1)} %select_add_fusion), channel_id=1, source_target_pairs={{0,128},{1,129},{2,130},{3,131},{4,132},{5,133},{6,134},{7,135},{8... | collective-permute-start | bytes 196616 | tf_op jit(solution)/shard_map/ppermute | solution.py:197
  23.1 0.0 copy-done.2
  23.1 0.9 %collective-permute-done.3 = f32[8,2048]{1,0:T(8,128)S(1)} collective-permute-done((f32[8,2048]{1,0:T(8,128)S(1)}, f32[8,2048]{1,0:T(8,128)S(1)}, u32[]{:S(2)}, u32[]{:S(2)}) %collective-permute-start.3) | collective-permute-done | bytes 65568 | tf_op jit(solution)/shard_map/ppermute | solution.py:197
  24.0 0.0 copy-done.6
  24.1 0.1 add_select_fusion
  24.1 5.3 %collective-permute-start.5 = (bf16[8,2048]{1,0:T(8,128)(2,1)S(1)}, bf16[8,2048]{1,0:T(8,128)(2,1)S(1)}, u32[]{:S(2)}, u32[]{:S(2)}) collective-permute-start(bf16[8,2048]{1,0:T(8,128)(2,1)S(1)} %get-tuple-element.17.own), channel_id=1, source_target_pairs={{0,0},{1,1},{2,4},{3,5},{4,2},{5,3},{6,8},{7,9},{8,6},{9,7},{10,12... | collective-permute-start | bytes 98312 | tf_op jit(solution)/shard_map/ppermute | solution.py:210
  29.4 0.1 collective-permute-start.4
  29.6 0.0 copy-done.1
  29.6 7.5 %shard_map.106 = (bf16[1,1,8,128,2048]{4,3,2,1,0:T(8,128)(2,1)}, f32[8,128]{1,0:T(8,128)S(1)}) custom-call(bf16[1,1,8,128,2048]{4,3,2,1,0:T(8,128)(2,1)} %columns.3, bf16[1,1,128,128]{3,2,1,0:T(8,128)(2,1)S(1)} %copy-done.1, f32[8,2048]{1,0:T(8,128)S(1)} %get-tuple-element.16.top), custom_call_target="tpu_custom_call" | custom-call | flops 536870912 | bytes 8388608 | tf_op jit(solution)/shard_map/pallas_call | solution.py:214
  37.0 0.0 collective-permute-done.5.first
  37.0 0.0 collective-permute-done.4.second
  37.0 1.4 %shard_map.107 = f32[8,2048]{1,0:T(8,128)S(1)} custom-call(s32[1,5,16]{2,1,0:T(8,128)S(1)} %fusion.3.codes, bf16[8,2048]{1,0:T(8,128)(2,1)S(1)} %collective-permute-done.4.second, bf16[8,2048]{1,0:T(8,128)(2,1)S(1)} %collective-permute-done.5.first, bf16[8,2048]{1,0:T(8,128)(2,1)S(1)} %get-tuple-element.17.own, bf16[1,5,16,128,128]{4,3,2,1,0:T(8,128)(2,1)S(1)} %copy-done, ...), custom_call_target="tpu_custom_call" | custom-call | tf_op jit(solution)/shard_map/pallas_call | solution.py:238
  38.5 1.2 %collective-permute-start.6 = (f32[8,2048]{1,0:T(8,128)S(1)}, f32[8,2048]{1,0:T(8,128)S(1)}, u32[]{:S(2)}, u32[]{:S(2)}) collective-permute-start(f32[8,2048]{1,0:T(8,128)S(1)} %shard_map.107), channel_id=1, source_target_pairs={{0,128},{1,129},{2,130},{3,131},{4,132},{5,133},{6,134},{7,135},{8... | collective-permute-start | bytes 196616 | tf_op jit(solution)/shard_map/ppermute | solution.py:249
  39.6 0.9 %collective-permute-done.6 = f32[8,2048]{1,0:T(8,128)S(1)} collective-permute-done((f32[8,2048]{1,0:T(8,128)S(1)}, f32[8,2048]{1,0:T(8,128)S(1)}, u32[]{:S(2)}, u32[]{:S(2)}) %collective-permute-start.6) | collective-permute-done | bytes 65568 | tf_op jit(solution)/shard_map/ppermute | solution.py:249
  40.5 0.6 %fusion.1 = bf16[1,1,8,2048]{3,2,1,0:T(8,128)(2,1)} fusion(bf16[8,2048]{1,0:T(8,128)(2,1)S(1)} %get-tuple-element.17.own, f32[8,2048]{1,0:T(8,128)S(1)} %shard_map.107, f32[8,2048]{1,0:T(8,128)S(1)} %collective-permute-done.6, pred[]{:T(512)S(6)} %eq.6), kind=kLoop, calls=%fused_computation.6 | loop fusion | flops 49152 | bytes 196609 | tf_op jit(solution)/shard_map/broadcast_in_dim | solution.py:251
  (6 shorter events, 0.1 us)
Async XLA Ops:
  0.6 28.9 %copy-start.1 = (bf16[1,1,128,128]{3,2,1,0:T(8,128)(2,1)S(1)}, bf16[1,1,128,128]{3,2,1,0:T(8,128)(2,1)}, u32[]{:S(2)}) copy-start(bf16[1,1,128,128]{3,2,1,0:T(8,128)(2,1)} %mixing.3) | copy-start | bytes 98308
  0.6 5.4 %copy-start = (bf16[1,5,16,128,128]{4,3,2,1,0:T(8,128)(2,1)S(1)}, bf16[1,5,16,128,128]{4,3,2,1,0:T(8,128)(2,1)}, u32[]{:S(2)}) copy-start(bf16[1,5,16,128,128]{4,3,2,1,0:T(8,128)(2,1)} %weights.1) | copy-start | bytes 7864324
  0.7 4.4 %copy-start.3 = (s32[1,5,16]{2,0,1:T(1,128)S(1)}, s32[1,5,16]{2,0,1:T(1,128)}, u32[]{:S(2)}) copy-start(s32[1,5,16]{2,0,1:T(1,128)} %param.16) | copy-start | bytes 964
  0.7 4.4 %copy-start.5 = (s32[1,5,16]{2,0,1:T(1,128)S(1)}, s32[1,5,16]{2,0,1:T(1,128)}, u32[]{:S(2)}) copy-start(s32[1,5,16]{2,0,1:T(1,128)} %param.15) | copy-start | bytes 964
  0.7 4.4 %copy-start.4 = (s32[1,5,16]{2,0,1:T(1,128)S(1)}, s32[1,5,16]{2,0,1:T(1,128)}, u32[]{:S(2)}) copy-start(s32[1,5,16]{2,0,1:T(1,128)} %param.14) | copy-start | bytes 964
  0.7 22.4 %copy-start.2 = (s32[1,2048]{1,0:T(1,128)S(1)}, s32[1,2048]{1,0:T(1,128)}, u32[]{:S(2)}) copy-start(s32[1,2048]{1,0:T(1,128)} %param.13) | copy-start | bytes 24580
  0.7 23.4 %copy-start.6 = (f32[8]{0:T(128)S(1)}, f32[8]{0:T(128)}, u32[]{:S(2)}) copy-start(f32[8]{0:T(128)} %param.12) | copy-start | bytes 100
  4.3 1.7 %collective-permute-start = (f32[8,2048]{1,0:T(8,128)S(1)}, f32[8,2048]{1,0:T(8,128)S(1)}, u32[]{:S(2)}, u32[]{:S(2)}) collective-permute-start(f32[8,2048]{1,0:T(8,128)S(1)} %shard_map.104), channel_id=1, source_target_pairs={{0,128},{1,129},{2,130},{3,131},{4,132},{5,133},{6,134},{7,135},{8... | collective-permute-start | bytes 196616 | tf_op jit(solution)/shard_map/ppermute | solution.py:174
  7.1 11.2 %collective-permute-start.1 = (bf16[8,2048]{1,0:T(8,128)(2,1)S(1)}, bf16[8,2048]{1,0:T(8,128)(2,1)S(1)}, u32[]{:S(2)}, u32[]{:S(2)}) collective-permute-start(bf16[8,2048]{1,0:T(8,128)(2,1)S(1)} %get-tuple-element.12), channel_id=1, source_target_pairs={{0,0},{1,1},{2,4},{3,5},{4,2},{5,3},{6,8},{7,9},{8,6},{9,7},{10,12... | collective-permute-start | bytes 98312 | tf_op jit(solution)/shard_map/ppermute | solution.py:190
  17.0 2.9 %collective-permute-start.2 = (bf16[8,2048]{1,0:T(8,128)(2,1)S(1)}, bf16[8,2048]{1,0:T(8,128)(2,1)S(1)}, u32[]{:S(2)}, u32[]{:S(2)}) collective-permute-start(bf16[8,2048]{1,0:T(8,128)(2,1)S(1)} %get-tuple-element.13), channel_id=1, source_target_pairs={{0,2},{1,3},{2,0},{3,1},{4,6},{5,7},{6,4},{7,5},{8,10},{9,11},{10,... | collective-permute-start | bytes 98312 | tf_op jit(solution)/shard_map/ppermute | solution.py:191
  19.9 4.1 %collective-permute-start.3 = (f32[8,2048]{1,0:T(8,128)S(1)}, f32[8,2048]{1,0:T(8,128)S(1)}, u32[]{:S(2)}, u32[]{:S(2)}) collective-permute-start(f32[8,2048]{1,0:T(8,128)S(1)} %select_add_fusion), channel_id=1, source_target_pairs={{0,128},{1,129},{2,130},{3,131},{4,132},{5,133},{6,134},{7,135},{8... | collective-permute-start | bytes 196616 | tf_op jit(solution)/shard_map/ppermute | solution.py:197
  24.1 12.9 %collective-permute-start.5 = (bf16[8,2048]{1,0:T(8,128)(2,1)S(1)}, bf16[8,2048]{1,0:T(8,128)(2,1)S(1)}, u32[]{:S(2)}, u32[]{:S(2)}) collective-permute-start(bf16[8,2048]{1,0:T(8,128)(2,1)S(1)} %get-tuple-element.17.own), channel_id=1, source_target_pairs={{0,0},{1,1},{2,4},{3,5},{4,2},{5,3},{6,8},{7,9},{8,6},{9,7},{10,12... | collective-permute-start | bytes 98312 | tf_op jit(solution)/shard_map/ppermute | solution.py:210
  29.4 7.6 %collective-permute-start.4 = (bf16[8,2048]{1,0:T(8,128)(2,1)S(1)}, bf16[8,2048]{1,0:T(8,128)(2,1)S(1)}, u32[]{:S(2)}, u32[]{:S(2)}) collective-permute-start(bf16[8,2048]{1,0:T(8,128)(2,1)S(1)} %get-tuple-element.17.own), channel_id=1, source_target_pairs={{0,2},{1,3},{2,0},{3,1},{4,6},{5,7},{6,4},{7,5},{8,10},{9,11},{10,... | collective-permute-start | bytes 98312 | tf_op jit(solution)/shard_map/ppermute | solution.py:211
  38.5 2.1 %collective-permute-start.6 = (f32[8,2048]{1,0:T(8,128)S(1)}, f32[8,2048]{1,0:T(8,128)S(1)}, u32[]{:S(2)}, u32[]{:S(2)}) collective-permute-start(f32[8,2048]{1,0:T(8,128)S(1)} %shard_map.107), channel_id=1, source_target_pairs={{0,128},{1,129},{2,130},{3,131},{4,132},{5,133},{6,134},{7,135},{8... | collective-permute-start | bytes 196616 | tf_op jit(solution)/shard_map/ppermute | solution.py:249

commit v3 on v2

v3 whole, which is shorter than its diff:
```python
import jax
import jax.numpy as jnp
from jax import lax
from jax.experimental import pallas as pl
from jax.experimental.pallas import tpu as pltpu
from jax.sharding import PartitionSpec as P

step_weight = 0.25
axes = ("sec", "blk")
VMEM = pl.BlockSpec(memory_space=pltpu.VMEM)
SMEM = pl.BlockSpec(memory_space=pltpu.SMEM)
ANY = pl.BlockSpec(memory_space=pl.ANY)
HBM = pl.BlockSpec(memory_space=pltpu.HBM)


def partner(block, distance, phase, count):
    other = block + distance if (block // distance) % 2 == phase else block - distance
    return other if 0 <= other < count else block


def exchange_pairs(count, phase):
    first = [(b, partner(b, 2, phase, count)) for b in range(count)]
    second = [(count + b, count + partner(b, 1, phase, count)) for b in range(count)]
    return first + second


def swap_pairs(count):
    return [(b, count + b) for b in range(count)] + [(count + b, b) for b in range(count)]


def place():
    count = lax.axis_size("blk")
    core = lax.axis_index("sec")
    block = lax.axis_index("blk")
    reach = 2 - core
    shift = 1 - core
    place_in_pair = jnp.bitwise_and(lax.shift_right_logical(block, shift), 1)
    wide_step = jnp.where(place_in_pair == 1, reach, -reach)
    near_step = -wide_step
    found = []
    for step in (wide_step, near_step):
        other = block + step
        found.append(jnp.logical_and(other >= 0, other < count))
    return core, (wide_step + 2, near_step + 2), found


def level_kernel(columns, mixing, lagged, out, buffer, rows, late, semaphore, extra):
    fields = out.shape[0]
    small = [
        pltpu.make_async_copy(mixing.at[0, 0, 0:16], rows, extra.at[0]),
        pltpu.make_async_copy(lagged.at[0], late, extra.at[1]),
    ]
    copies = [
        pltpu.make_async_copy(columns.at[0, 0, f], buffer.at[f], semaphore.at[f])
        for f in range(fields)
    ]
    small[0].start()
    for copy in copies:
        copy.start()
    small[1].start()
    small[0].wait()
    for f in range(fields):
        if f % 4 == 0:
            for copy in copies[f : f + 4]:
                copy.wait()
        product = jnp.dot(rows[...], buffer[f], preferred_element_type=jnp.float32)
        level = product + buffer[f, 0:16, :].astype(jnp.float32)
        out[f : f + 1, :] = level[0:1, :]
    small[1].wait()

    @pl.when(lax.axis_index("sec") == 0)
    def _():
        surface = out[...] - step_weight * late[...].astype(jnp.float32)
        out[...] = surface.astype(jnp.bfloat16).astype(jnp.float32)


def pick_kernel(weights, after, picked, semaphore):
    del after
    core, distances, _ = place()
    slots = weights.shape[2]
    half = slots // 2
    copies = [
        pltpu.make_async_copy(
            weights.at[0, distances[g]], picked.at[pl.ds(g * slots, slots)], semaphore.at[g]
        )
        for g in (0, 1)
    ]
    copies.append(
        pltpu.make_async_copy(
            weights.at[0, 2, pl.ds(core * half, half)],
            picked.at[pl.ds(2 * slots, half)],
            semaphore.at[2],
        )
    )
    for copy in copies:
        copy.start()
    for copy in copies:
        copy.wait()


def slot_jobs(core, distances, slots):
    half = slots // 2
    jobs = [(g, distances[g], k, g * slots + k) for k in range(slots) for g in (0, 1)]
    return jobs + [(2, 2, k + core * half, 2 * slots + k) for k in range(half)]


def remap_kernel(codes, level, other, weights, first, second, own, ocean, tiles, sums):
    count, fields, width = tiles.shape
    core, distances, found = place()

    def spread(surface, below):
        for t in range(count):
            tiles[t] = surface[:, t * width : (t + 1) * width]
        ocean[...] = below[...]

    @pl.when(core == 0)
    def _():
        spread(level, other)

    @pl.when(core == 1)
    def _():
        spread(other, level)

    sums[...] = jnp.zeros_like(sums)
    for g, p, slot, at in slot_jobs(core, distances, codes.shape[2]):
        code = codes[0, p, slot]
        part = tiles[jnp.bitwise_and(code, 255)].astype(jnp.bfloat16)
        product = jnp.dot(part, weights[at], preferred_element_type=jnp.float32)
        product = product.astype(jnp.bfloat16).astype(jnp.float32)
        target = jnp.bitwise_and(lax.shift_right_logical(code, 8), 255)
        keep = lax.shift_right_logical(code, 16) == 1
        if g < 2:
            keep = jnp.logical_and(keep, found[g])
        sums[g, target] = sums[g, target] + jnp.where(keep, product, 0.0)
    for t in range(count):
        span = slice(t * width, (t + 1) * width)
        first[:, span] = sums[0, t].astype(jnp.bfloat16)
        second[:, span] = sums[1, t].astype(jnp.bfloat16)
        own[:, span] = sums[2, t]


def back_kernel(codes, second, first, own, weights, after, kept, sent, tiles, sums):
    del after
    _, count, fields, width = tiles.shape
    core, distances, found = place()
    for t in range(count):
        span = slice(t * width, (t + 1) * width)
        tiles[0, t] = first[:, span].astype(jnp.float32)
        tiles[1, t] = second[:, span].astype(jnp.float32)
        tiles[2, t] = own[:, span].astype(jnp.float32)
    sums[...] = jnp.zeros_like(sums)
    for i, (g, p, slot, at) in enumerate(slot_jobs(core, distances, codes.shape[2])):
        code = codes[0, p, slot]
        source = jnp.bitwise_and(lax.shift_right_logical(code, 8), 255)
        part = tiles[g, source].astype(jnp.bfloat16)
        product = lax.dot_general(
            part,
            weights[at],
            (((1,), (1,)), ((), ())),
            preferred_element_type=jnp.float32,
        )
        target = jnp.bitwise_and(code, 255)
        keep = lax.shift_right_logical(code, 16) == 1
        if g < 2:
            keep = jnp.logical_and(keep, found[g])
        sums[i % 2, target] = sums[i % 2, target] + jnp.where(keep, product, 0.0)

    @pl.when(core == 0)
    def _():
        for t in range(count):
            kept[:, t * width : (t + 1) * width] = sums[0, t] + sums[1, t]
        sent[...] = jnp.zeros_like(sent)

    @pl.when(core == 1)
    def _():
        for t in range(count):
            sent[:, t * width : (t + 1) * width] = sums[0, t] + sums[1, t]
        kept[...] = own[...].astype(jnp.float32)


def mix_kernel(held, mixing, level, flux, out, done, mixed, semaphore):
    share = jnp.where(lax.axis_index("sec") == 1, step_weight, 0.0)
    top = level[...] + share * flux[...].astype(jnp.float32)
    fields, levels, cells = held.shape
    row = lax.broadcasted_iota(jnp.int32, (16, cells), 0)
    copies = []
    for f in range(fields):
        total = held[f].astype(jnp.float32) + jnp.dot(
            mixing[0, 0], held[f], preferred_element_type=jnp.float32
        )
        mixed[f] = total.astype(jnp.bfloat16)
        above = jnp.broadcast_to(top[f : f + 1, :], (16, cells))
        mixed[f, 0:16, :] = jnp.where(row == 0, above, total[0:16, :]).astype(jnp.bfloat16)
        copies.append(pltpu.make_async_copy(mixed.at[f], out.at[0, 0, f], semaphore.at[f]))
        copies[f].start()
    done[...] = jnp.zeros_like(done)
    for copy in copies:
        copy.wait()


def local(
    columns, mixing, lagged_flux, coefficients, ocean_mask, atm_tile, ocean_tile, live, weights
):
    _, _, fields, levels, cells = columns.shape
    width = weights.shape[3]
    tiles = cells // width
    count = lax.axis_size("blk")
    codes = atm_tile + 256 * ocean_tile + 65536 * live
    swap = swap_pairs(count)
    wide = exchange_pairs(count, 1)
    near = exchange_pairs(count, 0)
    field_f32 = jax.ShapeDtypeStruct((fields, cells), jnp.float32)
    field_bf16 = jax.ShapeDtypeStruct((fields, cells), jnp.bfloat16)

    level, held = pl.pallas_call(
        level_kernel,
        out_shape=(field_f32, jax.ShapeDtypeStruct(columns.shape[2:], jnp.bfloat16)),
        in_specs=[HBM, HBM, HBM],
        out_specs=(VMEM, VMEM),
        scratch_shapes=[
            pltpu.VMEM((16, levels), jnp.bfloat16),
            pltpu.VMEM((fields, cells), jnp.bfloat16),
            pltpu.SemaphoreType.DMA((fields,)),
            pltpu.SemaphoreType.DMA((2,)),
        ],
        compiler_params=pltpu.CompilerParams(vmem_limit_bytes=8 << 20),
    )(*(pltpu.with_memory_space_constraint(x, pltpu.HBM) for x in (columns, mixing, lagged_flux)))
    slots = weights.shape[2]
    picked = pl.pallas_call(
        pick_kernel,
        out_shape=jax.ShapeDtypeStruct((5 * slots // 2, width, width), jnp.bfloat16),
        in_specs=[HBM, ANY],
        out_specs=VMEM,
        scratch_shapes=[pltpu.SemaphoreType.DMA((3,))],
        compiler_params=pltpu.CompilerParams(vmem_limit_bytes=8 << 20),
    )(pltpu.with_memory_space_constraint(weights, pltpu.HBM), level)
    other_level = lax.ppermute(level, axes, swap)
    first, second, own, ocean_level = pl.pallas_call(
        remap_kernel,
        out_shape=(field_bf16, field_bf16, field_f32, field_f32),
        in_specs=[SMEM, VMEM, VMEM, VMEM],
        out_specs=(VMEM, VMEM, VMEM, VMEM),
        scratch_shapes=[
            pltpu.VMEM((tiles, fields, width), jnp.float32),
            pltpu.VMEM((3, tiles, fields, width), jnp.float32),
        ],
        compiler_params=pltpu.CompilerParams(vmem_limit_bytes=8 << 20),
    )(codes, level, other_level, picked)
    got_first = lax.ppermute(first, axes, wide)
    got_second = lax.ppermute(second, axes, near)
    partial = own + got_first.astype(jnp.float32) + got_second.astype(jnp.float32)
    remapped = partial + lax.ppermute(partial, axes, swap)

    difference = remapped - ocean_level
    speed = jnp.sqrt(
        difference[0:1] * difference[0:1] + difference[1:2] * difference[1:2] + 1.0
    )
    ocean_flux = (
        coefficients[:, None] * speed * difference * ocean_mask.astype(jnp.float32)
    ).astype(jnp.bfloat16)
    flux_first = lax.ppermute(ocean_flux, axes, wide)
    flux_second = lax.ppermute(ocean_flux, axes, near)

    new_columns, done = pl.pallas_call(
        mix_kernel,
        out_shape=(
            jax.ShapeDtypeStruct(columns.shape, jnp.bfloat16),
            jax.ShapeDtypeStruct((8, 128), jnp.float32),
        ),
        in_specs=[VMEM, VMEM, VMEM, VMEM],
        out_specs=(ANY, VMEM),
        scratch_shapes=[
            pltpu.VMEM((fields, levels, cells), jnp.bfloat16),
            pltpu.SemaphoreType.DMA((fields,)),
        ],
        cost_estimate=pl.CostEstimate(
            flops=2 * fields * levels * levels * cells,
            transcendentals=0,
            bytes_accessed=4 * fields * levels * cells,
        ),
        compiler_params=pltpu.CompilerParams(vmem_limit_bytes=8 << 20),
    )(pltpu.with_memory_space_constraint(held, pltpu.VMEM), mixing, level, ocean_flux)

    kept, sent = pl.pallas_call(
        back_kernel,
        out_shape=(field_f32, field_f32),
        in_specs=[SMEM, VMEM, VMEM, VMEM, VMEM, ANY],
        out_specs=(VMEM, VMEM),
        scratch_shapes=[
            pltpu.VMEM((3, tiles, fields, width), jnp.float32),
            pltpu.VMEM((2, tiles, fields, width), jnp.float32),
        ],
        compiler_params=pltpu.CompilerParams(vmem_limit_bytes=8 << 20),
    )(codes, flux_second, flux_first, ocean_flux, picked, done)
    flux_here = (kept + lax.ppermute(sent, axes, swap)).astype(jnp.bfloat16)
    return (new_columns, flux_here[None, None])


def solution(mesh):
    in_specs = (
        P("sec", "blk", None, None, None),
        P("sec", "blk", None, None),
        P("blk", None, None),
        P(),
        P("blk", None),
        P("blk", None, None),
        P("blk", None, None),
        P("blk", None, None),
        P("blk", None, None, None, None),
    )
    out_specs = (P("sec", "blk", None, None, None), P("sec", "blk", None, None))
    return jax.shard_map(local, mesh=mesh, in_specs=in_specs, out_specs=out_specs, check_vma=False)
```

time: 41.4 us -> 38 us (0.918)
  Pallas kernels: 13.6 us -> 9.06 us
  starting transfers between devices: 20.5 us -> 21.5 us
    pallas_call x3 -> x4, Pallas kernels: 12.5 us -> 7.96 us  [the longest x1 2.88 us: local(): pl.pallas_call(level_kernel, out_shape=(field_f32, jax.ShapeDtypeStruct(c...]
    ppermute x1, starting transfers between devices: 1.16 us -> 2.49 us  [local(): flux_here = (kept + lax.ppermute(sent, axes, swap)).astype(jnp.bfloat16)]
    ppermute x1, waiting for transfers between devices: 0.88 us -> 0.01 us  [local(): other_level = lax.ppermute(level, axes, swap)]
    ppermute x1, waiting for transfers between devices: 0.01 us -> 0.85 us  [local(): flux_first = lax.ppermute(ocean_flux, axes, wide)]
    ppermute x1, starting transfers between devices: 3.22 us -> 2.66 us  [local(): remapped = partial + lax.ppermute(partial, axes, swap)]
  transfers between devices with their start and end apart: 7 -> 7, of which waited for: 5 -> 5; matrix products, arithmetic and copies ran while one was open for 0% -> 0% of each run, Pallas kernels for 18% -> 10%
where the time goes in v3:
time: 38 us; the launch traced here: 37.8 us
  starting transfers between devices  21.5 us (57%)
  Pallas kernels  9.06 us (24%)
  waiting for transfers between devices  5.64 us (15%)
  between operations  0.8 us (2%)
  other arithmetic  0.78 us (2%)
    ppermute x1, starting transfers between devices, local(): got_first = lax.ppermute(first, axes, wide)  9.86 us
    ppermute x1, starting transfers between devices, local(): flux_first = lax.ppermute(ocean_flux, axes, wide)  5.54 us
    pallas_call x1, Pallas kernels, local(): pl.pallas_call(level_kernel, out_shape=(field_f32, jax.ShapeDtypeStruct(c...  2.88 us
    ppermute x1, starting transfers between devices, local(): remapped = partial + lax.ppermute(partial, axes, swap)  2.66 us
    ppermute x1, starting transfers between devices, local(): flux_here = (kept + lax.ppermute(sent, axes, swap)).astype(jnp.bfloat16)  2.49 us
    pallas_call x1, Pallas kernels, local(): pl.pallas_call(mix_kernel, out_shape=(jax.ShapeDtypeStruct(columns.shape,...  2.36 us
    ppermute x1, waiting for transfers between devices, local(): got_second = lax.ppermute(second, axes, near)  1.68 us
    pallas_call x1, Pallas kernels, local(): pl.pallas_call(back_kernel, out_shape=(field_f32, field_f32), in_specs=[S...  1.41 us
  transfers between devices with their start and end apart: 7, of which 5 were waited for; matrix products, arithmetic and copies ran while one was open for 0% of the time, Pallas kernels for 10%

profile of v3, /device:TPU:25, one launch (start us, length us, event | category | flops | bytes accessed | tf_op | source)
XLA Modules:
  0.0 37.8 jit_solution(8494527153524396421)
XLA Ops:
  0.6 0.0 copy-start
  0.6 0.0 copy-start.2
  0.7 0.0 copy-start.4
  0.7 0.0 copy-start.3
  0.7 0.0 copy-start.1
  0.7 0.0 copy-start.5
  0.7 2.9 %shard_map.104 = (f32[8,2048]{1,0:T(8,128)S(1)}, bf16[8,128,2048]{2,1,0:T(8,128)(2,1)S(1)}) custom-call(bf16[1,1,8,128,2048]{4,3,2,1,0:T(8,128)(2,1)} %columns.1, bf16[1,1,128,128]{3,2,1,0:T(8,128)(2,1)} %mixing.3, bf16[1,8,2048]{2,1,0:T(8,128)(2,1)} %lagged.1), custom_call_target="tpu_custom_call" | custom-call | tf_op jit(solution)/shard_map/pallas_call | solution.py:215
  3.6 0.8 %collective-permute-start = (f32[8,2048]{1,0:T(8,128)S(1)}, f32[8,2048]{1,0:T(8,128)S(1)}, u32[]{:S(2)}, u32[]{:S(2)}) collective-permute-start(f32[8,2048]{1,0:T(8,128)S(1)} %get-tuple-element.13.after.level), channel_id=1, source_target_pairs={{0,128},{1,129},{2,130},{3,131},{4,132},{5,133},{6,134},{7,135},{8... | collective-permute-start | bytes 196616 | tf_op jit(solution)/shard_map/ppermute | solution.py:237
  4.4 0.0 copy-done.2
  4.4 0.0 copy-done.4
  4.4 0.0 copy-done.3
  4.4 1.3 %shard_map.105.weights = bf16[40,128,128]{2,1,0:T(8,128)(2,1)S(1)} custom-call(bf16[1,5,16,128,128]{4,3,2,1,0:T(8,128)(2,1)} %weights.1, f32[8,2048]{1,0:T(8,128)S(1)} %get-tuple-element.13.after.level), custom_call_target="tpu_custom_call" | custom-call | tf_op jit(solution)/shard_map/pallas_call | solution.py:229
  5.7 0.0 collective-permute-done.other
  5.7 1.1 %shard_map.106 = (bf16[8,2048]{1,0:T(8,128)(2,1)S(1)}, bf16[8,2048]{1,0:T(8,128)(2,1)S(1)}, f32[8,2048]{1,0:T(8,128)S(1)}, f32[8,2048]{1,0:T(8,128)S(1)}) custom-call(s32[1,5,16]{2,1,0:T(8,128)S(1)} %fusion.2.codes, f32[8,2048]{1,0:T(8,128)S(1)} %get-tuple-element.13.after.level, f32[8,2048]{1,0:T(8,128)S(1)} %collective-permute-done.other, ...), custom_call_target="tpu_custom_call" | custom-call | tf_op jit(solution)/shard_map/pallas_call | solution.py:238
  6.8 9.9 %collective-permute-start.1 = (bf16[8,2048]{1,0:T(8,128)(2,1)S(1)}, bf16[8,2048]{1,0:T(8,128)(2,1)S(1)}, u32[]{:S(2)}, u32[]{:S(2)}) collective-permute-start(bf16[8,2048]{1,0:T(8,128)(2,1)S(1)} %get-tuple-element.15), channel_id=1, source_target_pairs={{0,0},{1,1},{2,4},{3,5},{4,2},{5,3},{6,8},{7,9},{8,6},{9,7},{10,12... | collective-permute-start | bytes 98312 | tf_op jit(solution)/shard_map/ppermute | solution.py:249
  16.7 0.1 collective-permute-start.2
  16.8 1.3 %collective-permute-done.1 = bf16[8,2048]{1,0:T(8,128)(2,1)S(1)} collective-permute-done((bf16[8,2048]{1,0:T(8,128)(2,1)S(1)}, bf16[8,2048]{1,0:T(8,128)(2,1)S(1)}, u32[]{:S(2)}, u32[]{:S(2)}) %collective-permute-start.1) | collective-permute-done | bytes 32800 | tf_op jit(solution)/shard_map/ppermute | solution.py:249
  18.1 1.7 %collective-permute-done.2 = bf16[8,2048]{1,0:T(8,128)(2,1)S(1)} collective-permute-done((bf16[8,2048]{1,0:T(8,128)(2,1)S(1)}, bf16[8,2048]{1,0:T(8,128)(2,1)S(1)}, u32[]{:S(2)}, u32[]{:S(2)}) %collective-permute-start.2) | collective-permute-done | bytes 32800 | tf_op jit(solution)/shard_map/ppermute | solution.py:250
  19.8 2.7 %collective-permute-start.3 = (f32[8,2048]{1,0:T(8,128)S(1)}, f32[8,2048]{1,0:T(8,128)S(1)}, u32[]{:S(2)}, u32[]{:S(2)}) collective-permute-start(f32[8,2048]{1,0:T(8,128)S(1)} %convert_add_fusion), channel_id=1, source_target_pairs={{0,128},{1,129},{2,130},{3,131},{4,132},{5,133},{6,134},{7,135},{8... | collective-permute-start | bytes 196616 | tf_op jit(solution)/shard_map/ppermute | solution.py:252
  22.4 0.0 copy-done.1
  22.5 0.9 %collective-permute-done.3 = f32[8,2048]{1,0:T(8,128)S(1)} collective-permute-done((f32[8,2048]{1,0:T(8,128)S(1)}, f32[8,2048]{1,0:T(8,128)S(1)}, u32[]{:S(2)}, u32[]{:S(2)}) %collective-permute-start.3) | collective-permute-done | bytes 65568 | tf_op jit(solution)/shard_map/ppermute | solution.py:252
  23.4 0.0 copy-done.5
  23.4 0.1 multiply_convert_fusion.flux.own
  23.5 5.5 %collective-permute-start.5 = (bf16[8,2048]{1,0:T(8,128)(2,1)S(1)}, bf16[8,2048]{1,0:T(8,128)(2,1)S(1)}, u32[]{:S(2)}, u32[]{:S(2)}) collective-permute-start(bf16[8,2048]{1,0:T(8,128)(2,1)S(1)} %multiply_convert_fusion.flux.own), channel_id=1, source_target_pairs={{0,0},{1,1},{2,4},{3,5},{4,2},{5,3},{6,8},{7,9},{8,6},{9,7},{10,12... | collective-permute-start | bytes 98312 | tf_op jit(solution)/shard_map/ppermute | solution.py:261
  29.1 0.1 collective-permute-start.4
  29.2 0.0 copy-done
  29.2 2.4 %shard_map.107 = (bf16[1,1,8,128,2048]{4,3,2,1,0:T(8,128)(2,1)}, f32[8,128]{1,0:T(8,128)S(1)}) custom-call(bf16[8,128,2048]{2,1,0:T(8,128)(2,1)S(1)} %get-tuple-element.12.held, bf16[1,1,128,128]{3,2,1,0:T(8,128)(2,1)S(1)} %copy-done, f32[8,2048]{1,0:T(8,128)S(1)} %get-tuple-element.13.after.level, bf16[8,2048]{1,0:T(8,128)(2,1)S(1)} %multiply_convert_fusion.flux.own), custom_call_target="tpu_custom_call" | custom-call | flops 536870912 | bytes 8388608 | tf_op jit(solution)/shard_map/pallas_call | solution.py:264
  31.5 0.8 %collective-permute-done.5.first = bf16[8,2048]{1,0:T(8,128)(2,1)S(1)} collective-permute-done((bf16[8,2048]{1,0:T(8,128)(2,1)S(1)}, bf16[8,2048]{1,0:T(8,128)(2,1)S(1)}, u32[]{:S(2)}, u32[]{:S(2)}) %collective-permute-start.5) | collective-permute-done | bytes 32800 | tf_op jit(solution)/shard_map/ppermute | solution.py:261
  32.4 0.0 collective-permute-done.4.second
  32.4 1.4 %shard_map.108 = (f32[8,2048]{1,0:T(8,128)S(1)}, f32[8,2048]{1,0:T(8,128)S(1)}) custom-call(s32[1,5,16]{2,1,0:T(8,128)S(1)} %fusion.2.codes, bf16[8,2048]{1,0:T(8,128)(2,1)S(1)} %collective-permute-done.4.second, bf16[8,2048]{1,0:T(8,128)(2,1)S(1)} %collective-permute-done.5.first, bf16[8,2048]{1,0:T(8,128)(2,1)S(1)} %multiply_convert_fusion.flux.own, ...), custom_call_target="tpu_custom_call" | custom-call | tf_op jit(solution)/shard_map/pallas_call | solution.py:284
  33.8 2.5 %collective-permute-start.6 = (f32[8,2048]{1,0:T(8,128)S(1)}, f32[8,2048]{1,0:T(8,128)S(1)}, u32[]{:S(2)}, u32[]{:S(2)}) collective-permute-start(f32[8,2048]{1,0:T(8,128)S(1)} %get-tuple-element.21), channel_id=1, source_target_pairs={{0,128},{1,129},{2,130},{3,131},{4,132},{5,133},{6,134},{7,135},{8... | collective-permute-start | bytes 196616 | tf_op jit(solution)/shard_map/ppermute | solution.py:295
  36.3 0.9 %collective-permute-done.6 = f32[8,2048]{1,0:T(8,128)S(1)} collective-permute-done((f32[8,2048]{1,0:T(8,128)S(1)}, f32[8,2048]{1,0:T(8,128)S(1)}, u32[]{:S(2)}, u32[]{:S(2)}) %collective-permute-start.6) | collective-permute-done | bytes 65568 | tf_op jit(solution)/shard_map/ppermute | solution.py:295
  37.2 0.6 %fusion = bf16[1,1,8,2048]{3,2,1,0:T(8,128)(2,1)} fusion(f32[8,2048]{1,0:T(8,128)S(1)} %get-tuple-element.20, f32[8,2048]{1,0:T(8,128)S(1)} %collective-permute-done.6), kind=kLoop, calls=%fused_computation.4 | loop fusion | flops 32768 | bytes 163840 | tf_op jit(solution)/shard_map/broadcast_in_dim | solution.py:296
  (5 shorter events, 0.1 us)
Async XLA Ops:
  0.6 28.5 %copy-start = (bf16[1,1,128,128]{3,2,1,0:T(8,128)(2,1)S(1)}, bf16[1,1,128,128]{3,2,1,0:T(8,128)(2,1)}, u32[]{:S(2)}) copy-start(bf16[1,1,128,128]{3,2,1,0:T(8,128)(2,1)} %mixing.3) | copy-start | bytes 98308
  0.6 3.7 %copy-start.2 = (s32[1,5,16]{2,0,1:T(1,128)S(1)}, s32[1,5,16]{2,0,1:T(1,128)}, u32[]{:S(2)}) copy-start(s32[1,5,16]{2,0,1:T(1,128)} %param.16) | copy-start | bytes 964
  0.7 3.7 %copy-start.4 = (s32[1,5,16]{2,0,1:T(1,128)S(1)}, s32[1,5,16]{2,0,1:T(1,128)}, u32[]{:S(2)}) copy-start(s32[1,5,16]{2,0,1:T(1,128)} %param.15) | copy-start | bytes 964
  0.7 3.7 %copy-start.3 = (s32[1,5,16]{2,0,1:T(1,128)S(1)}, s32[1,5,16]{2,0,1:T(1,128)}, u32[]{:S(2)}) copy-start(s32[1,5,16]{2,0,1:T(1,128)} %param.14) | copy-start | bytes 964
  0.7 21.8 %copy-start.1 = (s32[1,2048]{1,0:T(1,128)S(1)}, s32[1,2048]{1,0:T(1,128)}, u32[]{:S(2)}) copy-start(s32[1,2048]{1,0:T(1,128)} %param.13) | copy-start | bytes 24580
  0.7 22.7 %copy-start.5 = (f32[8]{0:T(128)S(1)}, f32[8]{0:T(128)}, u32[]{:S(2)}) copy-start(f32[8]{0:T(128)} %param.12) | copy-start | bytes 100
  3.6 2.1 %collective-permute-start = (f32[8,2048]{1,0:T(8,128)S(1)}, f32[8,2048]{1,0:T(8,128)S(1)}, u32[]{:S(2)}, u32[]{:S(2)}) collective-permute-start(f32[8,2048]{1,0:T(8,128)S(1)} %get-tuple-element.13.after.level), channel_id=1, source_target_pairs={{0,128},{1,129},{2,130},{3,131},{4,132},{5,133},{6,134},{7,135},{8... | collective-permute-start | bytes 196616 | tf_op jit(solution)/shard_map/ppermute | solution.py:237
  6.8 11.3 %collective-permute-start.1 = (bf16[8,2048]{1,0:T(8,128)(2,1)S(1)}, bf16[8,2048]{1,0:T(8,128)(2,1)S(1)}, u32[]{:S(2)}, u32[]{:S(2)}) collective-permute-start(bf16[8,2048]{1,0:T(8,128)(2,1)S(1)} %get-tuple-element.15), channel_id=1, source_target_pairs={{0,0},{1,1},{2,4},{3,5},{4,2},{5,3},{6,8},{7,9},{8,6},{9,7},{10,12... | collective-permute-start | bytes 98312 | tf_op jit(solution)/shard_map/ppermute | solution.py:249
  16.7 3.1 %collective-permute-start.2 = (bf16[8,2048]{1,0:T(8,128)(2,1)S(1)}, bf16[8,2048]{1,0:T(8,128)(2,1)S(1)}, u32[]{:S(2)}, u32[]{:S(2)}) collective-permute-start(bf16[8,2048]{1,0:T(8,128)(2,1)S(1)} %get-tuple-element.16), channel_id=1, source_target_pairs={{0,2},{1,3},{2,0},{3,1},{4,6},{5,7},{6,4},{7,5},{8,10},{9,11},{10,... | collective-permute-start | bytes 98312 | tf_op jit(solution)/shard_map/ppermute | solution.py:250
  19.8 3.6 %collective-permute-start.3 = (f32[8,2048]{1,0:T(8,128)S(1)}, f32[8,2048]{1,0:T(8,128)S(1)}, u32[]{:S(2)}, u32[]{:S(2)}) collective-permute-start(f32[8,2048]{1,0:T(8,128)S(1)} %convert_add_fusion), channel_id=1, source_target_pairs={{0,128},{1,129},{2,130},{3,131},{4,132},{5,133},{6,134},{7,135},{8... | collective-permute-start | bytes 196616 | tf_op jit(solution)/shard_map/ppermute | solution.py:252
  23.5 8.9 %collective-permute-start.5 = (bf16[8,2048]{1,0:T(8,128)(2,1)S(1)}, bf16[8,2048]{1,0:T(8,128)(2,1)S(1)}, u32[]{:S(2)}, u32[]{:S(2)}) collective-permute-start(bf16[8,2048]{1,0:T(8,128)(2,1)S(1)} %multiply_convert_fusion.flux.own), channel_id=1, source_target_pairs={{0,0},{1,1},{2,4},{3,5},{4,2},{5,3},{6,8},{7,9},{8,6},{9,7},{10,12... | collective-permute-start | bytes 98312 | tf_op jit(solution)/shard_map/ppermute | solution.py:261
  29.1 3.3 %collective-permute-start.4 = (bf16[8,2048]{1,0:T(8,128)(2,1)S(1)}, bf16[8,2048]{1,0:T(8,128)(2,1)S(1)}, u32[]{:S(2)}, u32[]{:S(2)}) collective-permute-start(bf16[8,2048]{1,0:T(8,128)(2,1)S(1)} %multiply_convert_fusion.flux.own), channel_id=1, source_target_pairs={{0,2},{1,3},{2,0},{3,1},{4,6},{5,7},{6,4},{7,5},{8,10},{9,11},{10,... | collective-permute-start | bytes 98312 | tf_op jit(solution)/shard_map/ppermute | solution.py:262
  33.8 3.4 %collective-permute-start.6 = (f32[8,2048]{1,0:T(8,128)S(1)}, f32[8,2048]{1,0:T(8,128)S(1)}, u32[]{:S(2)}, u32[]{:S(2)}) collective-permute-start(f32[8,2048]{1,0:T(8,128)S(1)} %get-tuple-element.21), channel_id=1, source_target_pairs={{0,128},{1,129},{2,130},{3,131},{4,132},{5,133},{6,134},{7,135},{8... | collective-permute-start | bytes 196616 | tf_op jit(solution)/shard_map/ppermute | solution.py:295

commit v4 on v3

--- a/solution.py
+++ b/solution.py
@@ -18,10 +18,25 @@
     return other if 0 <= other < count else block
 
 
-def exchange_pairs(count, phase):
-    first = [(b, partner(b, 2, phase, count)) for b in range(count)]
-    second = [(count + b, count + partner(b, 1, phase, count)) for b in range(count)]
-    return first + second
+def exchange_pairs(count):
+    lower, across, upper, alone = [], [], [], []
+    for b in range(count):
+        for core in (0, 1):
+            me = core * count + b
+            inside = (me, core * count + partner(b, 1 + core, 0, count))
+            idle = (me, (1 - core) * count + b)
+            lower.append(inside if b % 8 < 4 else idle)
+            upper.append(idle if b % 8 < 4 else inside)
+            other = partner(b, 2 - core, 1, count)
+            if other == b:
+                alone.append(me)
+            else:
+                across.append((me, core * count + other))
+    low = [d for d in alone if d % count < count // 2]
+    high = [d for d in alone if d % count >= count // 2]
+    for ring in (low, high):
+        across += [(d, ring[(i + 1) % len(ring)]) for i, d in enumerate(ring)]
+    return lower, across, upper
 
 
 def swap_pairs(count):
@@ -32,16 +47,19 @@
     count = lax.axis_size("blk")
     core = lax.axis_index("sec")
     block = lax.axis_index("blk")
-    reach = 2 - core
-    shift = 1 - core
-    place_in_pair = jnp.bitwise_and(lax.shift_right_logical(block, shift), 1)
-    wide_step = jnp.where(place_in_pair == 1, reach, -reach)
-    near_step = -wide_step
+    steps = []
+    for distance, phase in ((2 - core, 1), (1 + core, 0)):
+        position = jnp.bitwise_and(lax.shift_right_logical(block, distance - 1), 1)
+        steps.append(jnp.where(position == phase, distance, -distance))
     found = []
-    for step in (wide_step, near_step):
+    for step in steps:
         other = block + step
         found.append(jnp.logical_and(other >= 0, other < count))
-    return core, (wide_step + 2, near_step + 2), found
+    return core, (steps[0] + 2, steps[1] + 2), found
+
+
+def in_lower_half():
+    return jnp.bitwise_and(lax.axis_index("blk"), 7) < 4
 
 
 def level_kernel(columns, mixing, lagged, out, buffer, rows, late, semaphore, extra):
@@ -104,7 +122,7 @@
     return jobs + [(2, 2, k + core * half, 2 * slots + k) for k in range(half)]
 
 
-def remap_kernel(codes, level, other, weights, first, second, own, ocean, tiles, sums):
+def remap_kernel(codes, level, other, weights, across, inside, own, ocean, tiles, sums):
     count, fields, width = tiles.shape
     core, distances, found = place()
 
@@ -134,19 +152,19 @@
         sums[g, target] = sums[g, target] + jnp.where(keep, product, 0.0)
     for t in range(count):
         span = slice(t * width, (t + 1) * width)
-        first[:, span] = sums[0, t].astype(jnp.bfloat16)
-        second[:, span] = sums[1, t].astype(jnp.bfloat16)
+        across[:, span] = sums[0, t].astype(jnp.bfloat16)
+        inside[:, span] = sums[1, t].astype(jnp.bfloat16)
         own[:, span] = sums[2, t]
 
 
-def back_kernel(codes, second, first, own, weights, after, kept, sent, tiles, sums):
+def back_kernel(codes, across, inside, own, weights, after, kept, sent, tiles, sums):
     del after
     _, count, fields, width = tiles.shape
     core, distances, found = place()
     for t in range(count):
         span = slice(t * width, (t + 1) * width)
-        tiles[0, t] = first[:, span].astype(jnp.float32)
-        tiles[1, t] = second[:, span].astype(jnp.float32)
+        tiles[0, t] = across[:, span].astype(jnp.float32)
+        tiles[1, t] = inside[:, span].astype(jnp.float32)
         tiles[2, t] = own[:, span].astype(jnp.float32)
     sums[...] = jnp.zeros_like(sums)
     for i, (g, p, slot, at) in enumerate(slot_jobs(core, distances, codes.shape[2])):
@@ -178,20 +196,40 @@
         kept[...] = own[...].astype(jnp.float32)
 
 
-def mix_kernel(held, mixing, level, flux, out, done, mixed, semaphore):
-    share = jnp.where(lax.axis_index("sec") == 1, step_weight, 0.0)
-    top = level[...] + share * flux[...].astype(jnp.float32)
-    fields, levels, cells = held.shape
-    row = lax.broadcasted_iota(jnp.int32, (16, cells), 0)
+def mix_kernel(held, mixing, own, out, head, passed, mixed, semaphore):
+    fields, levels, _ = held.shape
+    rows = head.shape[1]
     copies = []
     for f in range(fields):
         total = held[f].astype(jnp.float32) + jnp.dot(
             mixing[0, 0], held[f], preferred_element_type=jnp.float32
         )
-        mixed[f] = total.astype(jnp.bfloat16)
-        above = jnp.broadcast_to(top[f : f + 1, :], (16, cells))
-        mixed[f, 0:16, :] = jnp.where(row == 0, above, total[0:16, :]).astype(jnp.bfloat16)
-        copies.append(pltpu.make_async_copy(mixed.at[f], out.at[0, 0, f], semaphore.at[f]))
+        head[f] = total[0:rows].astype(jnp.bfloat16)
+        mixed[f] = total[rows:].astype(jnp.bfloat16)
+        copies.append(
+            pltpu.make_async_copy(
+                mixed.at[f], out.at[0, 0, f, pl.ds(rows, levels - rows)], semaphore.at[f]
+            )
+        )
+        copies[f].start()
+    passed[...] = own[...]
+    for copy in copies:
+        copy.wait()
+
+
+def top_kernel(head, level, flux, columns, out, done, tops, semaphore):
+    del columns
+    fields, rows, cells = head.shape
+    share = jnp.where(lax.axis_index("sec") == 1, step_weight, 0.0)
+    top = level[...] + share * flux[...].astype(jnp.float32)
+    row = lax.broadcasted_iota(jnp.int32, (rows, cells), 0)
+    copies = []
+    for f in range(fields):
+        above = jnp.broadcast_to(top[f : f + 1, :], (rows, cells))
+        tops[f] = jnp.where(row == 0, above, head[f].astype(jnp.float32)).astype(jnp.bfloat16)
+        copies.append(
+            pltpu.make_async_copy(tops.at[f], out.at[0, 0, f, pl.ds(0, rows)], semaphore.at[f])
+        )
         copies[f].start()
     done[...] = jnp.zeros_like(done)
     for copy in copies:
@@ -207,8 +245,8 @@
     count = lax.axis_size("blk")
     codes = atm_tile + 256 * ocean_tile + 65536 * live
     swap = swap_pairs(count)
-    wide = exchange_pairs(count, 1)
-    near = exchange_pairs(count, 0)
+    lower, across, upper = exchange_pairs(count)
+    inside = [a if a[0] % count % 8 < 4 else b for a, b in zip(lower, upper)]
     field_f32 = jax.ShapeDtypeStruct((fields, cells), jnp.float32)
     field_bf16 = jax.ShapeDtypeStruct((fields, cells), jnp.bfloat16)
 
@@ -235,20 +273,40 @@
         compiler_params=pltpu.CompilerParams(vmem_limit_bytes=8 << 20),
     )(pltpu.with_memory_space_constraint(weights, pltpu.HBM), level)
     other_level = lax.ppermute(level, axes, swap)
-    first, second, own, ocean_level = pl.pallas_call(
+    to_across, to_inside, own, ocean_level = pl.pallas_call(
         remap_kernel,
         out_shape=(field_bf16, field_bf16, field_f32, field_f32),
         in_specs=[SMEM, VMEM, VMEM, VMEM],
-        out_specs=(VMEM, VMEM, VMEM, VMEM),
+        out_specs=(VMEM,) * 4,
         scratch_shapes=[
             pltpu.VMEM((tiles, fields, width), jnp.float32),
             pltpu.VMEM((3, tiles, fields, width), jnp.float32),
         ],
         compiler_params=pltpu.CompilerParams(vmem_limit_bytes=8 << 20),
     )(codes, level, other_level, picked)
-    got_first = lax.ppermute(first, axes, wide)
-    got_second = lax.ppermute(second, axes, near)
-    partial = own + got_first.astype(jnp.float32) + got_second.astype(jnp.float32)
+    most_columns, head, own = pl.pallas_call(
+        mix_kernel,
+        out_shape=(
+            jax.ShapeDtypeStruct(columns.shape, jnp.bfloat16),
+            jax.ShapeDtypeStruct((fields, 16, cells), jnp.bfloat16),
+            field_f32,
+        ),
+        in_specs=[VMEM, VMEM, VMEM],
+        out_specs=(HBM, VMEM, VMEM),
+        scratch_shapes=[
+            pltpu.VMEM((fields, levels - 16, cells), jnp.bfloat16),
+            pltpu.SemaphoreType.DMA((fields,)),
+        ],
+        cost_estimate=pl.CostEstimate(
+            flops=2 * fields * levels * levels * cells,
+            transcendentals=0,
+            bytes_accessed=4 * fields * levels * cells,
+        ),
+        compiler_params=pltpu.CompilerParams(vmem_limit_bytes=16 << 20),
+    )(pltpu.with_memory_space_constraint(held, pltpu.VMEM), mixing, own)
+    partial = own
+    for part, pairs in ((to_across, across), (to_inside, inside)):
+        partial = partial + lax.ppermute(part, axes, pairs).astype(jnp.float32)
     remapped = partial + lax.ppermute(partial, axes, swap)
 
     difference = remapped - ocean_level
@@ -258,28 +316,24 @@
     ocean_flux = (
         coefficients[:, None] * speed * difference * ocean_mask.astype(jnp.float32)
     ).astype(jnp.bfloat16)
-    flux_first = lax.ppermute(ocean_flux, axes, wide)
-    flux_second = lax.ppermute(ocean_flux, axes, near)
+    flux_across = lax.ppermute(ocean_flux, axes, across)
+    flux_inside = lax.ppermute(ocean_flux, axes, inside)
 
     new_columns, done = pl.pallas_call(
-        mix_kernel,
+        top_kernel,
         out_shape=(
             jax.ShapeDtypeStruct(columns.shape, jnp.bfloat16),
             jax.ShapeDtypeStruct((8, 128), jnp.float32),
         ),
-        in_specs=[VMEM, VMEM, VMEM, VMEM],
-        out_specs=(ANY, VMEM),
-        scratch_shapes=[
-            pltpu.VMEM((fields, levels, cells), jnp.bfloat16),
+        in_specs=[VMEM, VMEM, VMEM, HBM],
+        out_specs=(HBM, VMEM),
+        input_output_aliases={3: 0},
+        scratch_shapes=[
+            pltpu.VMEM((fields, 16, cells), jnp.bfloat16),
             pltpu.SemaphoreType.DMA((fields,)),
         ],
-        cost_estimate=pl.CostEstimate(
-            flops=2 * fields * levels * levels * cells,
-            transcendentals=0,
-            bytes_accessed=4 * fields * levels * cells,
-        ),
-        compiler_params=pltpu.CompilerParams(vmem_limit_bytes=8 << 20),
-    )(pltpu.with_memory_space_constraint(held, pltpu.VMEM), mixing, level, ocean_flux)
+        compiler_params=pltpu.CompilerParams(vmem_limit_bytes=8 << 20),
+    )(head, level, ocean_flux, most_columns)
 
     kept, sent = pl.pallas_call(
         back_kernel,
@@ -291,7 +345,7 @@
             pltpu.VMEM((2, tiles, fields, width), jnp.float32),
         ],
         compiler_params=pltpu.CompilerParams(vmem_limit_bytes=8 << 20),
-    )(codes, flux_second, flux_first, ocean_flux, picked, done)
+    )(codes, flux_across, flux_inside, ocean_flux, picked, done)
     flux_here = (kept + lax.ppermute(sent, axes, swap)).astype(jnp.bfloat16)
     return (new_columns, flux_here[None, None])
 

time: 38 us -> 33.3 us (0.88)
  starting transfers between devices: 21.5 us -> 15.5 us
  waiting for transfers between devices: 5.64 us -> 6.33 us
  Pallas kernels: 9.06 us -> 9.75 us
    ppermute x4, starting transfers between devices: 15.6 us -> 12.5 us  [the longest x2 8.05 us: local(): partial = partial + lax.ppermute(part, axes, pairs).astype(jnp.float32)]
    ppermute x1, starting transfers between devices: 2.66 us -> 1.13 us  [local(): remapped = partial + lax.ppermute(partial, axes, swap)]
    ppermute x1, starting transfers between devices: 2.49 us -> 1.12 us  [local(): flux_here = (kept + lax.ppermute(sent, axes, swap)).astype(jnp.bfloat16)]
    pallas_call x0 -> x1, Pallas kernels: none -> 0.87 us  [local(): pl.pallas_call(top_kernel, out_shape=(jax.ShapeDtypeStruct(columns.shape,...]
    ppermute x4, waiting for transfers between devices: 3.84 us -> 4.54 us  [the longest x1 1.71 us: local(): flux_across = lax.ppermute(ocean_flux, axes, across)]
  transfers between devices with their start and end apart: 7 -> 7, of which waited for: 5 -> 5; matrix products, arithmetic and copies ran while one was open for 0% -> 0% of each run, Pallas kernels for 10% -> 13%
where the time goes in v4:
time: 33.3 us; the launch traced here: 33.2 us
  starting transfers between devices  15.5 us (47%)
  Pallas kernels  9.75 us (29%)
  waiting for transfers between devices  6.33 us (19%)
  other arithmetic  0.78 us (2%)
  between operations  0.78 us (2%)
    ppermute x2, starting transfers between devices, local(): partial = partial + lax.ppermute(part, axes, pairs).astype(jnp.float32)  8.05 us
    ppermute x1, starting transfers between devices, local(): flux_across = lax.ppermute(ocean_flux, axes, across)  4.46 us
    pallas_call x1, Pallas kernels, local(): pl.pallas_call(level_kernel, out_shape=(field_f32, jax.ShapeDtypeStruct(c...  2.88 us
    pallas_call x1, Pallas kernels, local(): pl.pallas_call(mix_kernel, out_shape=(jax.ShapeDtypeStruct(columns.shape,...  2.18 us
    ppermute x1, waiting for transfers between devices, local(): flux_across = lax.ppermute(ocean_flux, axes, across)  1.71 us
    ppermute x2, waiting for transfers between devices, local(): partial = partial + lax.ppermute(part, axes, pairs).astype(jnp.float32)  1.46 us
    pallas_call x1, Pallas kernels, local(): pl.pallas_call(back_kernel, out_shape=(field_f32, field_f32), in_specs=[S...  1.4 us
    ppermute x1, waiting for transfers between devices, local(): flux_inside = lax.ppermute(ocean_flux, axes, inside)  1.37 us
  transfers between devices with their start and end apart: 7, of which 5 were waited for; matrix products, arithmetic and copies ran while one was open for 0% of the time, Pallas kernels for 13%

profile of v4, /device:TPU:25, one launch (start us, length us, event | category | flops | bytes accessed | tf_op | source)
XLA Modules:
  0.0 33.2 jit_solution(13698635208163359774)
XLA Ops:
  0.6 0.0 copy-start
  0.6 0.0 copy-start.3
  0.7 0.0 copy-start.4
  0.7 0.0 copy-start.2
  0.7 2.9 %shard_map.104 = (f32[8,2048]{1,0:T(8,128)S(1)}, bf16[8,128,2048]{2,1,0:T(8,128)(2,1)S(1)}) custom-call(bf16[1,1,8,128,2048]{4,3,2,1,0:T(8,128)(2,1)} %columns.1, bf16[1,1,128,128]{3,2,1,0:T(8,128)(2,1)} %mixing.3, bf16[1,8,2048]{2,1,0:T(8,128)(2,1)} %lagged.1), custom_call_target="tpu_custom_call" | custom-call | tf_op jit(solution)/shard_map/pallas_call | solution.py:253
  3.6 0.8 %collective-permute-start = (f32[8,2048]{1,0:T(8,128)S(1)}, f32[8,2048]{1,0:T(8,128)S(1)}, u32[]{:S(2)}, u32[]{:S(2)}) collective-permute-start(f32[8,2048]{1,0:T(8,128)S(1)} %get-tuple-element.16.after.level), channel_id=1, source_target_pairs={{0,128},{1,129},{2,130},{3,131},{4,132},{5,133},{6,134},{7,135},{8... | collective-permute-start | bytes 196616 | tf_op jit(solution)/shard_map/ppermute | solution.py:275
  4.3 0.0 copy-done.3
  4.3 0.0 copy-done.4
  4.3 0.0 copy-done.2
  4.4 0.0 copy-start.1
  4.4 0.0 copy-start.5
  4.4 1.3 %shard_map.105.weights = bf16[40,128,128]{2,1,0:T(8,128)(2,1)S(1)} custom-call(bf16[1,5,16,128,128]{4,3,2,1,0:T(8,128)(2,1)} %weights.1, f32[8,2048]{1,0:T(8,128)S(1)} %get-tuple-element.16.after.level), custom_call_target="tpu_custom_call" | custom-call | tf_op jit(solution)/shard_map/pallas_call | solution.py:267
  5.7 0.0 collective-permute-done.other
  5.7 1.1 %shard_map.106 = (bf16[8,2048]{1,0:T(8,128)(2,1)S(1)}, bf16[8,2048]{1,0:T(8,128)(2,1)S(1)}, f32[8,2048]{1,0:T(8,128)S(1)}, f32[8,2048]{1,0:T(8,128)S(1)}) custom-call(s32[1,5,16]{2,1,0:T(8,128)S(1)} %fusion.2.codes, f32[8,2048]{1,0:T(8,128)S(1)} %get-tuple-element.16.after.level, f32[8,2048]{1,0:T(8,128)S(1)} %collective-permute-done.other, ...), custom_call_target="tpu_custom_call" | custom-call | tf_op jit(solution)/shard_map/pallas_call | solution.py:276
  6.8 8.0 %collective-permute-start.1 = (bf16[8,2048]{1,0:T(8,128)(2,1)S(1)}, bf16[8,2048]{1,0:T(8,128)(2,1)S(1)}, u32[]{:S(2)}, u32[]{:S(2)}) collective-permute-start(bf16[8,2048]{1,0:T(8,128)(2,1)S(1)} %get-tuple-element.20), channel_id=1, source_target_pairs={{129,130},{2,4},{130,129},{3,5},{131,132},{4,2},{132,131},{5,3},{1... | collective-permute-start | bytes 98312 | tf_op jit(solution)/shard_map/ppermute | solution.py:309
  14.9 0.0 collective-permute-start.2
  14.9 0.0 copy-done
  14.9 2.2 %shard_map.107 = (bf16[1,1,8,128,2048]{4,3,2,1,0:T(8,128)(2,1)}, bf16[8,16,2048]{2,1,0:T(8,128)(2,1)S(1)}, f32[8,2048]{1,0:T(8,128)S(1)}) custom-call(bf16[8,128,2048]{2,1,0:T(8,128)(2,1)S(1)} %get-tuple-element.15.held, bf16[1,1,128,128]{3,2,1,0:T(8,128)(2,1)S(1)} %copy-done, f32[8,2048]{1,0:T(8,128)S(1)} %get-tuple-element.17.own), custom_call_target="tpu_custom_call" | custom-call | flops 536870912 | bytes 8388608 | tf_op jit(solution)/shard_map/pallas_call | solution.py:287
  17.1 0.0 collective-permute-done.1
  17.1 1.5 %collective-permute-done.2 = bf16[8,2048]{1,0:T(8,128)(2,1)S(1)} collective-permute-done((bf16[8,2048]{1,0:T(8,128)(2,1)S(1)}, bf16[8,2048]{1,0:T(8,128)(2,1)S(1)}, u32[]{:S(2)}, u32[]{:S(2)}) %collective-permute-start.2) | collective-permute-done | bytes 32800 | tf_op jit(solution)/shard_map/ppermute | solution.py:309
  18.5 1.1 %collective-permute-start.3 = (f32[8,2048]{1,0:T(8,128)S(1)}, f32[8,2048]{1,0:T(8,128)S(1)}, u32[]{:S(2)}, u32[]{:S(2)}) collective-permute-start(f32[8,2048]{1,0:T(8,128)S(1)} %convert_add_fusion), channel_id=1, source_target_pairs={{0,128},{1,129},{2,130},{3,131},{4,132},{5,133},{6,134},{7,135},{8... | collective-permute-start | bytes 196616 | tf_op jit(solution)/shard_map/ppermute | solution.py:310
  19.7 0.0 copy-done.1
  19.7 0.9 %collective-permute-done.3 = f32[8,2048]{1,0:T(8,128)S(1)} collective-permute-done((f32[8,2048]{1,0:T(8,128)S(1)}, f32[8,2048]{1,0:T(8,128)S(1)}, u32[]{:S(2)}, u32[]{:S(2)}) %collective-permute-start.3) | collective-permute-done | bytes 65568 | tf_op jit(solution)/shard_map/ppermute | solution.py:310
  20.6 0.0 copy-done.5
  20.6 0.1 multiply_convert_fusion.flux.own
  20.7 4.5 %collective-permute-start.4 = (bf16[8,2048]{1,0:T(8,128)(2,1)S(1)}, bf16[8,2048]{1,0:T(8,128)(2,1)S(1)}, u32[]{:S(2)}, u32[]{:S(2)}) collective-permute-start(bf16[8,2048]{1,0:T(8,128)(2,1)S(1)} %multiply_convert_fusion.flux.own), channel_id=1, source_target_pairs={{129,130},{2,4},{130,129},{3,5},{131,132},{4,2},{132,131},{5,3},{1... | collective-permute-start | bytes 98312 | tf_op jit(solution)/shard_map/ppermute | solution.py:319
  25.2 0.0 collective-permute-start.5
  25.2 0.9 %shard_map.108 = (bf16[1,1,8,128,2048]{4,3,2,1,0:T(8,128)(2,1)}, f32[8,128]{1,0:T(8,128)S(1)}) custom-call(bf16[8,16,2048]{2,1,0:T(8,128)(2,1)S(1)} %get-tuple-element.18.head, f32[8,2048]{1,0:T(8,128)S(1)} %get-tuple-element.16.after.level, bf16[8,2048]{1,0:T(8,128)(2,1)S(1)} %multiply_convert_fusion.flux.own, ...), custom_call_target="tpu_custom_call", output_to_operand_aliasing={{0}: (3, {})} | custom-call | tf_op jit(solution)/shard_map/pallas_call | solution.py:322
  26.1 1.7 %collective-permute-done.4.across = bf16[8,2048]{1,0:T(8,128)(2,1)S(1)} collective-permute-done((bf16[8,2048]{1,0:T(8,128)(2,1)S(1)}, bf16[8,2048]{1,0:T(8,128)(2,1)S(1)}, u32[]{:S(2)}, u32[]{:S(2)}) %collective-permute-start.4) | collective-permute-done | bytes 32800 | tf_op jit(solution)/shard_map/ppermute | solution.py:319
  27.8 1.4 %collective-permute-done.5.inside = bf16[8,2048]{1,0:T(8,128)(2,1)S(1)} collective-permute-done((bf16[8,2048]{1,0:T(8,128)(2,1)S(1)}, bf16[8,2048]{1,0:T(8,128)(2,1)S(1)}, u32[]{:S(2)}, u32[]{:S(2)}) %collective-permute-start.5) | collective-permute-done | bytes 32800 | tf_op jit(solution)/shard_map/ppermute | solution.py:320
  29.1 1.4 %shard_map.109 = (f32[8,2048]{1,0:T(8,128)S(1)}, f32[8,2048]{1,0:T(8,128)S(1)}) custom-call(s32[1,5,16]{2,1,0:T(8,128)S(1)} %fusion.2.codes, bf16[8,2048]{1,0:T(8,128)(2,1)S(1)} %collective-permute-done.4.across, bf16[8,2048]{1,0:T(8,128)(2,1)S(1)} %collective-permute-done.5.inside, bf16[8,2048]{1,0:T(8,128)(2,1)S(1)} %multiply_convert_fusion.flux.own, ...), custom_call_target="tpu_custom_call" | custom-call | tf_op jit(solution)/shard_map/pallas_call | solution.py:338
  30.6 1.1 %collective-permute-start.6 = (f32[8,2048]{1,0:T(8,128)S(1)}, f32[8,2048]{1,0:T(8,128)S(1)}, u32[]{:S(2)}, u32[]{:S(2)}) collective-permute-start(f32[8,2048]{1,0:T(8,128)S(1)} %get-tuple-element.27), channel_id=1, source_target_pairs={{0,128},{1,129},{2,130},{3,131},{4,132},{5,133},{6,134},{7,135},{8... | collective-permute-start | bytes 196616 | tf_op jit(solution)/shard_map/ppermute | solution.py:349
  31.7 0.9 %collective-permute-done.6 = f32[8,2048]{1,0:T(8,128)S(1)} collective-permute-done((f32[8,2048]{1,0:T(8,128)S(1)}, f32[8,2048]{1,0:T(8,128)S(1)}, u32[]{:S(2)}, u32[]{:S(2)}) %collective-permute-start.6) | collective-permute-done | bytes 65568 | tf_op jit(solution)/shard_map/ppermute | solution.py:349
  32.6 0.6 %fusion = bf16[1,1,8,2048]{3,2,1,0:T(8,128)(2,1)} fusion(f32[8,2048]{1,0:T(8,128)S(1)} %get-tuple-element.26, f32[8,2048]{1,0:T(8,128)S(1)} %collective-permute-done.6), kind=kLoop, calls=%fused_computation.4 | loop fusion | flops 32768 | bytes 163840 | tf_op jit(solution)/shard_map/broadcast_in_dim | solution.py:350
  (5 shorter events, 0.1 us)
Async XLA Ops:
  0.6 14.2 %copy-start = (bf16[1,1,128,128]{3,2,1,0:T(8,128)(2,1)S(1)}, bf16[1,1,128,128]{3,2,1,0:T(8,128)(2,1)}, u32[]{:S(2)}) copy-start(bf16[1,1,128,128]{3,2,1,0:T(8,128)(2,1)} %mixing.3) | copy-start | bytes 98308
  0.6 3.7 %copy-start.3 = (s32[1,5,16]{2,0,1:T(1,128)S(1)}, s32[1,5,16]{2,0,1:T(1,128)}, u32[]{:S(2)}) copy-start(s32[1,5,16]{2,0,1:T(1,128)} %param.14) | copy-start | bytes 964
  0.7 3.7 %copy-start.4 = (s32[1,5,16]{2,0,1:T(1,128)S(1)}, s32[1,5,16]{2,0,1:T(1,128)}, u32[]{:S(2)}) copy-start(s32[1,5,16]{2,0,1:T(1,128)} %param.15) | copy-start | bytes 964
  0.7 3.7 %copy-start.2 = (s32[1,5,16]{2,0,1:T(1,128)S(1)}, s32[1,5,16]{2,0,1:T(1,128)}, u32[]{:S(2)}) copy-start(s32[1,5,16]{2,0,1:T(1,128)} %param.16) | copy-start | bytes 964
  3.6 2.1 %collective-permute-start = (f32[8,2048]{1,0:T(8,128)S(1)}, f32[8,2048]{1,0:T(8,128)S(1)}, u32[]{:S(2)}, u32[]{:S(2)}) collective-permute-start(f32[8,2048]{1,0:T(8,128)S(1)} %get-tuple-element.16.after.level), channel_id=1, source_target_pairs={{0,128},{1,129},{2,130},{3,131},{4,132},{5,133},{6,134},{7,135},{8... | collective-permute-start | bytes 196616 | tf_op jit(solution)/shard_map/ppermute | solution.py:275
  4.4 15.3 %copy-start.1 = (s32[1,2048]{1,0:T(1,128)S(1)}, s32[1,2048]{1,0:T(1,128)}, u32[]{:S(2)}) copy-start(s32[1,2048]{1,0:T(1,128)} %param.13) | copy-start | bytes 24580
  4.4 16.3 %copy-start.5 = (f32[8]{0:T(128)S(1)}, f32[8]{0:T(128)}, u32[]{:S(2)}) copy-start(f32[8]{0:T(128)} %param.12) | copy-start | bytes 100
  6.8 10.2 %collective-permute-start.1 = (bf16[8,2048]{1,0:T(8,128)(2,1)S(1)}, bf16[8,2048]{1,0:T(8,128)(2,1)S(1)}, u32[]{:S(2)}, u32[]{:S(2)}) collective-permute-start(bf16[8,2048]{1,0:T(8,128)(2,1)S(1)} %get-tuple-element.20), channel_id=1, source_target_pairs={{129,130},{2,4},{130,129},{3,5},{131,132},{4,2},{132,131},{5,3},{1... | collective-permute-start | bytes 98312 | tf_op jit(solution)/shard_map/ppermute | solution.py:309
  14.9 3.7 %collective-permute-start.2 = (bf16[8,2048]{1,0:T(8,128)(2,1)S(1)}, bf16[8,2048]{1,0:T(8,128)(2,1)S(1)}, u32[]{:S(2)}, u32[]{:S(2)}) collective-permute-start(bf16[8,2048]{1,0:T(8,128)(2,1)S(1)} %get-tuple-element.21), channel_id=1, source_target_pairs={{0,1},{128,130},{1,0},{129,131},{2,3},{130,128},{3,2},{131,129},{4... | collective-permute-start | bytes 98312 | tf_op jit(solution)/shard_map/ppermute | solution.py:309
  18.5 2.0 %collective-permute-start.3 = (f32[8,2048]{1,0:T(8,128)S(1)}, f32[8,2048]{1,0:T(8,128)S(1)}, u32[]{:S(2)}, u32[]{:S(2)}) collective-permute-start(f32[8,2048]{1,0:T(8,128)S(1)} %convert_add_fusion), channel_id=1, source_target_pairs={{0,128},{1,129},{2,130},{3,131},{4,132},{5,133},{6,134},{7,135},{8... | collective-permute-start | bytes 196616 | tf_op jit(solution)/shard_map/ppermute | solution.py:310
  20.7 7.1 %collective-permute-start.4 = (bf16[8,2048]{1,0:T(8,128)(2,1)S(1)}, bf16[8,2048]{1,0:T(8,128)(2,1)S(1)}, u32[]{:S(2)}, u32[]{:S(2)}) collective-permute-start(bf16[8,2048]{1,0:T(8,128)(2,1)S(1)} %multiply_convert_fusion.flux.own), channel_id=1, source_target_pairs={{129,130},{2,4},{130,129},{3,5},{131,132},{4,2},{132,131},{5,3},{1... | collective-permute-start | bytes 98312 | tf_op jit(solution)/shard_map/ppermute | solution.py:319
  25.2 4.0 %collective-permute-start.5 = (bf16[8,2048]{1,0:T(8,128)(2,1)S(1)}, bf16[8,2048]{1,0:T(8,128)(2,1)S(1)}, u32[]{:S(2)}, u32[]{:S(2)}) collective-permute-start(bf16[8,2048]{1,0:T(8,128)(2,1)S(1)} %multiply_convert_fusion.flux.own), channel_id=1, source_target_pairs={{0,1},{128,130},{1,0},{129,131},{2,3},{130,128},{3,2},{131,129},{4... | collective-permute-start | bytes 98312 | tf_op jit(solution)/shard_map/ppermute | solution.py:320
  30.6 2.0 %collective-permute-start.6 = (f32[8,2048]{1,0:T(8,128)S(1)}, f32[8,2048]{1,0:T(8,128)S(1)}, u32[]{:S(2)}, u32[]{:S(2)}) collective-permute-start(f32[8,2048]{1,0:T(8,128)S(1)} %get-tuple-element.27), channel_id=1, source_target_pairs={{0,128},{1,129},{2,130},{3,131},{4,132},{5,133},{6,134},{7,135},{8... | collective-permute-start | bytes 196616 | tf_op jit(solution)/shard_map/ppermute | solution.py:349

commit v5 on v4

--- a/solution.py
+++ b/solution.py
@@ -8,7 +8,6 @@
 step_weight = 0.25
 axes = ("sec", "blk")
 VMEM = pl.BlockSpec(memory_space=pltpu.VMEM)
-SMEM = pl.BlockSpec(memory_space=pltpu.SMEM)
 ANY = pl.BlockSpec(memory_space=pl.ANY)
 HBM = pl.BlockSpec(memory_space=pltpu.HBM)
 
@@ -58,11 +57,9 @@
     return core, (steps[0] + 2, steps[1] + 2), found
 
 
-def in_lower_half():
-    return jnp.bitwise_and(lax.axis_index("blk"), 7) < 4
-
-
-def level_kernel(columns, mixing, lagged, out, buffer, rows, late, semaphore, extra):
+def level_kernel(
+    columns, mixing, lagged, weights, out, buffer, picked, rows, late, semaphore, extra, others
+):
     fields = out.shape[0]
     small = [
         pltpu.make_async_copy(mixing.at[0, 0, 0:16], rows, extra.at[0]),
@@ -76,6 +73,9 @@
     for copy in copies:
         copy.start()
     small[1].start()
+    picks = pick_copies(weights, picked, others)
+    for copy in picks:
+        copy.start()
     small[0].wait()
     for f in range(fields):
         if f % 4 == 0:
@@ -91,9 +91,11 @@
         surface = out[...] - step_weight * late[...].astype(jnp.float32)
         out[...] = surface.astype(jnp.bfloat16).astype(jnp.float32)
 
-
-def pick_kernel(weights, after, picked, semaphore):
-    del after
+    for copy in picks:
+        copy.wait()
+
+
+def pick_copies(weights, picked, semaphore):
     core, distances, _ = place()
     slots = weights.shape[2]
     half = slots // 2
@@ -110,10 +112,7 @@
             semaphore.at[2],
         )
     )
-    for copy in copies:
-        copy.start()
-    for copy in copies:
-        copy.wait()
+    return copies
 
 
 def slot_jobs(core, distances, slots):
@@ -122,24 +121,15 @@
     return jobs + [(2, 2, k + core * half, 2 * slots + k) for k in range(half)]
 
 
-def remap_kernel(codes, level, other, weights, across, inside, own, ocean, tiles, sums):
+def remap(slots, surface, weights, across, inside, own, codes, semaphore, tiles, sums):
     count, fields, width = tiles.shape
     core, distances, found = place()
-
-    def spread(surface, below):
-        for t in range(count):
-            tiles[t] = surface[:, t * width : (t + 1) * width]
-        ocean[...] = below[...]
-
-    @pl.when(core == 0)
-    def _():
-        spread(level, other)
-
-    @pl.when(core == 1)
-    def _():
-        spread(other, level)
-
+    fetch = pltpu.make_async_copy(slots, codes, semaphore)
+    fetch.start()
+    for t in range(count):
+        tiles[t] = surface[:, t * width : (t + 1) * width]
     sums[...] = jnp.zeros_like(sums)
+    fetch.wait()
     for g, p, slot, at in slot_jobs(core, distances, codes.shape[2]):
         code = codes[0, p, slot]
         part = tiles[jnp.bitwise_and(code, 255)].astype(jnp.bfloat16)
@@ -157,8 +147,36 @@
         own[:, span] = sums[2, t]
 
 
-def back_kernel(codes, across, inside, own, weights, after, kept, sent, tiles, sums):
+def first_remap_kernel(slots, level, weights, across, inside, own, *scratch):
+    @pl.when(lax.axis_index("sec") == 0)
+    def _():
+        remap(slots, level, weights, across, inside, own, *scratch)
+
+
+def second_remap_kernel(
+    slots, level, other, weights, across_0, inside_0, own_0, across, inside, own, ocean, *scratch
+):
+    core = lax.axis_index("sec")
+
+    @pl.when(core == 0)
+    def _():
+        across[...] = across_0[...]
+        inside[...] = inside_0[...]
+        own[...] = own_0[...]
+        ocean[...] = other[...]
+
+    @pl.when(core == 1)
+    def _():
+        remap(slots, other, weights, across, inside, own, *scratch)
+        ocean[...] = level[...]
+
+
+def back_kernel(
+    slots, across, inside, own, weights, after, kept, sent, codes, semaphore, tiles, sums
+):
     del after
+    fetch = pltpu.make_async_copy(slots, codes, semaphore)
+    fetch.start()
     _, count, fields, width = tiles.shape
     core, distances, found = place()
     for t in range(count):
@@ -167,6 +185,7 @@
         tiles[1, t] = inside[:, span].astype(jnp.float32)
         tiles[2, t] = own[:, span].astype(jnp.float32)
     sums[...] = jnp.zeros_like(sums)
+    fetch.wait()
     for i, (g, p, slot, at) in enumerate(slot_jobs(core, distances, codes.shape[2])):
         code = codes[0, p, slot]
         source = jnp.bitwise_and(lax.shift_right_logical(code, 8), 255)
@@ -250,40 +269,54 @@
     field_f32 = jax.ShapeDtypeStruct((fields, cells), jnp.float32)
     field_bf16 = jax.ShapeDtypeStruct((fields, cells), jnp.bfloat16)
 
-    level, held = pl.pallas_call(
+    slots = weights.shape[2]
+    level, held, picked = pl.pallas_call(
         level_kernel,
-        out_shape=(field_f32, jax.ShapeDtypeStruct(columns.shape[2:], jnp.bfloat16)),
-        in_specs=[HBM, HBM, HBM],
-        out_specs=(VMEM, VMEM),
+        out_shape=(
+            field_f32,
+            jax.ShapeDtypeStruct(columns.shape[2:], jnp.bfloat16),
+            jax.ShapeDtypeStruct((5 * slots // 2, width, width), jnp.bfloat16),
+        ),
+        in_specs=[HBM, HBM, HBM, HBM],
+        out_specs=(VMEM, VMEM, VMEM),
         scratch_shapes=[
             pltpu.VMEM((16, levels), jnp.bfloat16),
             pltpu.VMEM((fields, cells), jnp.bfloat16),
             pltpu.SemaphoreType.DMA((fields,)),
             pltpu.SemaphoreType.DMA((2,)),
+            pltpu.SemaphoreType.DMA((3,)),
         ],
         compiler_params=pltpu.CompilerParams(vmem_limit_bytes=8 << 20),
-    )(*(pltpu.with_memory_space_constraint(x, pltpu.HBM) for x in (columns, mixing, lagged_flux)))
-    slots = weights.shape[2]
-    picked = pl.pallas_call(
-        pick_kernel,
-        out_shape=jax.ShapeDtypeStruct((5 * slots // 2, width, width), jnp.bfloat16),
-        in_specs=[HBM, ANY],
-        out_specs=VMEM,
-        scratch_shapes=[pltpu.SemaphoreType.DMA((3,))],
+    )(*(pltpu.with_memory_space_constraint(x, pltpu.HBM) for x in (columns, mixing, lagged_flux, weights)))
+    other_level = lax.ppermute(level, axes, swap)
+
+    scratch = [
+        pltpu.SMEM(codes.shape, jnp.int32),
+        pltpu.SemaphoreType.DMA,
+        pltpu.VMEM((tiles, fields, width), jnp.float32),
+        pltpu.VMEM((3, tiles, fields, width), jnp.float32),
+    ]
+    early = pl.pallas_call(
+        first_remap_kernel,
+        out_shape=(field_bf16, field_bf16, field_f32),
+        in_specs=[VMEM, VMEM, VMEM],
+        out_specs=(VMEM,) * 3,
+        scratch_shapes=scratch,
+        cost_estimate=pl.CostEstimate(
+            flops=5 * slots * fields * width * width,
+            transcendentals=0,
+            bytes_accessed=5 * slots * width * width,
+        ),
         compiler_params=pltpu.CompilerParams(vmem_limit_bytes=8 << 20),
-    )(pltpu.with_memory_space_constraint(weights, pltpu.HBM), level)
-    other_level = lax.ppermute(level, axes, swap)
+    )(codes, level, picked)
     to_across, to_inside, own, ocean_level = pl.pallas_call(
-        remap_kernel,
+        second_remap_kernel,
         out_shape=(field_bf16, field_bf16, field_f32, field_f32),
-        in_specs=[SMEM, VMEM, VMEM, VMEM],
+        in_specs=[VMEM] * 7,
         out_specs=(VMEM,) * 4,
-        scratch_shapes=[
-            pltpu.VMEM((tiles, fields, width), jnp.float32),
-            pltpu.VMEM((3, tiles, fields, width), jnp.float32),
-        ],
+        scratch_shapes=scratch,
         compiler_params=pltpu.CompilerParams(vmem_limit_bytes=8 << 20),
-    )(codes, level, other_level, picked)
+    )(codes, level, other_level, picked, *early)
     most_columns, head, own = pl.pallas_call(
         mix_kernel,
         out_shape=(
@@ -338,9 +371,11 @@
     kept, sent = pl.pallas_call(
         back_kernel,
         out_shape=(field_f32, field_f32),
-        in_specs=[SMEM, VMEM, VMEM, VMEM, VMEM, ANY],
+        in_specs=[VMEM, VMEM, VMEM, VMEM, VMEM, ANY],
         out_specs=(VMEM, VMEM),
         scratch_shapes=[
+            pltpu.SMEM(codes.shape, jnp.int32),
+            pltpu.SemaphoreType.DMA,
             pltpu.VMEM((3, tiles, fields, width), jnp.float32),
             pltpu.VMEM((2, tiles, fields, width), jnp.float32),
         ],

time: 33.3 us -> 32.6 us (0.979)
  Pallas kernels: 9.75 us -> 8.82 us
  waiting for transfers between devices: 6.33 us -> 7.25 us
  starting transfers between devices: 15.5 us -> 14.9 us
    pallas_call x3, Pallas kernels: 3.81 us -> 2.48 us  [the longest x1 1.39 us: local(): pl.pallas_call(back_kernel, out_shape=(field_f32, field_f32), in_specs=[V...]
    ppermute x1, waiting for transfers between devices: 0.01 us -> 0.85 us  [local(): other_level = lax.ppermute(level, axes, swap)]
    ppermute x1, starting transfers between devices: 1.13 us -> 0.37 us  [local(): remapped = partial + lax.ppermute(partial, axes, swap)]
    pallas_call x1, Pallas kernels: 2.88 us -> 3.28 us  [local(): pl.pallas_call(level_kernel, out_shape=(field_f32, jax.ShapeDtypeStruct(c...]
  transfers between devices with their start and end apart: 7 -> 7, of which waited for: 5 -> 6; matrix products, arithmetic and copies ran while one was open for 0% -> 0% of each run, Pallas kernels for 13% -> 9%
where the time goes in v5:
time: 32.6 us; the launch traced here: 32.5 us
  starting transfers between devices  14.9 us (46%)
  Pallas kernels  8.82 us (27%)
  waiting for transfers between devices  7.25 us (22%)
  other arithmetic  0.78 us (2%)
  between operations  0.77 us (2%)
    ppermute x2, starting transfers between devices, local(): partial = partial + lax.ppermute(part, axes, pairs).astype(jnp.float32)  8.05 us
    ppermute x1, starting transfers between devices, local(): flux_across = lax.ppermute(ocean_flux, axes, across)  4.45 us
    pallas_call x1, Pallas kernels, local(): pl.pallas_call(level_kernel, out_shape=(field_f32, jax.ShapeDtypeStruct(c...  3.28 us
    pallas_call x1, Pallas kernels, local(): pl.pallas_call(mix_kernel, out_shape=(jax.ShapeDtypeStruct(columns.shape,...  2.18 us
    ppermute x1, waiting for transfers between devices, local(): flux_across = lax.ppermute(ocean_flux, axes, across)  1.71 us
    ppermute x2, waiting for transfers between devices, local(): partial = partial + lax.ppermute(part, axes, pairs).astype(jnp.float32)  1.46 us
    pallas_call x1, Pallas kernels, local(): pl.pallas_call(back_kernel, out_shape=(field_f32, field_f32), in_specs=[V...  1.39 us
    ppermute x1, waiting for transfers between devices, local(): flux_inside = lax.ppermute(ocean_flux, axes, inside)  1.36 us
  transfers between devices with their start and end apart: 7, of which 6 were waited for; matrix products, arithmetic and copies ran while one was open for 0% of the time, Pallas kernels for 9%

profile of v5, /device:TPU:25, one launch (start us, length us, event | category | flops | bytes accessed | tf_op | source)
XLA Modules:
  0.0 32.5 jit_solution(12746240075142358065)
XLA Ops:
  0.6 0.0 copy-start
  0.6 0.0 copy-start.3
  0.7 0.0 copy-start.4
  0.7 0.0 copy-start.2
  0.7 3.3 %shard_map.104 = (f32[8,2048]{1,0:T(8,128)S(1)}, bf16[8,128,2048]{2,1,0:T(8,128)(2,1)S(1)}, bf16[40,128,128]{2,1,0:T(8,128)(2,1)S(1)}) custom-call(bf16[1,1,8,128,2048]{4,3,2,1,0:T(8,128)(2,1)} %columns.1, bf16[1,1,128,128]{3,2,1,0:T(8,128)(2,1)} %mixing.3, bf16[1,8,2048]{2,1,0:T(8,128)(2,1)} %lagged.1, bf16[1,5,16,128,128]{4,3,2,1,0:T(8,128)(2,1)} %weights.1), custom_call_target="tpu_custom_call" | custom-call | tf_op jit(solution)/shard_map/pallas_call | solution.py:273
  4.0 0.0 copy-start.1
  4.0 0.0 copy-start.5
  4.0 0.8 %collective-permute-start = (f32[8,2048]{1,0:T(8,128)S(1)}, f32[8,2048]{1,0:T(8,128)S(1)}, u32[]{:S(2)}, u32[]{:S(2)}) collective-permute-start(f32[8,2048]{1,0:T(8,128)S(1)} %get-tuple-element.20.level), channel_id=1, source_target_pairs={{0,128},{1,129},{2,130},{3,131},{4,132},{5,133},{6,134},{7,135},{8... | collective-permute-start | bytes 196616 | tf_op jit(solution)/shard_map/ppermute | solution.py:291
  4.8 0.0 copy-done.3
  4.8 0.0 copy-done.4
  4.8 0.0 copy-done.2
  4.8 0.9 %collective-permute-done.other = f32[8,2048]{1,0:T(8,128)S(1)} collective-permute-done((f32[8,2048]{1,0:T(8,128)S(1)}, f32[8,2048]{1,0:T(8,128)S(1)}, u32[]{:S(2)}, u32[]{:S(2)}) %collective-permute-start) | collective-permute-done | bytes 65568 | tf_op jit(solution)/shard_map/ppermute | solution.py:291
  5.7 1.1 %shard_map.106 = (bf16[8,2048]{1,0:T(8,128)(2,1)S(1)}, bf16[8,2048]{1,0:T(8,128)(2,1)S(1)}, f32[8,2048]{1,0:T(8,128)S(1)}, f32[8,2048]{1,0:T(8,128)S(1)}) custom-call(s32[1,5,16]{2,1,0:T(8,128)S(1)} %fusion.2.slots, f32[8,2048]{1,0:T(8,128)S(1)} %get-tuple-element.20.level, f32[8,2048]{1,0:T(8,128)S(1)} %collective-permute-done.other, ...), custom_call_target="tpu_custom_call" | custom-call | tf_op jit(solution)/shard_map/pallas_call | solution.py:312
  6.7 8.0 %collective-permute-start.1 = (bf16[8,2048]{1,0:T(8,128)(2,1)S(1)}, bf16[8,2048]{1,0:T(8,128)(2,1)S(1)}, u32[]{:S(2)}, u32[]{:S(2)}) collective-permute-start(bf16[8,2048]{1,0:T(8,128)(2,1)S(1)} %get-tuple-element.28), channel_id=1, source_target_pairs={{129,130},{2,4},{130,129},{3,5},{131,132},{4,2},{132,131},{5,3},{1... | collective-permute-start | bytes 98312 | tf_op jit(solution)/shard_map/ppermute | solution.py:342
  14.8 0.0 collective-permute-start.2
  14.8 0.0 copy-done
  14.8 2.2 %shard_map.107 = (bf16[1,1,8,128,2048]{4,3,2,1,0:T(8,128)(2,1)}, bf16[8,16,2048]{2,1,0:T(8,128)(2,1)S(1)}, f32[8,2048]{1,0:T(8,128)S(1)}) custom-call(bf16[8,128,2048]{2,1,0:T(8,128)(2,1)S(1)} %get-tuple-element.19.held, bf16[1,1,128,128]{3,2,1,0:T(8,128)(2,1)S(1)} %copy-done, f32[8,2048]{1,0:T(8,128)S(1)} %get-tuple-element.25.own), custom_call_target="tpu_custom_call" | custom-call | flops 536870912 | bytes 8388608 | tf_op jit(solution)/shard_map/pallas_call | solution.py:320
  17.0 0.0 collective-permute-done.1
  17.0 1.5 %collective-permute-done.2 = bf16[8,2048]{1,0:T(8,128)(2,1)S(1)} collective-permute-done((bf16[8,2048]{1,0:T(8,128)(2,1)S(1)}, bf16[8,2048]{1,0:T(8,128)(2,1)S(1)}, u32[]{:S(2)}, u32[]{:S(2)}) %collective-permute-start.2) | collective-permute-done | bytes 32800 | tf_op jit(solution)/shard_map/ppermute | solution.py:342
  18.5 0.4 %collective-permute-start.3 = (f32[8,2048]{1,0:T(8,128)S(1)}, f32[8,2048]{1,0:T(8,128)S(1)}, u32[]{:S(2)}, u32[]{:S(2)}) collective-permute-start(f32[8,2048]{1,0:T(8,128)S(1)} %convert_add_fusion), channel_id=1, source_target_pairs={{0,128},{1,129},{2,130},{3,131},{4,132},{5,133},{6,134},{7,135},{8... | collective-permute-start | bytes 196616 | tf_op jit(solution)/shard_map/ppermute | solution.py:343
  18.8 0.0 copy-done.1
  18.8 1.0 %collective-permute-done.3 = f32[8,2048]{1,0:T(8,128)S(1)} collective-permute-done((f32[8,2048]{1,0:T(8,128)S(1)}, f32[8,2048]{1,0:T(8,128)S(1)}, u32[]{:S(2)}, u32[]{:S(2)}) %collective-permute-start.3) | collective-permute-done | bytes 65568 | tf_op jit(solution)/shard_map/ppermute | solution.py:343
  19.9 0.0 copy-done.5
  19.9 0.1 multiply_convert_fusion.flux.own
  20.0 4.5 %collective-permute-start.4 = (bf16[8,2048]{1,0:T(8,128)(2,1)S(1)}, bf16[8,2048]{1,0:T(8,128)(2,1)S(1)}, u32[]{:S(2)}, u32[]{:S(2)}) collective-permute-start(bf16[8,2048]{1,0:T(8,128)(2,1)S(1)} %multiply_convert_fusion.flux.own), channel_id=1, source_target_pairs={{129,130},{2,4},{130,129},{3,5},{131,132},{4,2},{132,131},{5,3},{1... | collective-permute-start | bytes 98312 | tf_op jit(solution)/shard_map/ppermute | solution.py:352
  24.4 0.0 collective-permute-start.5
  24.4 0.9 %shard_map.108 = (bf16[1,1,8,128,2048]{4,3,2,1,0:T(8,128)(2,1)}, f32[8,128]{1,0:T(8,128)S(1)}) custom-call(bf16[8,16,2048]{2,1,0:T(8,128)(2,1)S(1)} %get-tuple-element.26.head, f32[8,2048]{1,0:T(8,128)S(1)} %get-tuple-element.20.level, bf16[8,2048]{1,0:T(8,128)(2,1)S(1)} %multiply_convert_fusion.flux.own, ...), custom_call_target="tpu_custom_call", output_to_operand_aliasing={{0}: (3, {})} | custom-call | tf_op jit(solution)/shard_map/pallas_call | solution.py:355
  25.3 1.7 %collective-permute-done.4.across = bf16[8,2048]{1,0:T(8,128)(2,1)S(1)} collective-permute-done((bf16[8,2048]{1,0:T(8,128)(2,1)S(1)}, bf16[8,2048]{1,0:T(8,128)(2,1)S(1)}, u32[]{:S(2)}, u32[]{:S(2)}) %collective-permute-start.4) | collective-permute-done | bytes 32800 | tf_op jit(solution)/shard_map/ppermute | solution.py:352
  27.0 1.4 %collective-permute-done.5.inside = bf16[8,2048]{1,0:T(8,128)(2,1)S(1)} collective-permute-done((bf16[8,2048]{1,0:T(8,128)(2,1)S(1)}, bf16[8,2048]{1,0:T(8,128)(2,1)S(1)}, u32[]{:S(2)}, u32[]{:S(2)}) %collective-permute-start.5) | collective-permute-done | bytes 32800 | tf_op jit(solution)/shard_map/ppermute | solution.py:353
  28.4 1.4 %shard_map.109 = (f32[8,2048]{1,0:T(8,128)S(1)}, f32[8,2048]{1,0:T(8,128)S(1)}) custom-call(s32[1,5,16]{2,1,0:T(8,128)S(1)} %fusion.2.slots, bf16[8,2048]{1,0:T(8,128)(2,1)S(1)} %collective-permute-done.4.across, bf16[8,2048]{1,0:T(8,128)(2,1)S(1)} %collective-permute-done.5.inside, bf16[8,2048]{1,0:T(8,128)(2,1)S(1)} %multiply_convert_fusion.flux.own, ...), custom_call_target="tpu_custom_call" | custom-call | tf_op jit(solution)/shard_map/pallas_call | solution.py:371
  29.8 1.2 %collective-permute-start.6 = (f32[8,2048]{1,0:T(8,128)S(1)}, f32[8,2048]{1,0:T(8,128)S(1)}, u32[]{:S(2)}, u32[]{:S(2)}) collective-permute-start(f32[8,2048]{1,0:T(8,128)S(1)} %get-tuple-element.35), channel_id=1, source_target_pairs={{0,128},{1,129},{2,130},{3,131},{4,132},{5,133},{6,134},{7,135},{8... | collective-permute-start | bytes 196616 | tf_op jit(solution)/shard_map/ppermute | solution.py:384
  31.0 0.9 %collective-permute-done.6 = f32[8,2048]{1,0:T(8,128)S(1)} collective-permute-done((f32[8,2048]{1,0:T(8,128)S(1)}, f32[8,2048]{1,0:T(8,128)S(1)}, u32[]{:S(2)}, u32[]{:S(2)}) %collective-permute-start.6) | collective-permute-done | bytes 65568 | tf_op jit(solution)/shard_map/ppermute | solution.py:384
  31.9 0.6 %fusion = bf16[1,1,8,2048]{3,2,1,0:T(8,128)(2,1)} fusion(f32[8,2048]{1,0:T(8,128)S(1)} %get-tuple-element.34, f32[8,2048]{1,0:T(8,128)S(1)} %collective-permute-done.6), kind=kLoop, calls=%fused_computation.4 | loop fusion | flops 32768 | bytes 163840 | tf_op jit(solution)/shard_map/broadcast_in_dim | solution.py:385
  (6 shorter events, 0.1 us)
Async XLA Ops:
  0.6 14.2 %copy-start = (bf16[1,1,128,128]{3,2,1,0:T(8,128)(2,1)S(1)}, bf16[1,1,128,128]{3,2,1,0:T(8,128)(2,1)}, u32[]{:S(2)}) copy-start(bf16[1,1,128,128]{3,2,1,0:T(8,128)(2,1)} %mixing.3) | copy-start | bytes 98308
  0.6 4.1 %copy-start.3 = (s32[1,5,16]{2,0,1:T(1,128)S(1)}, s32[1,5,16]{2,0,1:T(1,128)}, u32[]{:S(2)}) copy-start(s32[1,5,16]{2,0,1:T(1,128)} %param.14) | copy-start | bytes 964
  0.7 4.1 %copy-start.4 = (s32[1,5,16]{2,0,1:T(1,128)S(1)}, s32[1,5,16]{2,0,1:T(1,128)}, u32[]{:S(2)}) copy-start(s32[1,5,16]{2,0,1:T(1,128)} %param.15) | copy-start | bytes 964
  0.7 4.1 %copy-start.2 = (s32[1,5,16]{2,0,1:T(1,128)S(1)}, s32[1,5,16]{2,0,1:T(1,128)}, u32[]{:S(2)}) copy-start(s32[1,5,16]{2,0,1:T(1,128)} %param.16) | copy-start | bytes 964
  4.0 14.9 %copy-start.1 = (s32[1,2048]{1,0:T(1,128)S(1)}, s32[1,2048]{1,0:T(1,128)}, u32[]{:S(2)}) copy-start(s32[1,2048]{1,0:T(1,128)} %param.13) | copy-start | bytes 24580
  4.0 15.9 %copy-start.5 = (f32[8]{0:T(128)S(1)}, f32[8]{0:T(128)}, u32[]{:S(2)}) copy-start(f32[8]{0:T(128)} %param.12) | copy-start | bytes 100
  4.0 1.7 %collective-permute-start = (f32[8,2048]{1,0:T(8,128)S(1)}, f32[8,2048]{1,0:T(8,128)S(1)}, u32[]{:S(2)}, u32[]{:S(2)}) collective-permute-start(f32[8,2048]{1,0:T(8,128)S(1)} %get-tuple-element.20.level), channel_id=1, source_target_pairs={{0,128},{1,129},{2,130},{3,131},{4,132},{5,133},{6,134},{7,135},{8... | collective-permute-start | bytes 196616 | tf_op jit(solution)/shard_map/ppermute | solution.py:291
  6.7 10.2 %collective-permute-start.1 = (bf16[8,2048]{1,0:T(8,128)(2,1)S(1)}, bf16[8,2048]{1,0:T(8,128)(2,1)S(1)}, u32[]{:S(2)}, u32[]{:S(2)}) collective-permute-start(bf16[8,2048]{1,0:T(8,128)(2,1)S(1)} %get-tuple-element.28), channel_id=1, source_target_pairs={{129,130},{2,4},{130,129},{3,5},{131,132},{4,2},{132,131},{5,3},{1... | collective-permute-start | bytes 98312 | tf_op jit(solution)/shard_map/ppermute | solution.py:342
  14.8 3.7 %collective-permute-start.2 = (bf16[8,2048]{1,0:T(8,128)(2,1)S(1)}, bf16[8,2048]{1,0:T(8,128)(2,1)S(1)}, u32[]{:S(2)}, u32[]{:S(2)}) collective-permute-start(bf16[8,2048]{1,0:T(8,128)(2,1)S(1)} %get-tuple-element.29), channel_id=1, source_target_pairs={{0,1},{128,130},{1,0},{129,131},{2,3},{130,128},{3,2},{131,129},{4... | collective-permute-start | bytes 98312 | tf_op jit(solution)/shard_map/ppermute | solution.py:342
  18.5 1.3 %collective-permute-start.3 = (f32[8,2048]{1,0:T(8,128)S(1)}, f32[8,2048]{1,0:T(8,128)S(1)}, u32[]{:S(2)}, u32[]{:S(2)}) collective-permute-start(f32[8,2048]{1,0:T(8,128)S(1)} %convert_add_fusion), channel_id=1, source_target_pairs={{0,128},{1,129},{2,130},{3,131},{4,132},{5,133},{6,134},{7,135},{8... | collective-permute-start | bytes 196616 | tf_op jit(solution)/shard_map/ppermute | solution.py:343
  20.0 7.1 %collective-permute-start.4 = (bf16[8,2048]{1,0:T(8,128)(2,1)S(1)}, bf16[8,2048]{1,0:T(8,128)(2,1)S(1)}, u32[]{:S(2)}, u32[]{:S(2)}) collective-permute-start(bf16[8,2048]{1,0:T(8,128)(2,1)S(1)} %multiply_convert_fusion.flux.own), channel_id=1, source_target_pairs={{129,130},{2,4},{130,129},{3,5},{131,132},{4,2},{132,131},{5,3},{1... | collective-permute-start | bytes 98312 | tf_op jit(solution)/shard_map/ppermute | solution.py:352
  24.4 4.0 %collective-permute-start.5 = (bf16[8,2048]{1,0:T(8,128)(2,1)S(1)}, bf16[8,2048]{1,0:T(8,128)(2,1)S(1)}, u32[]{:S(2)}, u32[]{:S(2)}) collective-permute-start(bf16[8,2048]{1,0:T(8,128)(2,1)S(1)} %multiply_convert_fusion.flux.own), channel_id=1, source_target_pairs={{0,1},{128,130},{1,0},{129,131},{2,3},{130,128},{3,2},{131,129},{4... | collective-permute-start | bytes 98312 | tf_op jit(solution)/shard_map/ppermute | solution.py:353
  29.8 2.1 %collective-permute-start.6 = (f32[8,2048]{1,0:T(8,128)S(1)}, f32[8,2048]{1,0:T(8,128)S(1)}, u32[]{:S(2)}, u32[]{:S(2)}) collective-permute-start(f32[8,2048]{1,0:T(8,128)S(1)} %get-tuple-element.35), channel_id=1, source_target_pairs={{0,128},{1,129},{2,130},{3,131},{4,132},{5,133},{6,134},{7,135},{8... | collective-permute-start | bytes 196616 | tf_op jit(solution)/shard_map/ppermute | solution.py:384

commit v6 on v5

--- a/solution.py
+++ b/solution.py
@@ -172,9 +172,8 @@
 
 
 def back_kernel(
-    slots, across, inside, own, weights, after, kept, sent, codes, semaphore, tiles, sums
+    slots, inside, across, own, turned, kept, sent, codes, semaphore, tiles, sums
 ):
-    del after
     fetch = pltpu.make_async_copy(slots, codes, semaphore)
     fetch.start()
     _, count, fields, width = tiles.shape
@@ -190,12 +189,7 @@
         code = codes[0, p, slot]
         source = jnp.bitwise_and(lax.shift_right_logical(code, 8), 255)
         part = tiles[g, source].astype(jnp.bfloat16)
-        product = lax.dot_general(
-            part,
-            weights[at],
-            (((1,), (1,)), ((), ())),
-            preferred_element_type=jnp.float32,
-        )
+        product = jnp.dot(part, turned[at], preferred_element_type=jnp.float32)
         target = jnp.bitwise_and(code, 255)
         keep = lax.shift_right_logical(code, 16) == 1
         if g < 2:
@@ -236,7 +230,7 @@
         copy.wait()
 
 
-def top_kernel(head, level, flux, columns, out, done, tops, semaphore):
+def top_kernel(head, level, flux, weights, columns, out, turned, tops, semaphore):
     del columns
     fields, rows, cells = head.shape
     share = jnp.where(lax.axis_index("sec") == 1, step_weight, 0.0)
@@ -250,7 +244,8 @@
             pltpu.make_async_copy(tops.at[f], out.at[0, 0, f, pl.ds(0, rows)], semaphore.at[f])
         )
         copies[f].start()
-    done[...] = jnp.zeros_like(done)
+    for at in range(weights.shape[0]):
+        turned[at] = weights[at].T
     for copy in copies:
         copy.wait()
 
@@ -352,26 +347,26 @@
     flux_across = lax.ppermute(ocean_flux, axes, across)
     flux_inside = lax.ppermute(ocean_flux, axes, inside)
 
-    new_columns, done = pl.pallas_call(
+    new_columns, turned = pl.pallas_call(
         top_kernel,
         out_shape=(
             jax.ShapeDtypeStruct(columns.shape, jnp.bfloat16),
-            jax.ShapeDtypeStruct((8, 128), jnp.float32),
-        ),
-        in_specs=[VMEM, VMEM, VMEM, HBM],
+            jax.ShapeDtypeStruct(picked.shape, jnp.bfloat16),
+        ),
+        in_specs=[VMEM, VMEM, VMEM, VMEM, HBM],
         out_specs=(HBM, VMEM),
-        input_output_aliases={3: 0},
+        input_output_aliases={4: 0},
         scratch_shapes=[
             pltpu.VMEM((fields, 16, cells), jnp.bfloat16),
             pltpu.SemaphoreType.DMA((fields,)),
         ],
         compiler_params=pltpu.CompilerParams(vmem_limit_bytes=8 << 20),
-    )(head, level, ocean_flux, most_columns)
+    )(head, level, ocean_flux, picked, most_columns)
 
     kept, sent = pl.pallas_call(
         back_kernel,
         out_shape=(field_f32, field_f32),
-        in_specs=[VMEM, VMEM, VMEM, VMEM, VMEM, ANY],
+        in_specs=[VMEM, VMEM, VMEM, VMEM, VMEM],
         out_specs=(VMEM, VMEM),
         scratch_shapes=[
             pltpu.SMEM(codes.shape, jnp.int32),
@@ -380,7 +375,7 @@
             pltpu.VMEM((2, tiles, fields, width), jnp.float32),
         ],
         compiler_params=pltpu.CompilerParams(vmem_limit_bytes=8 << 20),
-    )(codes, flux_across, flux_inside, ocean_flux, picked, done)
+    )(codes, flux_inside, flux_across, ocean_flux, turned)
     flux_here = (kept + lax.ppermute(sent, axes, swap)).astype(jnp.bfloat16)
     return (new_columns, flux_here[None, None])
 

time: 32.6 us -> 32.3 us (level)
    pallas_call x1, Pallas kernels: 1.39 us -> 1.06 us  [local(): pl.pallas_call(back_kernel, out_shape=(field_f32, field_f32), in_specs=[V...]
  transfers between devices with their start and end apart: 7 -> 7, of which waited for: 6 -> 6; matrix products, arithmetic and copies ran while one was open for 0% -> 0% of each run, Pallas kernels for 9% -> 11%
where the time goes in v6:
time: 32.3 us; the launch traced here: 32.2 us
  starting transfers between devices  14.9 us (46%)
  Pallas kernels  8.79 us (27%)
  waiting for transfers between devices  6.94 us (21%)
  other arithmetic  0.78 us (2%)
  between operations  0.77 us (2%)
    ppermute x2, starting transfers between devices, local(): partial = partial + lax.ppermute(part, axes, pairs).astype(jnp.float32)  8.04 us
    ppermute x1, starting transfers between devices, local(): flux_across = lax.ppermute(ocean_flux, axes, across)  4.45 us
    pallas_call x1, Pallas kernels, local(): pl.pallas_call(level_kernel, out_shape=(field_f32, jax.ShapeDtypeStruct(c...  3.28 us
    pallas_call x1, Pallas kernels, local(): pl.pallas_call(mix_kernel, out_shape=(jax.ShapeDtypeStruct(columns.shape,...  2.18 us
    ppermute x2, waiting for transfers between devices, local(): partial = partial + lax.ppermute(part, axes, pairs).astype(jnp.float32)  1.46 us
    ppermute x1, waiting for transfers between devices, local(): flux_across = lax.ppermute(ocean_flux, axes, across)  1.41 us
    ppermute x1, waiting for transfers between devices, local(): flux_inside = lax.ppermute(ocean_flux, axes, inside)  1.36 us
    ppermute x1, starting transfers between devices, local(): flux_here = (kept + lax.ppermute(sent, axes, swap)).astype(jnp.bfloat16)  1.23 us
  transfers between devices with their start and end apart: 7, of which 6 were waited for; matrix products, arithmetic and copies ran while one was open for 0% of the time, Pallas kernels for 11%

profile of v6, /device:TPU:25, one launch (start us, length us, event | category | flops | bytes accessed | tf_op | source)
XLA Modules:
  0.0 32.2 jit_solution(9370880528036359388)
XLA Ops:
  0.6 0.0 copy-start
  0.6 0.0 copy-start.2
  0.7 0.0 copy-start.4
  0.7 0.0 copy-start.3
  0.7 3.3 %shard_map.104 = (f32[8,2048]{1,0:T(8,128)S(1)}, bf16[8,128,2048]{2,1,0:T(8,128)(2,1)S(1)}, bf16[40,128,128]{2,1,0:T(8,128)(2,1)S(1)}) custom-call(bf16[1,1,8,128,2048]{4,3,2,1,0:T(8,128)(2,1)} %columns.1, bf16[1,1,128,128]{3,2,1,0:T(8,128)(2,1)} %mixing.3, bf16[1,8,2048]{2,1,0:T(8,128)(2,1)} %lagged.1, bf16[1,5,16,128,128]{4,3,2,1,0:T(8,128)(2,1)} %weights.1), custom_call_target="tpu_custom_call" | custom-call | tf_op jit(solution)/shard_map/pallas_call | solution.py:268
  4.0 0.0 copy-start.1
  4.0 0.0 copy-start.5
  4.0 0.8 %collective-permute-start = (f32[8,2048]{1,0:T(8,128)S(1)}, f32[8,2048]{1,0:T(8,128)S(1)}, u32[]{:S(2)}, u32[]{:S(2)}) collective-permute-start(f32[8,2048]{1,0:T(8,128)S(1)} %get-tuple-element.20.level), channel_id=1, source_target_pairs={{0,128},{1,129},{2,130},{3,131},{4,132},{5,133},{6,134},{7,135},{8... | collective-permute-start | bytes 196616 | tf_op jit(solution)/shard_map/ppermute | solution.py:286
  4.8 0.0 copy-done.2
  4.8 0.0 copy-done.4
  4.8 0.0 copy-done.3
  4.8 0.9 %collective-permute-done.other = f32[8,2048]{1,0:T(8,128)S(1)} collective-permute-done((f32[8,2048]{1,0:T(8,128)S(1)}, f32[8,2048]{1,0:T(8,128)S(1)}, u32[]{:S(2)}, u32[]{:S(2)}) %collective-permute-start) | collective-permute-done | bytes 65568 | tf_op jit(solution)/shard_map/ppermute | solution.py:286
  5.7 1.1 %shard_map.106 = (bf16[8,2048]{1,0:T(8,128)(2,1)S(1)}, bf16[8,2048]{1,0:T(8,128)(2,1)S(1)}, f32[8,2048]{1,0:T(8,128)S(1)}, f32[8,2048]{1,0:T(8,128)S(1)}) custom-call(s32[1,5,16]{2,1,0:T(8,128)S(1)} %fusion.2.slots, f32[8,2048]{1,0:T(8,128)S(1)} %get-tuple-element.20.level, f32[8,2048]{1,0:T(8,128)S(1)} %collective-permute-done.other, ...), custom_call_target="tpu_custom_call" | custom-call | tf_op jit(solution)/shard_map/pallas_call | solution.py:307
  6.7 8.0 %collective-permute-start.1 = (bf16[8,2048]{1,0:T(8,128)(2,1)S(1)}, bf16[8,2048]{1,0:T(8,128)(2,1)S(1)}, u32[]{:S(2)}, u32[]{:S(2)}) collective-permute-start(bf16[8,2048]{1,0:T(8,128)(2,1)S(1)} %get-tuple-element.28), channel_id=1, source_target_pairs={{129,130},{2,4},{130,129},{3,5},{131,132},{4,2},{132,131},{5,3},{1... | collective-permute-start | bytes 98312 | tf_op jit(solution)/shard_map/ppermute | solution.py:337
  14.8 0.0 collective-permute-start.2
  14.8 0.0 copy-done
  14.8 2.2 %shard_map.107 = (bf16[1,1,8,128,2048]{4,3,2,1,0:T(8,128)(2,1)}, bf16[8,16,2048]{2,1,0:T(8,128)(2,1)S(1)}, f32[8,2048]{1,0:T(8,128)S(1)}) custom-call(bf16[8,128,2048]{2,1,0:T(8,128)(2,1)S(1)} %get-tuple-element.19.held, bf16[1,1,128,128]{3,2,1,0:T(8,128)(2,1)S(1)} %copy-done, f32[8,2048]{1,0:T(8,128)S(1)} %get-tuple-element.25.own), custom_call_target="tpu_custom_call" | custom-call | flops 536870912 | bytes 8388608 | tf_op jit(solution)/shard_map/pallas_call | solution.py:315
  17.0 0.0 collective-permute-done.1
  17.0 1.5 %collective-permute-done.2 = bf16[8,2048]{1,0:T(8,128)(2,1)S(1)} collective-permute-done((bf16[8,2048]{1,0:T(8,128)(2,1)S(1)}, bf16[8,2048]{1,0:T(8,128)(2,1)S(1)}, u32[]{:S(2)}, u32[]{:S(2)}) %collective-permute-start.2) | collective-permute-done | bytes 32800 | tf_op jit(solution)/shard_map/ppermute | solution.py:337
  18.5 0.4 %collective-permute-start.3 = (f32[8,2048]{1,0:T(8,128)S(1)}, f32[8,2048]{1,0:T(8,128)S(1)}, u32[]{:S(2)}, u32[]{:S(2)}) collective-permute-start(f32[8,2048]{1,0:T(8,128)S(1)} %convert_add_fusion), channel_id=1, source_target_pairs={{0,128},{1,129},{2,130},{3,131},{4,132},{5,133},{6,134},{7,135},{8... | collective-permute-start | bytes 196616 | tf_op jit(solution)/shard_map/ppermute | solution.py:338
  18.8 0.0 copy-done.1
  18.8 1.0 %collective-permute-done.3 = f32[8,2048]{1,0:T(8,128)S(1)} collective-permute-done((f32[8,2048]{1,0:T(8,128)S(1)}, f32[8,2048]{1,0:T(8,128)S(1)}, u32[]{:S(2)}, u32[]{:S(2)}) %collective-permute-start.3) | collective-permute-done | bytes 65568 | tf_op jit(solution)/shard_map/ppermute | solution.py:338
  19.9 0.0 copy-done.5
  19.9 0.1 multiply_convert_fusion.flux.own
  20.0 4.5 %collective-permute-start.5 = (bf16[8,2048]{1,0:T(8,128)(2,1)S(1)}, bf16[8,2048]{1,0:T(8,128)(2,1)S(1)}, u32[]{:S(2)}, u32[]{:S(2)}) collective-permute-start(bf16[8,2048]{1,0:T(8,128)(2,1)S(1)} %multiply_convert_fusion.flux.own), channel_id=1, source_target_pairs={{129,130},{2,4},{130,129},{3,5},{131,132},{4,2},{132,131},{5,3},{1... | collective-permute-start | bytes 98312 | tf_op jit(solution)/shard_map/ppermute | solution.py:347
  24.4 0.0 collective-permute-start.4
  24.4 1.2 %shard_map.108 = (bf16[1,1,8,128,2048]{4,3,2,1,0:T(8,128)(2,1)}, bf16[40,128,128]{2,1,0:T(8,128)(2,1)S(1)}) custom-call(bf16[8,16,2048]{2,1,0:T(8,128)(2,1)S(1)} %get-tuple-element.26.head, f32[8,2048]{1,0:T(8,128)S(1)} %get-tuple-element.20.level, bf16[8,2048]{1,0:T(8,128)(2,1)S(1)} %multiply_convert_fusion.flux.own, ...), custom_call_target="tpu_custom_call", output_to_operand_aliasing={{0}: (4, {})} | custom-call | tf_op jit(solution)/shard_map/pallas_call | solution.py:350
  25.6 1.4 %collective-permute-done.5.across = bf16[8,2048]{1,0:T(8,128)(2,1)S(1)} collective-permute-done((bf16[8,2048]{1,0:T(8,128)(2,1)S(1)}, bf16[8,2048]{1,0:T(8,128)(2,1)S(1)}, u32[]{:S(2)}, u32[]{:S(2)}) %collective-permute-start.5) | collective-permute-done | bytes 32800 | tf_op jit(solution)/shard_map/ppermute | solution.py:347
  27.0 1.4 %collective-permute-done.4.inside = bf16[8,2048]{1,0:T(8,128)(2,1)S(1)} collective-permute-done((bf16[8,2048]{1,0:T(8,128)(2,1)S(1)}, bf16[8,2048]{1,0:T(8,128)(2,1)S(1)}, u32[]{:S(2)}, u32[]{:S(2)}) %collective-permute-start.4) | collective-permute-done | bytes 32800 | tf_op jit(solution)/shard_map/ppermute | solution.py:348
  28.4 1.1 %shard_map.109 = (f32[8,2048]{1,0:T(8,128)S(1)}, f32[8,2048]{1,0:T(8,128)S(1)}) custom-call(s32[1,5,16]{2,1,0:T(8,128)S(1)} %fusion.2.slots, bf16[8,2048]{1,0:T(8,128)(2,1)S(1)} %collective-permute-done.4.inside, bf16[8,2048]{1,0:T(8,128)(2,1)S(1)} %collective-permute-done.5.across, bf16[8,2048]{1,0:T(8,128)(2,1)S(1)} %multiply_convert_fusion.flux.own, ...), custom_call_target="tpu_custom_call" | custom-call | tf_op jit(solution)/shard_map/pallas_call | solution.py:366
  29.4 1.2 %collective-permute-start.6 = (f32[8,2048]{1,0:T(8,128)S(1)}, f32[8,2048]{1,0:T(8,128)S(1)}, u32[]{:S(2)}, u32[]{:S(2)}) collective-permute-start(f32[8,2048]{1,0:T(8,128)S(1)} %get-tuple-element.35), channel_id=1, source_target_pairs={{0,128},{1,129},{2,130},{3,131},{4,132},{5,133},{6,134},{7,135},{8... | collective-permute-start | bytes 196616 | tf_op jit(solution)/shard_map/ppermute | solution.py:379
  30.7 0.9 %collective-permute-done.6 = f32[8,2048]{1,0:T(8,128)S(1)} collective-permute-done((f32[8,2048]{1,0:T(8,128)S(1)}, f32[8,2048]{1,0:T(8,128)S(1)}, u32[]{:S(2)}, u32[]{:S(2)}) %collective-permute-start.6) | collective-permute-done | bytes 65568 | tf_op jit(solution)/shard_map/ppermute | solution.py:379
  31.6 0.6 %fusion = bf16[1,1,8,2048]{3,2,1,0:T(8,128)(2,1)} fusion(f32[8,2048]{1,0:T(8,128)S(1)} %get-tuple-element.34, f32[8,2048]{1,0:T(8,128)S(1)} %collective-permute-done.6), kind=kLoop, calls=%fused_computation.4 | loop fusion | flops 32768 | bytes 163840 | tf_op jit(solution)/shard_map/broadcast_in_dim | solution.py:380
  (6 shorter events, 0.1 us)
Async XLA Ops:
  0.6 14.2 %copy-start = (bf16[1,1,128,128]{3,2,1,0:T(8,128)(2,1)S(1)}, bf16[1,1,128,128]{3,2,1,0:T(8,128)(2,1)}, u32[]{:S(2)}) copy-start(bf16[1,1,128,128]{3,2,1,0:T(8,128)(2,1)} %mixing.3) | copy-start | bytes 98308
  0.6 4.1 %copy-start.2 = (s32[1,5,16]{2,0,1:T(1,128)S(1)}, s32[1,5,16]{2,0,1:T(1,128)}, u32[]{:S(2)}) copy-start(s32[1,5,16]{2,0,1:T(1,128)} %param.16) | copy-start | bytes 964
  0.7 4.1 %copy-start.4 = (s32[1,5,16]{2,0,1:T(1,128)S(1)}, s32[1,5,16]{2,0,1:T(1,128)}, u32[]{:S(2)}) copy-start(s32[1,5,16]{2,0,1:T(1,128)} %param.15) | copy-start | bytes 964
  0.7 4.1 %copy-start.3 = (s32[1,5,16]{2,0,1:T(1,128)S(1)}, s32[1,5,16]{2,0,1:T(1,128)}, u32[]{:S(2)}) copy-start(s32[1,5,16]{2,0,1:T(1,128)} %param.14) | copy-start | bytes 964
  4.0 14.9 %copy-start.1 = (s32[1,2048]{1,0:T(1,128)S(1)}, s32[1,2048]{1,0:T(1,128)}, u32[]{:S(2)}) copy-start(s32[1,2048]{1,0:T(1,128)} %param.13) | copy-start | bytes 24580
  4.0 15.9 %copy-start.5 = (f32[8]{0:T(128)S(1)}, f32[8]{0:T(128)}, u32[]{:S(2)}) copy-start(f32[8]{0:T(128)} %param.12) | copy-start | bytes 100
  4.0 1.7 %collective-permute-start = (f32[8,2048]{1,0:T(8,128)S(1)}, f32[8,2048]{1,0:T(8,128)S(1)}, u32[]{:S(2)}, u32[]{:S(2)}) collective-permute-start(f32[8,2048]{1,0:T(8,128)S(1)} %get-tuple-element.20.level), channel_id=1, source_target_pairs={{0,128},{1,129},{2,130},{3,131},{4,132},{5,133},{6,134},{7,135},{8... | collective-permute-start | bytes 196616 | tf_op jit(solution)/shard_map/ppermute | solution.py:286
  6.7 10.2 %collective-permute-start.1 = (bf16[8,2048]{1,0:T(8,128)(2,1)S(1)}, bf16[8,2048]{1,0:T(8,128)(2,1)S(1)}, u32[]{:S(2)}, u32[]{:S(2)}) collective-permute-start(bf16[8,2048]{1,0:T(8,128)(2,1)S(1)} %get-tuple-element.28), channel_id=1, source_target_pairs={{129,130},{2,4},{130,129},{3,5},{131,132},{4,2},{132,131},{5,3},{1... | collective-permute-start | bytes 98312 | tf_op jit(solution)/shard_map/ppermute | solution.py:337
  14.8 3.7 %collective-permute-start.2 = (bf16[8,2048]{1,0:T(8,128)(2,1)S(1)}, bf16[8,2048]{1,0:T(8,128)(2,1)S(1)}, u32[]{:S(2)}, u32[]{:S(2)}) collective-permute-start(bf16[8,2048]{1,0:T(8,128)(2,1)S(1)} %get-tuple-element.29), channel_id=1, source_target_pairs={{0,1},{128,130},{1,0},{129,131},{2,3},{130,128},{3,2},{131,129},{4... | collective-permute-start | bytes 98312 | tf_op jit(solution)/shard_map/ppermute | solution.py:337
  18.5 1.3 %collective-permute-start.3 = (f32[8,2048]{1,0:T(8,128)S(1)}, f32[8,2048]{1,0:T(8,128)S(1)}, u32[]{:S(2)}, u32[]{:S(2)}) collective-permute-start(f32[8,2048]{1,0:T(8,128)S(1)} %convert_add_fusion), channel_id=1, source_target_pairs={{0,128},{1,129},{2,130},{3,131},{4,132},{5,133},{6,134},{7,135},{8... | collective-permute-start | bytes 196616 | tf_op jit(solution)/shard_map/ppermute | solution.py:338
  20.0 7.1 %collective-permute-start.5 = (bf16[8,2048]{1,0:T(8,128)(2,1)S(1)}, bf16[8,2048]{1,0:T(8,128)(2,1)S(1)}, u32[]{:S(2)}, u32[]{:S(2)}) collective-permute-start(bf16[8,2048]{1,0:T(8,128)(2,1)S(1)} %multiply_convert_fusion.flux.own), channel_id=1, source_target_pairs={{129,130},{2,4},{130,129},{3,5},{131,132},{4,2},{132,131},{5,3},{1... | collective-permute-start | bytes 98312 | tf_op jit(solution)/shard_map/ppermute | solution.py:347
  24.4 4.0 %collective-permute-start.4 = (bf16[8,2048]{1,0:T(8,128)(2,1)S(1)}, bf16[8,2048]{1,0:T(8,128)(2,1)S(1)}, u32[]{:S(2)}, u32[]{:S(2)}) collective-permute-start(bf16[8,2048]{1,0:T(8,128)(2,1)S(1)} %multiply_convert_fusion.flux.own), channel_id=1, source_target_pairs={{0,1},{128,130},{1,0},{129,131},{2,3},{130,128},{3,2},{131,129},{4... | collective-permute-start | bytes 98312 | tf_op jit(solution)/shard_map/ppermute | solution.py:348
  29.4 2.1 %collective-permute-start.6 = (f32[8,2048]{1,0:T(8,128)S(1)}, f32[8,2048]{1,0:T(8,128)S(1)}, u32[]{:S(2)}, u32[]{:S(2)}) collective-permute-start(f32[8,2048]{1,0:T(8,128)S(1)} %get-tuple-element.35), channel_id=1, source_target_pairs={{0,128},{1,129},{2,130},{3,131},{4,132},{5,133},{6,134},{7,135},{8... | collective-permute-start | bytes 196616 | tf_op jit(solution)/shard_map/ppermute | solution.py:379
